TPU v7x, 32 devices: a whole 2x2x4 slice. The times are simulated.
32 devices in a mesh: groups: 2 (over y), seq: 16 (over z, x, core).
Axes of the slice: x: 2, y: 2, z: 4, core: 2. Of those that a mesh axis runs over, the one named last changes fastest.
Arguments:
- queries: bfloat16 [12288, 2048], P(('groups', 'seq')), parts along dimension 0, may hold values from -6 to 6
- key_vectors: bfloat16 [12288, 2048], P(('groups', 'seq')), parts along dimension 0, may hold values from -6 to 6
- value_vectors: bfloat16 [12288, 2048], P(('groups', 'seq')), parts along dimension 0, may hold values from -6 to 6
- out_cotangent: bfloat16 [12288, 2048], P(('groups', 'seq')), parts along dimension 0, may hold values from -6 to 6
- norm_gain: float32 [2048], replicated, may hold values from 0.1 to 1.9
Outputs:
- query_grad: bfloat16 [12288, 2048], P(('groups', 'seq')), parts along dimension 0
- key_grad: bfloat16 [12288, 2048], P(('groups', 'seq')), parts along dimension 0
- value_grad: bfloat16 [12288, 2048], P(('groups', 'seq')), parts along dimension 0
- gain_grad: float32 [4096], P('groups'), parts along dimension 0
There are 2 independent parts, one for each index of `groups`. A program takes and returns all parts, laid end to end along the dimension named above; an argument that names none is the same for every part. Nothing has to cross between parts.
All inputs are finite; a program needn't handle non-finite values.
Results may differ from a plain program's by a relative error of at most 0.011.
Values may be sent and summed in bfloat16 or wider, within the bound.
No kernel may reach another device: no remote copies, remote signals or barrier semaphores. Data moves between devices by JAX's collectives and lax.ppermute only.
A program may use at most 128 MiB of HBM per device.

v0:
```python
import jax
import jax.numpy as jnp
from jax import lax
from jax.sharding import PartitionSpec as P

HEADS = 16
HEAD = 128


norm_eps = 1e-05


def shifted(value, axis, steps):
    count = lax.axis_size(axis)
    first, last = (max(0, -steps), min(count, count - steps))
    return lax.ppermute(value, axis, [(source, source + steps) for source in range(first, last)])


def feature(x):
    return jnp.where(x > 0, x + 1.0, jnp.exp(jnp.minimum(x, 0.0)))


def slope(x):
    return jnp.where(x > 0, 1.0, jnp.exp(jnp.minimum(x, 0.0)))


def on_device(queries, key_vectors, value_vectors, out_cotangent, norm_gain):
    length = queries.shape[0]
    shards = lax.axis_size("seq")
    rounds = (shards - 1).bit_length()
    query_raw = queries.reshape(length, HEADS, HEAD)
    key_raw = key_vectors.reshape(length, HEADS, HEAD)
    value_rows = value_vectors.reshape(length, HEADS, HEAD)
    cotan = out_cotangent.reshape(length, HEADS, HEAD).astype(jnp.float32)
    query_map = feature(query_raw.astype(jnp.float32)).astype(jnp.bfloat16)
    key_map = feature(key_raw.astype(jnp.float32)).astype(jnp.bfloat16)
    own_state = jnp.einsum("thd,the->hde", key_map, value_rows, preferred_element_type=jnp.float32)
    running = own_state
    for level in range(rounds):
        running = running + shifted(running, "seq", 1 << level)
    state_low = (running - own_state).astype(jnp.bfloat16)
    causal = jnp.tril(jnp.ones((length, length), dtype=bool))[None]
    scores = jnp.einsum("thd,shd->hts", query_map, key_map, preferred_element_type=jnp.float32)
    weights = jnp.where(causal, scores, 0.0).astype(jnp.bfloat16)
    mixed = jnp.einsum("hts,she->the", weights, value_rows, preferred_element_type=jnp.float32)
    mixed = mixed + jnp.einsum(
        "thd,hde->the", query_map, state_low, preferred_element_type=jnp.float32
    )
    rms = jnp.sqrt(jnp.mean(mixed * mixed, axis=-1, keepdims=True) + norm_eps)
    normed = mixed / rms
    gain_part = jnp.sum(cotan * normed, axis=0)
    scaled = cotan * norm_gain.reshape(HEADS, HEAD)
    grad_mixed = (
        (scaled - normed * jnp.mean(scaled * normed, axis=-1, keepdims=True)) / rms
    ).astype(jnp.bfloat16)
    query_state = jnp.einsum(
        "thd,the->hde", query_map, grad_mixed, preferred_element_type=jnp.float32
    )
    later = query_state
    for level in range(rounds):
        later = later + shifted(later, "seq", -(1 << level))
    back_low = (later - query_state).astype(jnp.bfloat16)
    gain_total = lax.psum(gain_part, "seq")
    d_scores = jnp.einsum(
        "the,she->hts", grad_mixed, value_rows, preferred_element_type=jnp.float32
    )
    d_weights = jnp.where(causal, d_scores, 0.0).astype(jnp.bfloat16)
    d_query = jnp.einsum("hts,shd->thd", d_weights, key_map, preferred_element_type=jnp.float32)
    d_query = d_query + jnp.einsum(
        "the,hde->thd", grad_mixed, state_low, preferred_element_type=jnp.float32
    )
    d_key = jnp.einsum("hts,thd->shd", d_weights, query_map, preferred_element_type=jnp.float32)
    d_key = d_key + jnp.einsum(
        "the,hde->thd", value_rows, back_low, preferred_element_type=jnp.float32
    )
    d_value = jnp.einsum("hts,the->she", weights, grad_mixed, preferred_element_type=jnp.float32)
    d_value = d_value + jnp.einsum(
        "thd,hde->the", key_map, back_low, preferred_element_type=jnp.float32
    )
    query_grad = (d_query * slope(query_raw.astype(jnp.float32))).astype(jnp.bfloat16)
    key_grad = (d_key * slope(key_raw.astype(jnp.float32))).astype(jnp.bfloat16)
    value_grad = d_value.astype(jnp.bfloat16)
    flat = (length, HEADS * HEAD)
    return (
        query_grad.reshape(flat),
        key_grad.reshape(flat),
        value_grad.reshape(flat),
        gain_total.reshape(HEADS * HEAD),
    )


def solution(mesh):
    placed = (
        P(("groups", "seq"), None),
        P(("groups", "seq"), None),
        P(("groups", "seq"), None),
        P(("groups", "seq"), None),
        P(),
    )
    return jax.shard_map(
        on_device,
        mesh=mesh,
        in_specs=placed,
        out_specs=(
            P(("groups", "seq"), None),
            P(("groups", "seq"), None),
            P(("groups", "seq"), None),
            P("groups"),
        ),
        check_vma=False,
    )
```

profile of v0, /device:TPU:16, one launch (start us, length us, event | category | flops | bytes accessed | tf_op | source)
XLA Modules:
  0.0 292.3 jit_solution(8299461528966683161)
XLA Ops:
  0.6 4.7 %fusion.3 = (f32[384,2048]{1,0:T(8,128)}, bf16[48,16,8,128]{3,2,1,0:T(8,128)(2,1)}, bf16[48,8,16,128]{3,1,2,0:T(8,128)(2,1)S(1)}) fusion(bf16[384,2048]{1,0:T(8,128)(2,1)} %param.6), kind=kLoop, calls=%fused_computation.11 | loop fusion | flops 5505024 | bytes 7864320 | tf_op jit(solution)/shard_map/jit(_where)/select_n | solution.py:24
  5.3 1.6 copy.40
  6.9 2.1 copy.19
  9.0 0.6 fusion.14
  9.6 1.9 collective-permute-start
  11.5 15.1 %collective-permute-done = f32[16,128,128]{2,1,0:T(8,128)S(1)} collective-permute-done((f32[16,128,128]{2,1,0:T(8,128)S(1)}, f32[16,128,128]{2,1,0:T(8,128)S(1)}, u32[]{:S(2)}, u32[]{:S(2)}) %collective-permute-start) | collective-permute-done | bytes 1048608 | tf_op jit(solution)/shard_map/ppermute | solution.py:16
  26.8 2.5 collective-permute-start.1
  29.3 23.6 %collective-permute-done.1 = f32[16,128,128]{2,1,0:T(8,128)S(1)} collective-permute-done((f32[16,128,128]{2,1,0:T(8,128)S(1)}, f32[16,128,128]{2,1,0:T(8,128)S(1)}, u32[]{:S(2)}, u32[]{:S(2)}) %collective-permute-start.1) | collective-permute-done | bytes 1048608 | tf_op jit(solution)/shard_map/ppermute | solution.py:16
  53.0 3.6 %collective-permute-start.2 = (f32[16,128,128]{2,1,0:T(8,128)S(1)}, f32[16,128,128]{2,1,0:T(8,128)S(1)}, u32[]{:S(2)}, u32[]{:S(2)}) collective-permute-start(f32[16,128,128]{2,1,0:T(8,128)S(1)} %add.67), channel_id=1, source_target_pairs={{0,4},{1,5},{2,6},{3,7},{4,8},{5,9},{6,10},{7,11},{8,12},{9,13},{1... | collective-permute-start | bytes 3145736 | tf_op jit(solution)/shard_map/ppermute | solution.py:16
  56.7 20.8 %collective-permute-done.2 = f32[16,128,128]{2,1,0:T(8,128)S(1)} collective-permute-done((f32[16,128,128]{2,1,0:T(8,128)S(1)}, f32[16,128,128]{2,1,0:T(8,128)S(1)}, u32[]{:S(2)}, u32[]{:S(2)}) %collective-permute-start.2) | collective-permute-done | bytes 1048608 | tf_op jit(solution)/shard_map/ppermute | solution.py:16
  77.4 1.1 add.68
  78.6 1.4 collective-permute-start.3
  80.0 3.1 %fusion.5 = (bf16[384,2048]{1,0:T(8,128)(2,1)}, f32[384,2048]{1,0:T(8,128)}) fusion(bf16[384,2048]{1,0:T(8,128)(2,1)S(1)} %copy-done.17), kind=kLoop, calls=%fused_computation.13 | loop fusion | flops 5505024 | bytes 6291456 | tf_op jit(solution)/shard_map/convert.1
  83.0 2.1 copy.9
  85.2 1.9 copy.37
  87.1 3.1 %select_convert_fusion.1 = bf16[16,384,384]{2,1,0:T(8,128)(2,1)S(1)} fusion(pred[384,384]{1,0:T(8,128)(4,1)S(1)} %iota_compare_fusion, bf16[384,16,128]{0,2,1:T(8,128)(2,1)S(1)} %bitcast.76, bf16[48,16,8,128]{3,2,1,0:T(8,128)(2,1)} %get-tuple-element.11), kind=kOutput, calls=%fused_computation.1 | convolution fusion | flops 608698368 | bytes 8011776 | tf_op jit(solution)/shard_map/thd,shd->hts/dot_general | solution.py:43
  90.2 1.6 fusion.10
  92.3 11.0 %collective-permute-done.3 = f32[16,128,128]{2,1,0:T(8,128)} collective-permute-done((f32[16,128,128]{2,1,0:T(8,128)}, f32[16,128,128]{2,1,0:T(8,128)}, u32[]{:S(2)}, u32[]{:S(2)}) %collective-permute-start.3) | collective-permute-done | bytes 1048608 | tf_op jit(solution)/shard_map/ppermute | solution.py:16
  103.3 1.8 subtract_convert_fusion.1
  105.1 0.7 multiply_reduce_fusion.2
  105.9 1.3 copy-done.1
  107.2 1.3 multiply_reduce_fusion
  108.5 0.8 divide_convert_fusion
  109.3 0.8 fusion.28
  110.1 23.0 %collective-permute-start.4 = (f32[16,128,128]{2,1,0:T(8,128)S(1)}, f32[16,128,128]{2,1,0:T(8,128)S(1)}, u32[]{:S(2)}, u32[]{:S(2)}) collective-permute-start(f32[16,128,128]{2,1,0:T(8,128)S(1)} %fusion.28), channel_id=1, source_target_pairs={{1,0},{2,1},{3,2},{4,3},{5,4},{6,5},{7,6},{8,7},{9,8},{10,9},{11,1... | collective-permute-start | bytes 3145736 | tf_op jit(solution)/shard_map/ppermute | solution.py:16
  133.1 12.3 %collective-permute-done.4 = f32[16,128,128]{2,1,0:T(8,128)S(1)} collective-permute-done((f32[16,128,128]{2,1,0:T(8,128)S(1)}, f32[16,128,128]{2,1,0:T(8,128)S(1)}, u32[]{:S(2)}, u32[]{:S(2)}) %collective-permute-start.4) | collective-permute-done | bytes 1048608 | tf_op jit(solution)/shard_map/ppermute | solution.py:16
  145.6 3.8 %collective-permute-start.5 = (f32[16,128,128]{2,1,0:T(8,128)S(1)}, f32[16,128,128]{2,1,0:T(8,128)S(1)}, u32[]{:S(2)}, u32[]{:S(2)}) collective-permute-start(f32[16,128,128]{2,1,0:T(8,128)S(1)} %add.75), channel_id=1, source_target_pairs={{2,0},{3,1},{4,2},{5,3},{6,4},{7,5},{8,6},{9,7},{10,8},{11,9},{12,... | collective-permute-start | bytes 3145736 | tf_op jit(solution)/shard_map/ppermute | solution.py:16
  149.4 23.2 %collective-permute-done.5 = f32[16,128,128]{2,1,0:T(8,128)S(1)} collective-permute-done((f32[16,128,128]{2,1,0:T(8,128)S(1)}, f32[16,128,128]{2,1,0:T(8,128)S(1)}, u32[]{:S(2)}, u32[]{:S(2)}) %collective-permute-start.5) | collective-permute-done | bytes 1048608 | tf_op jit(solution)/shard_map/ppermute | solution.py:16
  172.7 1.1 add.76
  173.7 2.9 collective-permute-start.6
  176.6 3.5 %copy.21 = f32[384,2048]{0,1:T(8,128)} copy(f32[384,2048]{1,0:T(8,128)} %get-tuple-element.14) | data formatting | bytes 6291456 | tf_op jit(solution)/shard_map/jit(_where)/select_n | solution.py:24
  180.1 3.5 %copy.26 = f32[384,2048]{0,1:T(8,128)} copy(f32[384,2048]{1,0:T(8,128)} %get-tuple-element.10) | data formatting | bytes 6291456 | tf_op jit(solution)/shard_map/jit(_where)/select_n | solution.py:24
  183.7 3.2 %select_convert_fusion = bf16[16,384,384]{2,1,0:T(8,128)(2,1)S(1)} fusion(pred[384,384]{1,0:T(8,128)(4,1)S(1)} %iota_compare_fusion, bf16[384,16,128]{0,2,1:T(8,128)(2,1)} %copy-done.2, bf16[384,2048]{1,0:T(8,128)(2,1)S(1)} %copy-done), kind=kOutput, calls=%fused_computation | convolution fusion | flops 608698368 | bytes 8011776 | tf_op jit(solution)/shard_map/the,she->hts/dot_general | solution.py:64
  186.9 1.6 fusion.26
  188.5 0.8 copy-done.5
  189.3 12.7 %collective-permute-done.6 = f32[16,128,128]{2,1,0:T(8,128)} collective-permute-done((f32[16,128,128]{2,1,0:T(8,128)}, f32[16,128,128]{2,1,0:T(8,128)}, u32[]{:S(2)}, u32[]{:S(2)}) %collective-permute-start.6) | collective-permute-done | bytes 1048608 | tf_op jit(solution)/shard_map/ppermute | solution.py:16
  202.0 2.6 add.77
  204.6 3.1 %collective-permute-start.7 = (f32[16,128,128]{2,1,0:T(8,128)}, f32[16,128,128]{2,1,0:T(8,128)}, u32[]{:S(2)}, u32[]{:S(2)}) collective-permute-start(f32[16,128,128]{2,1,0:T(8,128)} %add.77), channel_id=1, source_target_pairs={{8,0},{9,1},{10,2},{11,3},{12,4},{13,5},{14,6},{15,7},{24,16},{25,... | collective-permute-start | bytes 3145736 | tf_op jit(solution)/shard_map/ppermute | solution.py:16
  207.7 2.0 fusion.9
  209.6 2.6 copy.29
  212.2 60.8 %psum.7 = f32[2048]{0:T(1024)} all-reduce(f32[2048]{0:T(1024)S(1)} %bitcast.88), channel_id=1, replica_groups=mesh['groups'=2,'seq'=16] {'seq'}, use_global_device_ids=true, to_apply=%region_3.4 | all-reduce | flops 2048 | bytes 16384 | tf_op jit(solution)/shard_map/psum | solution.py:63
  273.1 4.0 %fusion.29 = f32[16,128,384]{2,1,0:T(8,128)S(1)} fusion(bf16[384,16,128]{0,2,1:T(8,128)(2,1)} %copy-done.2, bf16[16,384,384]{2,1,0:T(8,128)(2,1)} %copy-done.4), kind=kOutput, calls=%fused_computation.51 | convolution fusion | flops 603979776 | bytes 9437184 | tf_op jit(solution)/shard_map/hts,the->she/dot_general | solution.py:76
  277.1 5.3 %fusion.27 = f32[16,128,384]{2,1,0:T(8,128)} fusion(bf16[384,16,128]{0,2,1:T(8,128)(2,1)S(1)} %bitcast.79, bf16[16,384,384]{2,1,0:T(8,128)(2,1)} %copy-done.5), kind=kOutput, calls=%fused_computation.49 | convolution fusion | flops 603979776 | bytes 9437184 | tf_op jit(solution)/shard_map/hts,thd->shd/dot_general | solution.py:72
  282.4 1.9 subtract_convert_fusion
  284.5 0.8 add_convert_fusion
  285.3 1.6 copy.31
  286.9 3.8 %fusion.8 = bf16[384,16,128]{0,2,1:T(8,128)(2,1)S(1)} fusion(f32[384,16,128]{0,2,1:T(8,128)} %bitcast.80, f32[16,128,384]{2,1,0:T(8,128)} %fusion.27, bf16[16,128,128]{2,1,0:T(8,128)(2,1)} %copy-done.16, bf16[384,2048]{1,0:T(8,128)(2,1)S(1)} %copy-done), kind=kOutput, calls=%fused_computation.17 | convolution fusion | flops 203685888 | bytes 9961472 | tf_op jit(solution)/shard_map/the,hde->thd/dot_general | solution.py:73
  290.7 1.6 copy.30
  (45 shorter events, 1.2 us)
Async XLA Ops:
  0.6 8.4 %copy-start = (bf16[384,2048]{1,0:T(8,128)(2,1)S(1)}, bf16[384,2048]{1,0:T(8,128)(2,1)}, u32[]{:S(2)}) copy-start(bf16[384,2048]{1,0:T(8,128)(2,1)} %param.7) | copy-start | bytes 4718596
  9.0 17.8 %copy-start.6 = (bf16[384,16,128]{0,2,1:T(8,128)(2,1)}, bf16[384,16,128]{0,2,1:T(8,128)(2,1)S(1)}, u32[]{:S(2)}) copy-start(bf16[384,16,128]{0,2,1:T(8,128)(2,1)S(1)} %copy.19) | copy-start | bytes 4718596
  9.6 43.4 %copy-start.11 = (f32[16,128,128]{2,1,0:T(8,128)}, f32[16,128,128]{2,1,0:T(8,128)S(1)}, u32[]{:S(2)}) copy-start(f32[16,128,128]{2,1,0:T(8,128)S(1)} %fusion.14) | copy-start | bytes 3145732
  9.6 17.0 %collective-permute-start = (f32[16,128,128]{2,1,0:T(8,128)S(1)}, f32[16,128,128]{2,1,0:T(8,128)S(1)}, u32[]{:S(2)}, u32[]{:S(2)}) collective-permute-start(f32[16,128,128]{2,1,0:T(8,128)S(1)} %fusion.14), channel_id=1, source_target_pairs={{0,1},{1,2},{2,3},{3,4},{4,5},{5,6},{6,7},{7,8},{8,9},{9,10},{10,1... | collective-permute-start | bytes 3145736 | tf_op jit(solution)/shard_map/ppermute | solution.py:16
  26.8 26.1 %collective-permute-start.1 = (f32[16,128,128]{2,1,0:T(8,128)S(1)}, f32[16,128,128]{2,1,0:T(8,128)S(1)}, u32[]{:S(2)}, u32[]{:S(2)}) collective-permute-start(f32[16,128,128]{2,1,0:T(8,128)S(1)} %add.66), channel_id=1, source_target_pairs={{0,2},{1,3},{2,4},{3,5},{4,6},{5,7},{6,8},{7,9},{8,10},{9,11},{10,... | collective-permute-start | bytes 3145736 | tf_op jit(solution)/shard_map/ppermute | solution.py:16
  53.0 27.0 %copy-start.17 = (bf16[384,2048]{1,0:T(8,128)(2,1)S(1)}, bf16[384,2048]{1,0:T(8,128)(2,1)}, u32[]{:S(2)}) copy-start(bf16[384,2048]{1,0:T(8,128)(2,1)} %param.5) | copy-start | bytes 4718596
  53.0 24.4 %collective-permute-start.2 = (f32[16,128,128]{2,1,0:T(8,128)S(1)}, f32[16,128,128]{2,1,0:T(8,128)S(1)}, u32[]{:S(2)}, u32[]{:S(2)}) collective-permute-start(f32[16,128,128]{2,1,0:T(8,128)S(1)} %add.67), channel_id=1, source_target_pairs={{0,4},{1,5},{2,6},{3,7},{4,8},{5,9},{6,10},{7,11},{8,12},{9,13},{1... | collective-permute-start | bytes 3145736 | tf_op jit(solution)/shard_map/ppermute | solution.py:16
  78.6 4.5 %copy-start.18 = (bf16[384,2048]{1,0:T(8,128)(2,1)S(1)}, bf16[384,2048]{1,0:T(8,128)(2,1)}, u32[]{:S(2)}) copy-start(bf16[384,2048]{1,0:T(8,128)(2,1)} %param.8) | copy-start | bytes 4718596
  78.6 24.8 %collective-permute-start.3 = (f32[16,128,128]{2,1,0:T(8,128)}, f32[16,128,128]{2,1,0:T(8,128)}, u32[]{:S(2)}, u32[]{:S(2)}) collective-permute-start(f32[16,128,128]{2,1,0:T(8,128)} %add.68), channel_id=1, source_target_pairs={{0,8},{1,9},{2,10},{3,11},{4,12},{5,13},{6,14},{7,15},{16,24},{17,... | collective-permute-start | bytes 3145736 | tf_op jit(solution)/shard_map/ppermute | solution.py:16
  90.2 2.1 copy-start.4
  90.2 13.1 %copy-start.12 = (f32[16,128,128]{2,1,0:T(8,128)S(1)}, f32[16,128,128]{2,1,0:T(8,128)}, u32[]{:S(2)}) copy-start(f32[16,128,128]{2,1,0:T(8,128)} %copy-done.11) | copy-start | bytes 3145732
  105.1 0.8 copy-start.14
  105.1 2.1 copy-start.1
  105.1 2.1 copy-start.19
  109.3 36.3 %copy-start.2 = (bf16[384,16,128]{0,2,1:T(8,128)(2,1)}, bf16[384,16,128]{0,2,1:T(8,128)(2,1)S(1)}, u32[]{:S(2)}) copy-start(bf16[384,16,128]{0,2,1:T(8,128)(2,1)S(1)} %divide_convert_fusion) | copy-start | bytes 4718596
  110.1 63.6 %copy-start.9 = (f32[16,128,128]{2,1,0:T(8,128)}, f32[16,128,128]{2,1,0:T(8,128)S(1)}, u32[]{:S(2)}) copy-start(f32[16,128,128]{2,1,0:T(8,128)S(1)} %fusion.28) | copy-start | bytes 3145732
  110.1 35.3 %collective-permute-start.4 = (f32[16,128,128]{2,1,0:T(8,128)S(1)}, f32[16,128,128]{2,1,0:T(8,128)S(1)}, u32[]{:S(2)}, u32[]{:S(2)}) collective-permute-start(f32[16,128,128]{2,1,0:T(8,128)S(1)} %fusion.28), channel_id=1, source_target_pairs={{1,0},{2,1},{3,2},{4,3},{5,4},{6,5},{7,6},{8,7},{9,8},{10,9},{11,1... | collective-permute-start | bytes 3145736 | tf_op jit(solution)/shard_map/ppermute | solution.py:16
  145.6 27.1 %collective-permute-start.5 = (f32[16,128,128]{2,1,0:T(8,128)S(1)}, f32[16,128,128]{2,1,0:T(8,128)S(1)}, u32[]{:S(2)}, u32[]{:S(2)}) collective-permute-start(f32[16,128,128]{2,1,0:T(8,128)S(1)} %add.75), channel_id=1, source_target_pairs={{2,0},{3,1},{4,2},{5,3},{6,4},{7,5},{8,6},{9,7},{10,8},{11,9},{12,... | collective-permute-start | bytes 3145736 | tf_op jit(solution)/shard_map/ppermute | solution.py:16
  173.7 28.2 %collective-permute-start.6 = (f32[16,128,128]{2,1,0:T(8,128)}, f32[16,128,128]{2,1,0:T(8,128)}, u32[]{:S(2)}, u32[]{:S(2)}) collective-permute-start(f32[16,128,128]{2,1,0:T(8,128)} %add.76), channel_id=1, source_target_pairs={{4,0},{5,1},{6,2},{7,3},{8,4},{9,5},{10,6},{11,7},{12,8},{13,9},{1... | collective-permute-start | bytes 3145736 | tf_op jit(solution)/shard_map/ppermute | solution.py:16
  183.7 3.2 %copy-start.7 = (bf16[384,16,128]{0,2,1:T(8,128)(2,1)S(1)}, bf16[384,16,128]{0,2,1:T(8,128)(2,1)}, u32[]{:S(2)}) copy-start(bf16[384,16,128]{0,2,1:T(8,128)(2,1)} %copy-done.6) | copy-start | bytes 4718596
  186.9 2.4 copy-start.5
  186.9 20.8 %copy-start.8 = (f32[384,2048]{0,1:T(8,128)S(1)}, f32[384,2048]{0,1:T(8,128)}, u32[]{:S(2)}) copy-start(f32[384,2048]{0,1:T(8,128)} %copy.21) | copy-start | bytes 9437188
  189.3 18.4 %copy-start.3 = (bf16[384,16,128]{0,2,1:T(8,128)(2,1)S(1)}, bf16[384,16,128]{0,2,1:T(8,128)(2,1)}, u32[]{:S(2)}) copy-start(bf16[384,16,128]{0,2,1:T(8,128)(2,1)} %copy-done.2) | copy-start | bytes 4718596
  189.3 18.4 %copy-start.15 = (bf16[16,128,128]{2,1,0:T(8,128)(2,1)S(1)}, bf16[16,128,128]{2,1,0:T(8,128)(2,1)}, u32[]{:S(2)}) copy-start(bf16[16,128,128]{2,1,0:T(8,128)(2,1)} %copy-done.14) | copy-start | bytes 1572868
  204.6 77.8 %collective-permute-start.7 = (f32[16,128,128]{2,1,0:T(8,128)}, f32[16,128,128]{2,1,0:T(8,128)}, u32[]{:S(2)}, u32[]{:S(2)}) collective-permute-start(f32[16,128,128]{2,1,0:T(8,128)} %add.77), channel_id=1, source_target_pairs={{8,0},{9,1},{10,2},{11,3},{12,4},{13,5},{14,6},{15,7},{24,16},{25,... | collective-permute-start | bytes 3145736 | tf_op jit(solution)/shard_map/ppermute | solution.py:16
  277.1 5.3 %copy-start.10 = (f32[16,128,128]{2,1,0:T(8,128)S(1)}, f32[16,128,128]{2,1,0:T(8,128)}, u32[]{:S(2)}) copy-start(f32[16,128,128]{2,1,0:T(8,128)} %copy-done.9) | copy-start | bytes 3145732
  282.4 2.0 copy-start.13
  284.5 0.8 copy-start.16
where the time goes:
time: 293 us; the launch traced here: 292 us
  waiting for transfers between devices  119 us (41%)
  blocking collectives  60.8 us (21%)
  starting transfers between devices  42.2 us (14%)
  matrix products  27.4 us (9%)
  local copies, waits for them, and re-layouts  23.4 us (8%)
  other arithmetic  18.8 us (6%)
    ppermute x8, waiting for transfers between devices, shifted(): lax.ppermute(value, axis, [(source, source + steps) for source in range(f...  119 us
    psum x1, blocking collectives, on_device(): gain_total = lax.psum(gain_part, 'seq')  60.8 us
    ppermute x8, starting transfers between devices, shifted(): lax.ppermute(value, axis, [(source, source + steps) for source in range(f...  42.2 us
    unnamed x44, local copies, waits for them, and re-layouts  10.2 us
    select_n x2, local copies, waits for them, and re-layouts, slope(): return jnp.where(x > 0, 1.0, jnp.exp(jnp.minimum(x, 0.0)))  7.07 us
  transfers between devices with their start and end apart: 8, of which 7 were waited for; matrix products, arithmetic and copies ran while one was open for 13% of the time, Pallas kernels for 0%

commit v1 on v0

v1 whole, which is shorter than its diff:
```python
import functools

import jax
import jax.numpy as jnp
from jax import lax
from jax.experimental import pallas as pl
from jax.experimental.pallas import tpu as pltpu
from jax.sharding import PartitionSpec as P

HEADS = 16
HEAD = 128
TILE = 128
GROUP = 2
norm_eps = 1e-05
f32 = jnp.float32
bf16 = jnp.bfloat16


def decay(x):
    return jnp.exp(jnp.minimum(x, 0.0))


def feature(x):
    return jnp.where(x > 0, x + 1.0, decay(x)).astype(bf16)


def mm(a, b):
    return lax.dot_general(a, b, (((1,), (0,)), ((), ())), preferred_element_type=f32)


def mm_nt(a, b):
    return lax.dot_general(a, b, (((1,), (1,)), ((), ())), preferred_element_type=f32)


def mm_tn(a, b):
    return lax.dot_general(a, b, (((0,), (0,)), ((), ())), preferred_element_type=f32)


def cols(head):
    return slice(head * HEAD, (head + 1) * HEAD)


def lower(rows, depth, length):
    keep = lax.broadcasted_iota(jnp.int32, (TILE, TILE), 0) >= lax.broadcasted_iota(
        jnp.int32, (TILE, TILE), 1
    )
    strips = []
    for start in range(0, length, TILE):
        strip = mm_nt(rows[start : start + TILE], depth[: start + TILE])
        last = jnp.where(keep, strip[:, start:], 0.0).astype(bf16)
        if start:
            last = jnp.concatenate([strip[:, :start].astype(bf16), last], axis=1)
        strips.append(last)
    return strips


def upper(rows, depth, length):
    keep = lax.broadcasted_iota(jnp.int32, (TILE, TILE), 0) <= lax.broadcasted_iota(
        jnp.int32, (TILE, TILE), 1
    )
    strips = []
    for start in range(0, length, TILE):
        strip = mm_nt(rows[start : start + TILE], depth[start:])
        first = jnp.where(keep, strip[:, :TILE], 0.0).astype(bf16)
        if start + TILE < length:
            first = jnp.concatenate([first, strip[:, TILE:].astype(bf16)], axis=1)
        strips.append(first)
    return strips


def state_kernel(_, key_ref, value_ref, own_ref):
    for head in range(GROUP):
        key_map = feature(key_ref[:, cols(head)].astype(f32))
        own_ref[cols(head), :] = mm_tn(key_map, value_ref[:, cols(head)]).astype(bf16)


def inner_kernel(query_ref, key_ref, value_ref, mixed_ref):
    length = query_ref.shape[0]
    for head in range(GROUP):
        at = cols(head)
        query_map = feature(query_ref[:, at].astype(f32))
        key_map = feature(key_ref[:, at].astype(f32))
        value = value_ref[:, at]
        for i, strip in enumerate(lower(query_map, key_map, length)):
            start = i * TILE
            mixed_ref[start : start + TILE, at] = mm(strip, value[: start + TILE])


def norm_kernel(_, query_ref, cotan_ref, gain_ref, state_ref, mixed_ref, *refs):
    grad_ref, own_ref, part_ref = refs[-3:]
    for head in range(GROUP):
        at = cols(head)
        query_map = feature(query_ref[:, at].astype(f32))
        mixed = mixed_ref[:, at] + mm(query_map, state_ref[at, :])
        inverse = lax.rsqrt(jnp.mean(mixed * mixed, axis=1, keepdims=True) + norm_eps)
        normed = mixed * inverse
        cotan = cotan_ref[:, at].astype(f32)
        part_ref[:, at] = jnp.sum(cotan * normed, axis=0, keepdims=True)
        scaled = cotan * gain_ref[:, at]
        along = jnp.mean(scaled * normed, axis=1, keepdims=True)
        grad = ((scaled - normed * along) * inverse).astype(bf16)
        grad_ref[:, at] = grad
        own_ref[at, :] = mm_tn(query_map, grad).astype(bf16)


def back_kernel(query_ref, key_ref, value_ref, grad_ref, state_ref, dq_ref, dk_ref, dv_ref):
    length = query_ref.shape[0]
    for head in range(GROUP):
        at = cols(head)
        query = query_ref[:, at].astype(f32)
        query_map = feature(query)
        key_map = feature(key_ref[:, at].astype(f32))
        value = value_ref[:, at]
        grad = grad_ref[:, at]
        far = mm_nt(grad, state_ref[at, :])
        slope = decay(query)
        for i, strip in enumerate(lower(grad, value, length)):
            rows = slice(i * TILE, (i + 1) * TILE)
            near = mm(strip, key_map[: (i + 1) * TILE])
            dq_ref[rows, at] = ((near + far[rows]) * slope[rows]).astype(bf16)
        for i, strip in enumerate(upper(value, grad, length)):
            rows = slice(i * TILE, (i + 1) * TILE)
            dk_ref[rows, at] = mm(strip, query_map[i * TILE :])
        for i, strip in enumerate(upper(key_map, query_map, length)):
            rows = slice(i * TILE, (i + 1) * TILE)
            dv_ref[rows, at] = mm(strip, grad[i * TILE :])


def last_kernel(_, key_ref, value_ref, back_ref, dk_ref, dv_ref, *refs):
    key_grad_ref, value_grad_ref = refs[-2:]
    for head in range(GROUP):
        at = cols(head)
        key = key_ref[:, at].astype(f32)
        back = back_ref[at, :]
        far = mm_nt(value_ref[:, at], back)
        key_grad_ref[:, at] = ((dk_ref[:, at] + far) * decay(key)).astype(bf16)
        value_grad_ref[:, at] = (dv_ref[:, at] + mm(feature(key), back)).astype(bf16)


def call(kernel, half, ins, outs, steps, kept=()):
    picks = half is not None

    def spec(kind, shape):
        offset = picks and not (
            (kind == "state" and shape[0] == steps * GROUP * HEAD)
            or (kind != "state" and shape[1] == steps * GROUP * HEAD)
        )

        def place(j, *refs):
            j = refs[0][0] * steps + j if offset else j
            return (j, 0) if kind == "state" else (0, j)

        block = (GROUP * HEAD, HEAD) if kind == "state" else (shape[0], GROUP * HEAD)
        return pl.BlockSpec(block, place)

    out_shapes = [jax.ShapeDtypeStruct(shape, dtype) for _, shape, dtype in outs]
    grid_spec = pltpu.PrefetchScalarGridSpec(
        num_scalar_prefetch=int(picks),
        grid=(steps,),
        in_specs=[spec(kind, a.shape) for kind, a in ins]
        + [pl.BlockSpec(memory_space=pl.ANY)] * len(kept),
        out_specs=[spec(kind, shape) for kind, shape, _ in outs],
    )
    first = int(picks) + len(ins)
    return pl.pallas_call(
        kernel,
        out_shape=out_shapes,
        grid_spec=grid_spec,
        input_output_aliases={first + i: i for i in range(len(kept))},
        compiler_params=pltpu.CompilerParams(vmem_limit_bytes=40 << 20),
    )(*([half] if picks else []), *[a for _, a in ins], *kept)


def permute(value, pairs):
    return lax.ppermute(value, "seq", pairs)


def sum_low(*terms):
    return functools.reduce(lambda a, b: a + b, [t.astype(f32) for t in terms]).astype(bf16)


def part(value, index, rows):
    return lax.dynamic_slice_in_dim(value, index * rows, rows, 0)


class Scan:
    def __init__(self, shards, reverse):
        index = lax.axis_index("seq")
        self.shards = shards
        self.sign = -1 if reverse else 1
        self.core = (1 - index % 2) if reverse else index % 2
        self.chip = (1 - index // 2 % 2) if reverse else index // 2 % 2
        self.swap_core = [(i, i ^ 1) for i in range(shards)]
        self.swap_chip = [(i, i ^ 2) for i in range(shards)]

    def shift(self, value, fours):
        step = 4 * fours * self.sign
        pairs = [(i, i + step) for i in range(self.shards) if 0 <= i + step < self.shards]
        return permute(value, pairs)

    def before(self, total):
        count = self.shards // 4
        if count <= 4:
            return [self.shift(total, k) for k in range(count - 1, 0, -1)]
        running, step = self.shift(total, 1), 1
        while step < count - 1:
            running = sum_low(running, self.shift(running, step))
            step *= 2
        return [running]

    def start(self, theirs):
        return permute(theirs, self.swap_core)

    def totals(self, mine, got):
        rows = mine.shape[0] // 2
        self.mine, self.got = mine, got
        send = sum_low(part(mine, 1 - self.chip, rows), part(got, 1 - self.chip, rows))
        self.near = sum_low(part(mine, self.chip, rows), part(got, self.chip, rows))
        self.other = permute(send, self.swap_chip)
        return sum_low(self.near, self.other)

    def finish(self, earlier):
        base = functools.reduce(lambda a, b: a + b, [e.astype(f32) for e in earlier])
        first = jnp.where(self.chip == 0, self.near, self.other).astype(f32)
        low, high = base.astype(bf16), (base + first).astype(bf16)
        keep = jnp.where(self.chip == 0, low, high)
        back = permute(jnp.where(self.chip == 0, high, low), self.swap_chip)
        half = jnp.where(
            self.chip == 0, jnp.concatenate([keep, back]), jnp.concatenate([back, keep])
        )
        first = jnp.where(self.core == 0, self.mine, self.got)
        low, high = half, sum_low(half, first)
        mine = jnp.where(self.core == 0, low, high)
        theirs = permute(jnp.where(self.core == 0, high, low), self.swap_core)
        return mine, theirs


def on_device(queries, key_vectors, value_vectors, out_cotangent, norm_gain):
    length, width = queries.shape
    shards = lax.axis_size("seq")
    steps = HEADS // GROUP
    core = lax.axis_index("seq") % 2
    mine = core.astype(jnp.int32).reshape(1)
    theirs = 1 - mine
    gain = norm_gain.reshape(1, width)
    half_state = ("state", (width // 2, HEAD), bf16)

    def own_of(half):
        return call(
            state_kernel, half, [("tok", key_vectors), ("tok", value_vectors)], [half_state], steps // 2
        )[0]

    fore = Scan(shards, False)
    sent = own_of(theirs)
    got = fore.start(sent)
    total = fore.totals(own_of(mine), got)
    earlier = fore.before(total)
    (inner_queries, _) = lax.optimization_barrier((queries, total))
    (inner,) = call(
        inner_kernel,
        None,
        [("tok", inner_queries), ("tok", key_vectors), ("tok", value_vectors)],
        [("tok", (length, width), f32)],
        steps,
    )
    state_mine, state_theirs = fore.finish(earlier)

    def norm_of(half, state, kept):
        return call(
            norm_kernel,
            half,
            [
                ("tok", queries),
                ("tok", out_cotangent),
                ("row", gain),
                ("state", state),
                ("tok", inner),
            ],
            [("tok", (length, width), bf16), half_state, ("row", (1, width // 2), f32)],
            steps // 2,
            kept,
        )

    aft = Scan(shards, True)
    grad, sent, part_mine = norm_of(mine, state_mine, ())
    got = aft.start(sent)
    grad, own, part_theirs = norm_of(theirs, state_theirs, (grad,))
    gain_part = jnp.where(
        core == 0,
        jnp.concatenate([part_mine, part_theirs], 1),
        jnp.concatenate([part_theirs, part_mine], 1),
    )
    gain_total = jnp.sum(lax.all_gather(gain_part.reshape(HEADS, HEAD), "seq"), axis=0)
    total = aft.totals(own, got)
    later = aft.before(total)
    state = jnp.where(
        core == 0,
        jnp.concatenate([state_mine, state_theirs]),
        jnp.concatenate([state_theirs, state_mine]),
    )
    (back_grad, _) = lax.optimization_barrier((grad, total))
    query_grad, key_inner, value_inner = call(
        back_kernel,
        None,
        [
            ("tok", queries),
            ("tok", key_vectors),
            ("tok", value_vectors),
            ("tok", back_grad),
            ("state", state),
        ],
        [("tok", (length, width), bf16), ("tok", (length, width), f32), ("tok", (length, width), f32)],
        steps,
    )
    back_theirs, back_mine = aft.finish(later)

    def last_of(half, back, kept):
        return call(
            last_kernel,
            half,
            [
                ("tok", key_vectors),
                ("tok", value_vectors),
                ("state", back),
                ("tok", key_inner),
                ("tok", value_inner),
            ],
            [("tok", (length, width), bf16)] * 2,
            steps // 2,
            kept,
        )

    grads = last_of(theirs, back_theirs, ())
    key_grad, value_grad = last_of(mine, back_mine, tuple(grads))
    return query_grad, key_grad, value_grad, gain_total.reshape(width)


def solution(mesh):
    tokens = P(("groups", "seq"), None)
    return jax.shard_map(
        on_device,
        mesh=mesh,
        in_specs=(tokens, tokens, tokens, tokens, P()),
        out_specs=(tokens, tokens, tokens, P("groups")),
        check_vma=False,
    )
```

time: 293 us -> 122 us (0.42)
  the two profiles are of different devices: /device:TPU:16 before, /device:TPU:0 now
where the time goes in v1:
time: 122 us; the launch traced here: 121 us
  Pallas kernels  34.4 us (28%)
  waiting for transfers between devices  23.8 us (20%)
  starting transfers between devices  23.3 us (19%)
  blocking collectives  19 us (16%)
  other arithmetic  11.8 us (10%)
  local copies, waits for them, and re-layouts  8.22 us (7%)
    pallas_call x8, Pallas kernels, call(): pl.pallas_call(kernel, out_shape=out_shapes, grid_spec=grid_spec, input_o...  34.4 us
    ppermute x14, waiting for transfers between devices, permute(): return lax.ppermute(value, 'seq', pairs)  23.8 us
    ppermute x14, starting transfers between devices, permute(): return lax.ppermute(value, 'seq', pairs)  23.3 us
    all_gather x1, blocking collectives, on_device(): lax.all_gather(gain_part.reshape(HEADS, HEAD), 'seq')  19 us
    unnamed x38, local copies, waits for them, and re-layouts  8.22 us
    convert_element_type x4, other arithmetic, sum_low(): functools.reduce(lambda a, b: a + b, [t.astype(f32) for t in terms])  3.95 us
    select_n x2, other arithmetic, finish(): back = permute(jnp.where(self.chip == 0, high, low), self.swap_chip)  2.62 us
  transfers between devices with their start and end apart: 14, of which 6 were waited for; matrix products, arithmetic and copies ran while one was open for 3% of the time, Pallas kernels for 23%

profile of v1, /device:TPU:0, one launch (start us, length us, event | category | flops | bytes accessed | tf_op | source)
XLA Modules:
  0.0 121.3 jit_solution(10628854243546254254)
XLA Ops:
  0.7 1.4 %copy-done = bf16[384,2048]{1,0:T(8,128)(2,1)S(1)} copy-done((bf16[384,2048]{1,0:T(8,128)(2,1)S(1)}, bf16[384,2048]{1,0:T(8,128)(2,1)}, u32[]{:S(2)}) %copy-start) | copy-done | bytes 1572888
  2.1 1.4 %copy-done.2 = bf16[384,2048]{1,0:T(8,128)(2,1)S(1)} copy-done((bf16[384,2048]{1,0:T(8,128)(2,1)S(1)}, bf16[384,2048]{1,0:T(8,128)(2,1)}, u32[]{:S(2)}) %copy-start.2) | copy-done | bytes 1572888
  3.5 2.3 %shard_map.85 = bf16[1024,128]{1,0:T(8,128)(2,1)} custom-call(s32[1]{0:T(128)S(6)} %sub.18._, bf16[384,2048]{1,0:T(8,128)(2,1)S(1)} %copy-done, bf16[384,2048]{1,0:T(8,128)(2,1)S(1)} %copy-done.2), custom_call_target="tpu_custom_call" | custom-call | tf_op jit(solution)/shard_map/pallas_call | solution.py:165
  5.8 0.5 collective-permute-start
  6.2 1.4 %shard_map.84 = bf16[1024,128]{1,0:T(8,128)(2,1)S(1)} custom-call(s32[1]{0:T(128)} %bitcast._, bf16[384,2048]{1,0:T(8,128)(2,1)S(1)} %copy-done.1, bf16[384,2048]{1,0:T(8,128)(2,1)S(1)} %copy-done.3), custom_call_target="tpu_custom_call" | custom-call | tf_op jit(solution)/shard_map/pallas_call | solution.py:165
  7.7 0.0 collective-permute-done
  7.7 1.6 %add_convert_fusion.8 = bf16[512,128]{1,0:T(8,128)(2,1)} fusion(bf16[1024,128]{1,0:T(8,128)(2,1)} %collective-permute-done, s32[]{:T(128)S(6)} %select_n.138, bf16[1024,128]{1,0:T(8,128)(2,1)S(1)} %shard_map.84), kind=kLoop, calls=%fused_computation.17 | loop fusion | flops 262144 | bytes 393220 | tf_op jit(solution)/shard_map/convert_element_type | solution.py:179
  9.3 2.9 %collective-permute-start.1 = (bf16[512,128]{1,0:T(8,128)(2,1)}, bf16[512,128]{1,0:T(8,128)(2,1)S(1)}, u32[]{:S(2)}, u32[]{:S(2)}) collective-permute-start(bf16[512,128]{1,0:T(8,128)(2,1)} %add_convert_fusion.8), channel_id=1, source_target_pairs={{0,2},{1,3},{2,0},{3,1},{4,6},{5,7},{6,4},{7,5},{8,10},{9,11},{10,... | collective-permute-start | bytes 393224 | tf_op jit(solution)/shard_map/ppermute | solution.py:175
  12.2 4.0 %collective-permute-done.1 = bf16[512,128]{1,0:T(8,128)(2,1)S(1)} collective-permute-done((bf16[512,128]{1,0:T(8,128)(2,1)}, bf16[512,128]{1,0:T(8,128)(2,1)S(1)}, u32[]{:S(2)}, u32[]{:S(2)}) %collective-permute-start.1) | collective-permute-done | bytes 131104 | tf_op jit(solution)/shard_map/ppermute | solution.py:175
  16.2 1.6 %add_convert_fusion.7 = bf16[512,128]{1,0:T(8,128)(2,1)} fusion(bf16[512,128]{1,0:T(8,128)(2,1)S(1)} %collective-permute-done.1, bf16[1024,128]{1,0:T(8,128)(2,1)} %collective-permute-done, s32[]{:T(128)S(6)} %select_n.137, bf16[1024,128]{1,0:T(8,128)(2,1)S(1)} %shard_map.84), kind=kLoop, calls=%fused_computation.16 | loop fusion | flops 524288 | bytes 524292 | tf_op jit(solution)/shard_map/convert_element_type | solution.py:179
  17.8 4.4 %collective-permute-start.4 = (bf16[512,128]{1,0:T(8,128)(2,1)}, bf16[512,128]{1,0:T(8,128)(2,1)}, u32[]{:S(2)}, u32[]{:S(2)}) collective-permute-start(bf16[512,128]{1,0:T(8,128)(2,1)} %add_convert_fusion.7), channel_id=1, source_target_pairs={{0,4},{1,5},{2,6},{3,7},{4,8},{5,9},{6,10},{7,11},{8,12},{9,13},{1... | collective-permute-start | bytes 393224 | tf_op jit(solution)/shard_map/ppermute | solution.py:175
  22.2 4.5 %collective-permute-start.3 = (bf16[512,128]{1,0:T(8,128)(2,1)}, bf16[512,128]{1,0:T(8,128)(2,1)}, u32[]{:S(2)}, u32[]{:S(2)}) collective-permute-start(bf16[512,128]{1,0:T(8,128)(2,1)} %add_convert_fusion.7), channel_id=1, source_target_pairs={{0,8},{1,9},{2,10},{3,11},{4,12},{5,13},{6,14},{7,15},{16,24},{17,... | collective-permute-start | bytes 393224 | tf_op jit(solution)/shard_map/ppermute | solution.py:175
  26.7 1.9 %collective-permute-start.2 = (bf16[512,128]{1,0:T(8,128)(2,1)}, bf16[512,128]{1,0:T(8,128)(2,1)}, u32[]{:S(2)}, u32[]{:S(2)}) collective-permute-start(bf16[512,128]{1,0:T(8,128)(2,1)} %add_convert_fusion.7), channel_id=1, source_target_pairs={{0,12},{1,13},{2,14},{3,15},{16,28},{17,29},{18,30},{19,31}} | collective-permute-start | bytes 393224 | tf_op jit(solution)/shard_map/ppermute | solution.py:175
  28.6 1.4 %copy-done.4 = bf16[384,2048]{1,0:T(8,128)(2,1)S(1)} copy-done((bf16[384,2048]{1,0:T(8,128)(2,1)S(1)}, bf16[384,2048]{1,0:T(8,128)(2,1)}, u32[]{:S(2)}) %copy-start.4) | copy-done | bytes 1572888
  30.0 5.5 %shard_map.86.mixed_ref = f32[384,2048]{1,0:T(8,128)S(1)} custom-call(bf16[384,2048]{1,0:T(8,128)(2,1)S(1)} %copy-done.4, bf16[384,2048]{1,0:T(8,128)(2,1)S(1)} %copy-done.1, bf16[384,2048]{1,0:T(8,128)(2,1)S(1)} %copy-done.3), custom_call_target="tpu_custom_call" | custom-call | tf_op jit(solution)/shard_map/pallas_call | solution.py:165
  35.5 0.0 copy-start.5
  35.6 1.3 %broadcast_select_fusion.4 = (bf16[512,128]{1,0:T(8,128)(2,1)S(1)}, bf16[512,128]{1,0:T(8,128)(2,1)S(1)}) fusion(pred[]{:T(512)S(6)} %eq.15, bf16[512,128]{1,0:T(8,128)(2,1)} %collective-permute-done.4, bf16[512,128]{1,0:T(8,128)(2,1)} %collective-permute-done.3, bf16[512,128]{1,0:T(8,128)(2,1)} %collective-permute-done.2, ...), kind=kLoop, calls=%fused_computation.25 | loop fusion | flops 983040 | bytes 1048581 | tf_op jit(solution)/shard_map/jit(_where)/select_n | solution.py:227
  36.9 1.6 %collective-permute-start.5 = (bf16[512,128]{1,0:T(8,128)(2,1)S(1)}, bf16[512,128]{1,0:T(8,128)(2,1)S(1)}, u32[]{:S(2)}, u32[]{:S(2)}) collective-permute-start(bf16[512,128]{1,0:T(8,128)(2,1)S(1)} %get-tuple-element.36), channel_id=1, source_target_pairs={{0,2},{1,3},{2,0},{3,1},{4,6},{5,7},{6,4},{7,5},{8,10},{9,11},{10,... | collective-permute-start | bytes 393224 | tf_op jit(solution)/shard_map/ppermute | solution.py:175
  38.5 1.1 broadcast_select_fusion.5
  39.6 2.4 %collective-permute-done.5 = bf16[512,128]{1,0:T(8,128)(2,1)S(1)} collective-permute-done((bf16[512,128]{1,0:T(8,128)(2,1)S(1)}, bf16[512,128]{1,0:T(8,128)(2,1)S(1)}, u32[]{:S(2)}, u32[]{:S(2)}) %collective-permute-start.5) | collective-permute-done | bytes 131104 | tf_op jit(solution)/shard_map/ppermute | solution.py:175
  42.0 0.2 fusion
  42.2 0.1 collective-permute-start.6
  42.3 2.9 %shard_map.87 = (bf16[384,2048]{1,0:T(8,128)(2,1)S(1)}, bf16[1024,128]{1,0:T(8,128)(2,1)S(1)}, f32[1,1024]{1,0:T(1,128)S(1)}) custom-call(s32[1]{0:T(128)} %bitcast._, bf16[384,2048]{1,0:T(8,128)(2,1)S(1)} %copy-done.5, bf16[384,2048]{1,0:T(8,128)(2,1)S(1)} %copy-done.7, f32[1,2048]{1,0:T(1,128)S(1)} %bitcast.5, ...), custom_call_target="tpu_custom_call" | custom-call | tf_op jit(solution)/shard_map/pallas_call | solution.py:165
  45.2 0.5 collective-permute-start.7
  45.7 2.8 %shard_map.88 = (bf16[384,2048]{1,0:T(8,128)(2,1)S(1)}, bf16[1024,128]{1,0:T(8,128)(2,1)S(1)}, f32[1,1024]{1,0:T(1,128)S(1)}) custom-call(s32[1]{0:T(128)S(6)} %sub.18._, bf16[384,2048]{1,0:T(8,128)(2,1)S(1)} %copy-done.5, bf16[384,2048]{1,0:T(8,128)(2,1)S(1)} %copy-done.7, f32[1,2048]{1,0:T(1,128)S(1)} %bitcast.6, ...), custom_call_target="tpu_custom_call", output_to_operand_aliasing={{0}: (6, {})} | custom-call | tf_op jit(solution)/shard_map/pallas_call | solution.py:165
  48.6 1.1 copy-done.8
  49.8 1.5 %collective-permute-start.8 = (bf16[512,128]{1,0:T(8,128)(2,1)S(1)}, bf16[512,128]{1,0:T(8,128)(2,1)S(1)}, u32[]{:S(2)}, u32[]{:S(2)}) collective-permute-start(bf16[512,128]{1,0:T(8,128)(2,1)S(1)} %add_convert_fusion.4), channel_id=1, source_target_pairs={{0,2},{1,3},{2,0},{3,1},{4,6},{5,7},{6,4},{7,5},{8,10},{9,11},{10,... | collective-permute-start | bytes 393224 | tf_op jit(solution)/shard_map/ppermute | solution.py:175
  51.3 4.0 %collective-permute-done.8 = bf16[512,128]{1,0:T(8,128)(2,1)S(1)} collective-permute-done((bf16[512,128]{1,0:T(8,128)(2,1)S(1)}, bf16[512,128]{1,0:T(8,128)(2,1)S(1)}, u32[]{:S(2)}, u32[]{:S(2)}) %collective-permute-start.8) | collective-permute-done | bytes 131104 | tf_op jit(solution)/shard_map/ppermute | solution.py:175
  55.3 0.7 add_convert_fusion.3
  56.0 1.3 %collective-permute-start.11 = (bf16[512,128]{1,0:T(8,128)(2,1)}, bf16[512,128]{1,0:T(8,128)(2,1)}, u32[]{:S(2)}, u32[]{:S(2)}) collective-permute-start(bf16[512,128]{1,0:T(8,128)(2,1)} %add_convert_fusion.3), channel_id=1, source_target_pairs={{4,0},{5,1},{6,2},{7,3},{8,4},{9,5},{10,6},{11,7},{12,8},{13,9},{1... | collective-permute-start | bytes 393224 | tf_op jit(solution)/shard_map/ppermute | solution.py:175
  57.3 1.3 %collective-permute-start.10 = (bf16[512,128]{1,0:T(8,128)(2,1)}, bf16[512,128]{1,0:T(8,128)(2,1)}, u32[]{:S(2)}, u32[]{:S(2)}) collective-permute-start(bf16[512,128]{1,0:T(8,128)(2,1)} %add_convert_fusion.3), channel_id=1, source_target_pairs={{8,0},{9,1},{10,2},{11,3},{12,4},{13,5},{14,6},{15,7},{24,16},{25,... | collective-permute-start | bytes 393224 | tf_op jit(solution)/shard_map/ppermute | solution.py:175
  58.6 1.3 %collective-permute-start.9 = (bf16[512,128]{1,0:T(8,128)(2,1)}, bf16[512,128]{1,0:T(8,128)(2,1)}, u32[]{:S(2)}, u32[]{:S(2)}) collective-permute-start(bf16[512,128]{1,0:T(8,128)(2,1)} %add_convert_fusion.3), channel_id=1, source_target_pairs={{12,0},{13,1},{14,2},{15,3},{28,16},{29,17},{30,18},{31,19}} | collective-permute-start | bytes 393224 | tf_op jit(solution)/shard_map/ppermute | solution.py:175
  60.0 4.8 %collective-permute-done.11 = bf16[512,128]{1,0:T(8,128)(2,1)} collective-permute-done((bf16[512,128]{1,0:T(8,128)(2,1)}, bf16[512,128]{1,0:T(8,128)(2,1)}, u32[]{:S(2)}, u32[]{:S(2)}) %collective-permute-start.11) | collective-permute-done | bytes 131104 | tf_op jit(solution)/shard_map/ppermute | solution.py:175
  64.7 6.3 %collective-permute-done.10 = bf16[512,128]{1,0:T(8,128)(2,1)} collective-permute-done((bf16[512,128]{1,0:T(8,128)(2,1)}, bf16[512,128]{1,0:T(8,128)(2,1)}, u32[]{:S(2)}, u32[]{:S(2)}) %collective-permute-start.10) | collective-permute-done | bytes 131104 | tf_op jit(solution)/shard_map/ppermute | solution.py:175
  71.0 1.3 %broadcast_select_fusion.2 = (bf16[512,128]{1,0:T(8,128)(2,1)S(1)}, bf16[512,128]{1,0:T(8,128)(2,1)S(1)}) fusion(pred[]{:T(512)S(6)} %eq.17, bf16[512,128]{1,0:T(8,128)(2,1)} %collective-permute-done.11, bf16[512,128]{1,0:T(8,128)(2,1)} %collective-permute-done.10, bf16[512,128]{1,0:T(8,128)(2,1)} %collective-permute-done.9, ...), kind=kLoop, calls=%fused_computation.23 | loop fusion | flops 983040 | bytes 1048581 | tf_op jit(solution)/shard_map/jit(_where)/select_n | solution.py:227
  72.3 1.6 %collective-permute-start.12 = (bf16[512,128]{1,0:T(8,128)(2,1)S(1)}, bf16[512,128]{1,0:T(8,128)(2,1)S(1)}, u32[]{:S(2)}, u32[]{:S(2)}) collective-permute-start(bf16[512,128]{1,0:T(8,128)(2,1)S(1)} %get-tuple-element.34), channel_id=1, source_target_pairs={{0,2},{1,3},{2,0},{3,1},{4,6},{5,7},{6,4},{7,5},{8,10},{9,11},{10,... | collective-permute-start | bytes 393224 | tf_op jit(solution)/shard_map/ppermute | solution.py:175
  73.8 1.1 broadcast_select_fusion.3
  75.0 2.4 %collective-permute-done.12 = bf16[512,128]{1,0:T(8,128)(2,1)S(1)} collective-permute-done((bf16[512,128]{1,0:T(8,128)(2,1)S(1)}, bf16[512,128]{1,0:T(8,128)(2,1)S(1)}, u32[]{:S(2)}, u32[]{:S(2)}) %collective-permute-start.12) | collective-permute-done | bytes 131104 | tf_op jit(solution)/shard_map/ppermute | solution.py:175
  77.3 1.0 fusion.2
  78.3 19.0 %all_gather.3 = f32[16,16,128]{2,1,0:T(8,128)S(1)} all-gather(f32[1,16,128]{2,1,0:T(8,128)S(1)} %maximum_select_fusion.3), channel_id=1, replica_groups=mesh['groups'=2,'seq'=16] {'seq'}, dimensions={0}, use_global_device_ids=true | all-gather | bytes 139264 | tf_op jit(solution)/shard_map/all_gather | solution.py:293
  97.3 0.6 reduce_sum.9
  97.9 1.2 maximum_select_fusion.state_ref
  99.1 0.0 copy-start.6
  99.1 1.4 %copy-done.6 = bf16[384,2048]{1,0:T(8,128)(2,1)S(1)} copy-done((bf16[384,2048]{1,0:T(8,128)(2,1)S(1)}, bf16[384,2048]{1,0:T(8,128)(2,1)}, u32[]{:S(2)}) %copy-start.6) | copy-done | bytes 1572888
  100.5 1.4 %copy-done.9 = bf16[384,2048]{1,0:T(8,128)(2,1)S(1)} copy-done((bf16[384,2048]{1,0:T(8,128)(2,1)S(1)}, bf16[384,2048]{1,0:T(8,128)(2,1)}, u32[]{:S(2)}) %copy-start.9) | copy-done | bytes 1572888
  101.9 12.9 %shard_map.89 = (bf16[384,2048]{1,0:T(8,128)(2,1)}, f32[384,2048]{1,0:T(8,128)S(1)}, f32[384,2048]{1,0:T(8,128)S(1)}) custom-call(bf16[384,2048]{1,0:T(8,128)(2,1)S(1)} %copy-done.6, bf16[384,2048]{1,0:T(8,128)(2,1)S(1)} %copy-done.1, bf16[384,2048]{1,0:T(8,128)(2,1)S(1)} %copy-done.3, bf16[384,2048]{1,0:T(8,128)(2,1)S(1)} %copy-done.9, ...), custom_call_target="tpu_custom_call" | custom-call | tf_op jit(solution)/shard_map/pallas_call | solution.py:165
  114.8 2.7 %shard_map.90 = (bf16[384,2048]{1,0:T(8,128)(2,1)}, bf16[384,2048]{1,0:T(8,128)(2,1)}) custom-call(s32[1]{0:T(128)S(6)} %sub.18._, bf16[384,2048]{1,0:T(8,128)(2,1)S(1)} %copy-done.1, bf16[384,2048]{1,0:T(8,128)(2,1)S(1)} %copy-done.3, bf16[1024,128]{1,0:T(8,128)(2,1)S(1)} %copy-done.15, f32[384,2048]{1,0:T(8,128)S(1)} %get-tuple-element.26.dk_ref, ...), custom_call_target="tpu_custom_call" | custom-call | tf_op jit(solution)/shard_map/pallas_call | solution.py:165
  117.5 3.8 %shard_map.91 = (bf16[384,2048]{1,0:T(8,128)(2,1)}, bf16[384,2048]{1,0:T(8,128)(2,1)}) custom-call(s32[1]{0:T(128)} %bitcast._, bf16[384,2048]{1,0:T(8,128)(2,1)S(1)} %copy-done.1, bf16[384,2048]{1,0:T(8,128)(2,1)S(1)} %copy-done.3, bf16[1024,128]{1,0:T(8,128)(2,1)} %collective-permute-done.13.back_ref, ...), custom_call_target="tpu_custom_call", output_to_operand_aliasing={{0}: (6, {}), {1}: (7, {})} | custom-call | tf_op jit(solution)/shard_map/pallas_call | solution.py:165
  (40 shorter events, 0.1 us)
Async XLA Ops:
  0.6 1.4 %copy-start = (bf16[384,2048]{1,0:T(8,128)(2,1)S(1)}, bf16[384,2048]{1,0:T(8,128)(2,1)}, u32[]{:S(2)}) copy-start(bf16[384,2048]{1,0:T(8,128)(2,1)} %key_ref.11) | copy-start | bytes 4718596
  2.1 1.4 %copy-start.2 = (bf16[384,2048]{1,0:T(8,128)(2,1)S(1)}, bf16[384,2048]{1,0:T(8,128)(2,1)}, u32[]{:S(2)}) copy-start(bf16[384,2048]{1,0:T(8,128)(2,1)} %value_ref.11) | copy-start | bytes 4718596
  3.5 2.8 %copy-start.1 = (bf16[384,2048]{1,0:T(8,128)(2,1)S(1)}, bf16[384,2048]{1,0:T(8,128)(2,1)}, u32[]{:S(2)}) copy-start(bf16[384,2048]{1,0:T(8,128)(2,1)} %key_ref.11) | copy-start | bytes 4718596
  3.5 2.8 %copy-start.3 = (bf16[384,2048]{1,0:T(8,128)(2,1)S(1)}, bf16[384,2048]{1,0:T(8,128)(2,1)}, u32[]{:S(2)}) copy-start(bf16[384,2048]{1,0:T(8,128)(2,1)} %value_ref.11) | copy-start | bytes 4718596
  5.8 2.0 %collective-permute-start = (bf16[1024,128]{1,0:T(8,128)(2,1)}, bf16[1024,128]{1,0:T(8,128)(2,1)}, u32[]{:S(2)}, u32[]{:S(2)}) collective-permute-start(bf16[1024,128]{1,0:T(8,128)(2,1)} %shard_map.85), channel_id=1, source_target_pairs={{0,1},{1,0},{2,3},{3,2},{4,5},{5,4},{6,7},{7,6},{8,9},{9,8},{10,11... | collective-permute-start | bytes 786440 | tf_op jit(solution)/shard_map/ppermute | solution.py:175
  9.3 6.9 %collective-permute-start.1 = (bf16[512,128]{1,0:T(8,128)(2,1)}, bf16[512,128]{1,0:T(8,128)(2,1)S(1)}, u32[]{:S(2)}, u32[]{:S(2)}) collective-permute-start(bf16[512,128]{1,0:T(8,128)(2,1)} %add_convert_fusion.8), channel_id=1, source_target_pairs={{0,2},{1,3},{2,0},{3,1},{4,6},{5,7},{6,4},{7,5},{8,10},{9,11},{10,... | collective-permute-start | bytes 393224 | tf_op jit(solution)/shard_map/ppermute | solution.py:175
  17.8 17.8 %collective-permute-start.4 = (bf16[512,128]{1,0:T(8,128)(2,1)}, bf16[512,128]{1,0:T(8,128)(2,1)}, u32[]{:S(2)}, u32[]{:S(2)}) collective-permute-start(bf16[512,128]{1,0:T(8,128)(2,1)} %add_convert_fusion.7), channel_id=1, source_target_pairs={{0,4},{1,5},{2,6},{3,7},{4,8},{5,9},{6,10},{7,11},{8,12},{9,13},{1... | collective-permute-start | bytes 393224 | tf_op jit(solution)/shard_map/ppermute | solution.py:175
  22.2 13.4 %collective-permute-start.3 = (bf16[512,128]{1,0:T(8,128)(2,1)}, bf16[512,128]{1,0:T(8,128)(2,1)}, u32[]{:S(2)}, u32[]{:S(2)}) collective-permute-start(bf16[512,128]{1,0:T(8,128)(2,1)} %add_convert_fusion.7), channel_id=1, source_target_pairs={{0,8},{1,9},{2,10},{3,11},{4,12},{5,13},{6,14},{7,15},{16,24},{17,... | collective-permute-start | bytes 393224 | tf_op jit(solution)/shard_map/ppermute | solution.py:175
  26.7 8.9 %collective-permute-start.2 = (bf16[512,128]{1,0:T(8,128)(2,1)}, bf16[512,128]{1,0:T(8,128)(2,1)}, u32[]{:S(2)}, u32[]{:S(2)}) collective-permute-start(bf16[512,128]{1,0:T(8,128)(2,1)} %add_convert_fusion.7), channel_id=1, source_target_pairs={{0,12},{1,13},{2,14},{3,15},{16,28},{17,29},{18,30},{19,31}} | collective-permute-start | bytes 393224 | tf_op jit(solution)/shard_map/ppermute | solution.py:175
  28.6 1.4 %copy-start.4 = (bf16[384,2048]{1,0:T(8,128)(2,1)S(1)}, bf16[384,2048]{1,0:T(8,128)(2,1)}, u32[]{:S(2)}) copy-start(bf16[384,2048]{1,0:T(8,128)(2,1)} %query_ref.6) | copy-start | bytes 4718596
  30.0 12.2 %copy-start.7 = (bf16[384,2048]{1,0:T(8,128)(2,1)S(1)}, bf16[384,2048]{1,0:T(8,128)(2,1)}, u32[]{:S(2)}) copy-start(bf16[384,2048]{1,0:T(8,128)(2,1)} %cotan_ref.3) | copy-start | bytes 4718596
  35.5 6.7 %copy-start.5 = (bf16[384,2048]{1,0:T(8,128)(2,1)S(1)}, bf16[384,2048]{1,0:T(8,128)(2,1)}, u32[]{:S(2)}) copy-start(bf16[384,2048]{1,0:T(8,128)(2,1)} %query_ref.6) | copy-start | bytes 4718596
  35.6 6.7 %copy-start.16 = (f32[2048]{0:T(1024)S(1)}, f32[2048]{0:T(1024)}, u32[]{:S(2)}) copy-start(f32[2048]{0:T(1024)} %param.9) | copy-start | bytes 24580
  36.9 5.0 %collective-permute-start.5 = (bf16[512,128]{1,0:T(8,128)(2,1)S(1)}, bf16[512,128]{1,0:T(8,128)(2,1)S(1)}, u32[]{:S(2)}, u32[]{:S(2)}) collective-permute-start(bf16[512,128]{1,0:T(8,128)(2,1)S(1)} %get-tuple-element.36), channel_id=1, source_target_pairs={{0,2},{1,3},{2,0},{3,1},{4,6},{5,7},{6,4},{7,5},{8,10},{9,11},{10,... | collective-permute-start | bytes 393224 | tf_op jit(solution)/shard_map/ppermute | solution.py:175
  42.2 3.0 %copy-start.10 = (bf16[1024,128]{1,0:T(8,128)(2,1)}, bf16[1024,128]{1,0:T(8,128)(2,1)S(1)}, u32[]{:S(2)}) copy-start(bf16[1024,128]{1,0:T(8,128)(2,1)S(1)} %get-tuple-element.40.state_ref) | copy-start | bytes 786436
  42.2 3.5 %collective-permute-start.6 = (bf16[1024,128]{1,0:T(8,128)(2,1)S(1)}, bf16[1024,128]{1,0:T(8,128)(2,1)S(1)}, u32[]{:S(2)}, u32[]{:S(2)}) collective-permute-start(bf16[1024,128]{1,0:T(8,128)(2,1)S(1)} %get-tuple-element.41), channel_id=1, source_target_pairs={{0,1},{1,0},{2,3},{3,2},{4,5},{5,4},{6,7},{7,6},{8,9},{9,8},{10,11... | collective-permute-start | bytes 786440 | tf_op jit(solution)/shard_map/ppermute | solution.py:175
  45.2 4.6 %collective-permute-start.7 = (bf16[1024,128]{1,0:T(8,128)(2,1)S(1)}, bf16[1024,128]{1,0:T(8,128)(2,1)S(1)}, u32[]{:S(2)}, u32[]{:S(2)}) collective-permute-start(bf16[1024,128]{1,0:T(8,128)(2,1)S(1)} %get-tuple-element.23), channel_id=1, source_target_pairs={{0,1},{1,0},{2,3},{3,2},{4,5},{5,4},{6,7},{7,6},{8,9},{9,8},{10,11... | collective-permute-start | bytes 786440 | tf_op jit(solution)/shard_map/ppermute | solution.py:175
  45.7 2.9 %copy-start.14 = (bf16[1024,128]{1,0:T(8,128)(2,1)}, bf16[1024,128]{1,0:T(8,128)(2,1)S(1)}, u32[]{:S(2)}) copy-start(bf16[1024,128]{1,0:T(8,128)(2,1)S(1)} %collective-permute-done.6.state_ref) | copy-start | bytes 786436
  48.6 1.1 copy-start.8
  49.7 5.6 %copy-start.12 = (bf16[1024,128]{1,0:T(8,128)(2,1)}, bf16[1024,128]{1,0:T(8,128)(2,1)S(1)}, u32[]{:S(2)}) copy-start(bf16[1024,128]{1,0:T(8,128)(2,1)S(1)} %get-tuple-element.22) | copy-start | bytes 786436
  49.7 6.3 %copy-start.17 = (bf16[1024,128]{1,0:T(8,128)(2,1)}, bf16[1024,128]{1,0:T(8,128)(2,1)S(1)}, u32[]{:S(2)}) copy-start(bf16[1024,128]{1,0:T(8,128)(2,1)S(1)} %collective-permute-done.7) | copy-start | bytes 786436
  49.8 5.5 %collective-permute-start.8 = (bf16[512,128]{1,0:T(8,128)(2,1)S(1)}, bf16[512,128]{1,0:T(8,128)(2,1)S(1)}, u32[]{:S(2)}, u32[]{:S(2)}) collective-permute-start(bf16[512,128]{1,0:T(8,128)(2,1)S(1)} %add_convert_fusion.4), channel_id=1, source_target_pairs={{0,2},{1,3},{2,0},{3,1},{4,6},{5,7},{6,4},{7,5},{8,10},{9,11},{10,... | collective-permute-start | bytes 393224 | tf_op jit(solution)/shard_map/ppermute | solution.py:175
  56.0 8.7 %collective-permute-start.11 = (bf16[512,128]{1,0:T(8,128)(2,1)}, bf16[512,128]{1,0:T(8,128)(2,1)}, u32[]{:S(2)}, u32[]{:S(2)}) collective-permute-start(bf16[512,128]{1,0:T(8,128)(2,1)} %add_convert_fusion.3), channel_id=1, source_target_pairs={{4,0},{5,1},{6,2},{7,3},{8,4},{9,5},{10,6},{11,7},{12,8},{13,9},{1... | collective-permute-start | bytes 393224 | tf_op jit(solution)/shard_map/ppermute | solution.py:175
  57.3 13.7 %collective-permute-start.10 = (bf16[512,128]{1,0:T(8,128)(2,1)}, bf16[512,128]{1,0:T(8,128)(2,1)}, u32[]{:S(2)}, u32[]{:S(2)}) collective-permute-start(bf16[512,128]{1,0:T(8,128)(2,1)} %add_convert_fusion.3), channel_id=1, source_target_pairs={{8,0},{9,1},{10,2},{11,3},{12,4},{13,5},{14,6},{15,7},{24,16},{25,... | collective-permute-start | bytes 393224 | tf_op jit(solution)/shard_map/ppermute | solution.py:175
  58.6 12.4 %collective-permute-start.9 = (bf16[512,128]{1,0:T(8,128)(2,1)}, bf16[512,128]{1,0:T(8,128)(2,1)}, u32[]{:S(2)}, u32[]{:S(2)}) collective-permute-start(bf16[512,128]{1,0:T(8,128)(2,1)} %add_convert_fusion.3), channel_id=1, source_target_pairs={{12,0},{13,1},{14,2},{15,3},{28,16},{29,17},{30,18},{31,19}} | collective-permute-start | bytes 393224 | tf_op jit(solution)/shard_map/ppermute | solution.py:175
  59.9 17.4 %copy-start.13 = (bf16[1024,128]{1,0:T(8,128)(2,1)S(1)}, bf16[1024,128]{1,0:T(8,128)(2,1)}, u32[]{:S(2)}) copy-start(bf16[1024,128]{1,0:T(8,128)(2,1)} %copy-done.12) | copy-start | bytes 786436
  59.9 17.4 %copy-start.18 = (bf16[1024,128]{1,0:T(8,128)(2,1)S(1)}, bf16[1024,128]{1,0:T(8,128)(2,1)}, u32[]{:S(2)}) copy-start(bf16[1024,128]{1,0:T(8,128)(2,1)} %copy-done.17) | copy-start | bytes 786436
  59.9 38.0 %copy-start.11 = (bf16[1024,128]{1,0:T(8,128)(2,1)S(1)}, bf16[1024,128]{1,0:T(8,128)(2,1)}, u32[]{:S(2)}) copy-start(bf16[1024,128]{1,0:T(8,128)(2,1)} %copy-done.10) | copy-start | bytes 786436
  72.3 5.0 %collective-permute-start.12 = (bf16[512,128]{1,0:T(8,128)(2,1)S(1)}, bf16[512,128]{1,0:T(8,128)(2,1)S(1)}, u32[]{:S(2)}, u32[]{:S(2)}) collective-permute-start(bf16[512,128]{1,0:T(8,128)(2,1)S(1)} %get-tuple-element.34), channel_id=1, source_target_pairs={{0,2},{1,3},{2,0},{3,1},{4,6},{5,7},{6,4},{7,5},{8,10},{9,11},{10,... | collective-permute-start | bytes 393224 | tf_op jit(solution)/shard_map/ppermute | solution.py:175
  78.3 39.2 %collective-permute-start.13 = (bf16[1024,128]{1,0:T(8,128)(2,1)}, bf16[1024,128]{1,0:T(8,128)(2,1)}, u32[]{:S(2)}, u32[]{:S(2)}) collective-permute-start(bf16[1024,128]{1,0:T(8,128)(2,1)} %get-tuple-element.39), channel_id=1, source_target_pairs={{0,1},{1,0},{2,3},{3,2},{4,5},{5,4},{6,7},{7,6},{8,9},{9,8},{10,11... | collective-permute-start | bytes 786440 | tf_op jit(solution)/shard_map/ppermute | solution.py:175
  99.1 1.4 %copy-start.6 = (bf16[384,2048]{1,0:T(8,128)(2,1)S(1)}, bf16[384,2048]{1,0:T(8,128)(2,1)}, u32[]{:S(2)}) copy-start(bf16[384,2048]{1,0:T(8,128)(2,1)} %query_ref.6) | copy-start | bytes 4718596
  100.5 1.4 %copy-start.9 = (bf16[384,2048]{1,0:T(8,128)(2,1)S(1)}, bf16[384,2048]{1,0:T(8,128)(2,1)}, u32[]{:S(2)}) copy-start(bf16[384,2048]{1,0:T(8,128)(2,1)} %copy-done.8) | copy-start | bytes 4718596
  101.9 12.9 %copy-start.15 = (bf16[1024,128]{1,0:T(8,128)(2,1)S(1)}, bf16[1024,128]{1,0:T(8,128)(2,1)}, u32[]{:S(2)}) copy-start(bf16[1024,128]{1,0:T(8,128)(2,1)} %get-tuple-element.38.back_ref) | copy-start | bytes 786436

commit v2 on v1

--- a/solution.py
+++ b/solution.py
@@ -167,7 +167,7 @@
         out_shape=out_shapes,
         grid_spec=grid_spec,
         input_output_aliases={first + i: i for i in range(len(kept))},
-        compiler_params=pltpu.CompilerParams(vmem_limit_bytes=40 << 20),
+        compiler_params=pltpu.CompilerParams(vmem_limit_bytes=16 << 20),
     )(*([half] if picks else []), *[a for _, a in ins], *kept)
 
 
@@ -235,7 +235,32 @@
         return mine, theirs
 
 
+class Butterfly:
+    def __init__(self, value, shards):
+        self.value, self.level, self.shards = value, 0, shards
+
+    def round(self):
+        if 1 << self.level < self.shards:
+            pairs = [(i, i ^ 1 << self.level) for i in range(self.shards)]
+            self.value = self.value + permute(self.value, pairs)
+            self.level += 1
+
+    def beside(self, value):
+        self.round()
+        value, self.value = lax.optimization_barrier((value, self.value))
+        return value
+
+    def total(self):
+        while 1 << self.level < self.shards:
+            self.round()
+        return self.value
+
+
 def on_device(queries, key_vectors, value_vectors, out_cotangent, norm_gain):
+    queries, key_vectors, value_vectors, out_cotangent = (
+        pltpu.with_memory_space_constraint(a, pltpu.HBM)
+        for a in (queries, key_vectors, value_vectors, out_cotangent)
+    )
     length, width = queries.shape
     shards = lax.axis_size("seq")
     steps = HEADS // GROUP
@@ -290,8 +315,8 @@
         jnp.concatenate([part_mine, part_theirs], 1),
         jnp.concatenate([part_theirs, part_mine], 1),
     )
-    gain_total = jnp.sum(lax.all_gather(gain_part.reshape(HEADS, HEAD), "seq"), axis=0)
-    total = aft.totals(own, got)
+    gains = Butterfly(gain_part.reshape(HEADS, HEAD), shards)
+    total = gains.beside(aft.totals(own, got))
     later = aft.before(total)
     state = jnp.where(
         core == 0,
@@ -312,7 +337,9 @@
         [("tok", (length, width), bf16), ("tok", (length, width), f32), ("tok", (length, width), f32)],
         steps,
     )
+    later = gains.beside(lax.optimization_barrier((*later, key_inner))[:-1])
     back_theirs, back_mine = aft.finish(later)
+    back_theirs = gains.beside(back_theirs)
 
     def last_of(half, back, kept):
         return call(
@@ -332,7 +359,7 @@
 
     grads = last_of(theirs, back_theirs, ())
     key_grad, value_grad = last_of(mine, back_mine, tuple(grads))
-    return query_grad, key_grad, value_grad, gain_total.reshape(width)
+    return query_grad, key_grad, value_grad, gains.total().reshape(width)
 
 
 def solution(mesh):

time: 122 us -> 92.7 us (0.76)
  blocking collectives: 19 us -> 0 us
  other arithmetic: 11.8 us -> 1.75 us
  Pallas kernels: 34.4 us -> 43 us
  local copies, waits for them, and re-layouts: 8.22 us -> 0.01 us
  waiting for transfers between devices: 23.8 us -> 17.4 us
  starting transfers between devices: 23.3 us -> 28.8 us
    all_gather x1 -> x0, blocking collectives: 19 us -> none  [on_device(): lax.all_gather(gain_part.reshape(HEADS, HEAD), 'seq')]
    pallas_call x8, Pallas kernels: 34.4 us -> 43 us  [call(): pl.pallas_call(kernel, out_shape=out_shapes, grid_spec=grid_spec, input_o...]
    unnamed x38 -> x2, local copies, waits for them, and re-layouts: 8.22 us -> 0.01 us
    ppermute x14 -> x18, waiting for transfers between devices: 23.8 us -> 17.4 us  [permute(): return lax.ppermute(value, 'seq', pairs)]
    ppermute x14 -> x18, starting transfers between devices: 23.3 us -> 28.8 us  [permute(): return lax.ppermute(value, 'seq', pairs)]
    convert_element_type x4, other arithmetic: 3.95 us -> 0.2 us  [sum_low(): functools.reduce(lambda a, b: a + b, [t.astype(f32) for t in terms])]
    select_n x2, other arithmetic: 2.62 us -> 0.26 us  [finish(): back = permute(jnp.where(self.chip == 0, high, low), self.swap_chip)]
    select_n x2, other arithmetic: 2.21 us -> 0.15 us  [finish(): keep = jnp.where(self.chip == 0, low, high)]
  transfers between devices with their start and end apart: 14 -> 18, of which waited for: 6 -> 6; matrix products, arithmetic and copies ran while one was open for 3% -> 1% of each run, Pallas kernels for 23% -> 39%
where the time goes in v2:
time: 92.7 us; the launch traced here: 91.9 us
  Pallas kernels  43 us (46%)
  starting transfers between devices  28.8 us (31%)
  waiting for transfers between devices  17.4 us (19%)
  other arithmetic  1.75 us (2%)
  between operations  0.95 us (1%)
    pallas_call x8, Pallas kernels, call(): pl.pallas_call(kernel, out_shape=out_shapes, grid_spec=grid_spec, input_o...  43 us
    ppermute x18, starting transfers between devices, permute(): return lax.ppermute(value, 'seq', pairs)  28.8 us
    ppermute x18, waiting for transfers between devices, permute(): return lax.ppermute(value, 'seq', pairs)  17.4 us
  transfers between devices with their start and end apart: 18, of which 6 were waited for; matrix products, arithmetic and copies ran while one was open for 1% of the time, Pallas kernels for 39%

profile of v2, /device:TPU:0, one launch (start us, length us, event | category | flops | bytes accessed | tf_op | source)
XLA Modules:
  0.0 91.9 jit_solution(6262956437506246266)
XLA Ops:
  0.6 3.0 %shard_map.85 = bf16[1024,128]{1,0:T(8,128)(2,1)S(1)} custom-call(s32[1]{0:T(128)S(6)} %sub.18._, bf16[384,2048]{1,0:T(8,128)(2,1)} %key_ref.11, bf16[384,2048]{1,0:T(8,128)(2,1)} %value_ref.11), custom_call_target="tpu_custom_call" | custom-call | tf_op jit(solution)/shard_map/pallas_call | solution.py:165
  3.6 0.5 collective-permute-start
  4.2 3.0 %shard_map.84 = bf16[1024,128]{1,0:T(8,128)(2,1)S(1)} custom-call(s32[1]{0:T(128)} %bitcast._, bf16[384,2048]{1,0:T(8,128)(2,1)} %key_ref.11, bf16[384,2048]{1,0:T(8,128)(2,1)} %value_ref.11), custom_call_target="tpu_custom_call" | custom-call | tf_op jit(solution)/shard_map/pallas_call | solution.py:165
  7.2 0.0 collective-permute-done
  7.2 2.6 %collective-permute-start.1 = (bf16[512,128]{1,0:T(8,128)(2,1)S(1)}, bf16[512,128]{1,0:T(8,128)(2,1)S(1)}, u32[]{:S(2)}, u32[]{:S(2)}) collective-permute-start(bf16[512,128]{1,0:T(8,128)(2,1)S(1)} %add_convert_fusion.8), channel_id=1, source_target_pairs={{0,2},{1,3},{2,0},{3,1},{4,6},{5,7},{6,4},{7,5},{8,10},{9,11},{10,... | collective-permute-start | bytes 393224 | tf_op jit(solution)/shard_map/ppermute | solution.py:175
  9.8 4.1 %collective-permute-done.1 = bf16[512,128]{1,0:T(8,128)(2,1)S(1)} collective-permute-done((bf16[512,128]{1,0:T(8,128)(2,1)S(1)}, bf16[512,128]{1,0:T(8,128)(2,1)S(1)}, u32[]{:S(2)}, u32[]{:S(2)}) %collective-permute-start.1) | collective-permute-done | bytes 131104 | tf_op jit(solution)/shard_map/ppermute | solution.py:175
  14.0 0.1 add_convert_fusion.7
  14.0 3.7 %collective-permute-start.4 = (bf16[512,128]{1,0:T(8,128)(2,1)S(1)}, bf16[512,128]{1,0:T(8,128)(2,1)S(1)}, u32[]{:S(2)}, u32[]{:S(2)}) collective-permute-start(bf16[512,128]{1,0:T(8,128)(2,1)S(1)} %add_convert_fusion.7), channel_id=1, source_target_pairs={{0,4},{1,5},{2,6},{3,7},{4,8},{5,9},{6,10},{7,11},{8,12},{9,13},{1... | collective-permute-start | bytes 393224 | tf_op jit(solution)/shard_map/ppermute | solution.py:175
  17.8 4.5 %collective-permute-start.3 = (bf16[512,128]{1,0:T(8,128)(2,1)S(1)}, bf16[512,128]{1,0:T(8,128)(2,1)S(1)}, u32[]{:S(2)}, u32[]{:S(2)}) collective-permute-start(bf16[512,128]{1,0:T(8,128)(2,1)S(1)} %add_convert_fusion.7), channel_id=1, source_target_pairs={{0,8},{1,9},{2,10},{3,11},{4,12},{5,13},{6,14},{7,15},{16,24},{17,... | collective-permute-start | bytes 393224 | tf_op jit(solution)/shard_map/ppermute | solution.py:175
  22.3 1.3 %collective-permute-start.2 = (bf16[512,128]{1,0:T(8,128)(2,1)S(1)}, bf16[512,128]{1,0:T(8,128)(2,1)S(1)}, u32[]{:S(2)}, u32[]{:S(2)}) collective-permute-start(bf16[512,128]{1,0:T(8,128)(2,1)S(1)} %add_convert_fusion.7), channel_id=1, source_target_pairs={{0,12},{1,13},{2,14},{3,15},{16,28},{17,29},{18,30},{19,31}} | collective-permute-start | bytes 393224 | tf_op jit(solution)/shard_map/ppermute | solution.py:175
  23.6 7.5 %shard_map.86.mixed_ref = f32[384,2048]{1,0:T(8,128)S(1)} custom-call(bf16[384,2048]{1,0:T(8,128)(2,1)} %query_ref.6, bf16[384,2048]{1,0:T(8,128)(2,1)} %key_ref.11, bf16[384,2048]{1,0:T(8,128)(2,1)} %value_ref.11), custom_call_target="tpu_custom_call" | custom-call | tf_op jit(solution)/shard_map/pallas_call | solution.py:165
  31.1 0.0 copy-start
  31.1 0.0 collective-permute-done.3
  31.1 0.1 broadcast_select_fusion.4
  31.3 1.6 %collective-permute-start.5 = (bf16[512,128]{1,0:T(8,128)(2,1)S(1)}, bf16[512,128]{1,0:T(8,128)(2,1)S(1)}, u32[]{:S(2)}, u32[]{:S(2)}) collective-permute-start(bf16[512,128]{1,0:T(8,128)(2,1)S(1)} %get-tuple-element.58), channel_id=1, source_target_pairs={{0,2},{1,3},{2,0},{3,1},{4,6},{5,7},{6,4},{7,5},{8,10},{9,11},{10,... | collective-permute-start | bytes 393224 | tf_op jit(solution)/shard_map/ppermute | solution.py:175
  32.8 0.1 broadcast_select_fusion.5
  32.9 3.4 %collective-permute-done.5 = bf16[512,128]{1,0:T(8,128)(2,1)S(1)} collective-permute-done((bf16[512,128]{1,0:T(8,128)(2,1)S(1)}, bf16[512,128]{1,0:T(8,128)(2,1)S(1)}, u32[]{:S(2)}, u32[]{:S(2)}) %collective-permute-start.5) | collective-permute-done | bytes 131104 | tf_op jit(solution)/shard_map/ppermute | solution.py:175
  36.3 0.2 fusion
  36.5 0.1 collective-permute-start.6
  36.6 4.0 %shard_map.87 = (bf16[384,2048]{1,0:T(8,128)(2,1)S(1)}, bf16[1024,128]{1,0:T(8,128)(2,1)S(1)}, f32[1,1024]{1,0:T(1,128)S(1)}) custom-call(s32[1]{0:T(128)} %bitcast._, bf16[384,2048]{1,0:T(8,128)(2,1)} %query_ref.6, bf16[384,2048]{1,0:T(8,128)(2,1)} %cotan_ref.3, f32[1,2048]{1,0:T(1,128)S(1)} %bitcast.5, bf16[1024,128]{1,0:T(8,128)(2,1)S(1)} %get-tuple-element.62.state_ref, ...), custom_call_target="tpu_custom_call" | custom-call | tf_op jit(solution)/shard_map/pallas_call | solution.py:165
  40.6 0.5 collective-permute-start.7
  41.2 4.0 %shard_map.88 = (bf16[384,2048]{1,0:T(8,128)(2,1)S(1)}, bf16[1024,128]{1,0:T(8,128)(2,1)S(1)}, f32[1,1024]{1,0:T(1,128)S(1)}) custom-call(s32[1]{0:T(128)S(6)} %sub.18._, bf16[384,2048]{1,0:T(8,128)(2,1)} %query_ref.6, bf16[384,2048]{1,0:T(8,128)(2,1)} %cotan_ref.3, f32[1,2048]{1,0:T(1,128)S(1)} %bitcast.6, ...), custom_call_target="tpu_custom_call", output_to_operand_aliasing={{0}: (6, {})} | custom-call | tf_op jit(solution)/shard_map/pallas_call | solution.py:165
  45.2 0.0 collective-permute-done.7
  45.2 1.6 %collective-permute-start.8 = (bf16[512,128]{1,0:T(8,128)(2,1)S(1)}, bf16[512,128]{1,0:T(8,128)(2,1)S(1)}, u32[]{:S(2)}, u32[]{:S(2)}) collective-permute-start(bf16[512,128]{1,0:T(8,128)(2,1)S(1)} %add_convert_fusion.4), channel_id=1, source_target_pairs={{0,2},{1,3},{2,0},{3,1},{4,6},{5,7},{6,4},{7,5},{8,10},{9,11},{10,... | collective-permute-start | bytes 393224 | tf_op jit(solution)/shard_map/ppermute | solution.py:175
  46.8 0.1 collective-permute-start.9
  46.9 1.1 %collective-permute-done.9 = f32[16,128]{1,0:T(8,128)S(1)} collective-permute-done((f32[16,128]{1,0:T(8,128)S(1)}, f32[16,128]{1,0:T(8,128)S(1)}, u32[]{:S(2)}, u32[]{:S(2)}) %collective-permute-start.9) | collective-permute-done | bytes 8224 | tf_op jit(solution)/shard_map/ppermute | solution.py:175
  48.1 2.7 %collective-permute-done.8 = bf16[512,128]{1,0:T(8,128)(2,1)S(1)} collective-permute-done((bf16[512,128]{1,0:T(8,128)(2,1)S(1)}, bf16[512,128]{1,0:T(8,128)(2,1)S(1)}, u32[]{:S(2)}, u32[]{:S(2)}) %collective-permute-start.8) | collective-permute-done | bytes 131104 | tf_op jit(solution)/shard_map/ppermute | solution.py:175
  50.8 0.1 add_convert_fusion.3
  50.8 1.3 %collective-permute-start.12 = (bf16[512,128]{1,0:T(8,128)(2,1)S(1)}, bf16[512,128]{1,0:T(8,128)(2,1)S(1)}, u32[]{:S(2)}, u32[]{:S(2)}) collective-permute-start(bf16[512,128]{1,0:T(8,128)(2,1)S(1)} %add_convert_fusion.3), channel_id=1, source_target_pairs={{4,0},{5,1},{6,2},{7,3},{8,4},{9,5},{10,6},{11,7},{12,8},{13,9},{1... | collective-permute-start | bytes 393224 | tf_op jit(solution)/shard_map/ppermute | solution.py:175
  52.1 1.3 %collective-permute-start.11 = (bf16[512,128]{1,0:T(8,128)(2,1)S(1)}, bf16[512,128]{1,0:T(8,128)(2,1)S(1)}, u32[]{:S(2)}, u32[]{:S(2)}) collective-permute-start(bf16[512,128]{1,0:T(8,128)(2,1)S(1)} %add_convert_fusion.3), channel_id=1, source_target_pairs={{8,0},{9,1},{10,2},{11,3},{12,4},{13,5},{14,6},{15,7},{24,16},{25,... | collective-permute-start | bytes 393224 | tf_op jit(solution)/shard_map/ppermute | solution.py:175
  53.4 1.3 %collective-permute-start.10 = (bf16[512,128]{1,0:T(8,128)(2,1)S(1)}, bf16[512,128]{1,0:T(8,128)(2,1)S(1)}, u32[]{:S(2)}, u32[]{:S(2)}) collective-permute-start(bf16[512,128]{1,0:T(8,128)(2,1)S(1)} %add_convert_fusion.3), channel_id=1, source_target_pairs={{12,0},{13,1},{14,2},{15,3},{28,16},{29,17},{30,18},{31,19}} | collective-permute-start | bytes 393224 | tf_op jit(solution)/shard_map/ppermute | solution.py:175
  54.7 1.6 %collective-permute-start.13 = (f32[16,128]{1,0:T(8,128)S(1)}, f32[16,128]{1,0:T(8,128)S(1)}, u32[]{:S(2)}, u32[]{:S(2)}) collective-permute-start(f32[16,128]{1,0:T(8,128)S(1)} %add.91), channel_id=1, source_target_pairs={{0,2},{1,3},{2,0},{3,1},{4,6},{5,7},{6,4},{7,5},{8,10},{9,11},{10,... | collective-permute-start | bytes 24584 | tf_op jit(solution)/shard_map/ppermute | solution.py:175
  56.3 0.1 maximum_select_fusion.state_ref
  56.4 13.4 %shard_map.89 = (bf16[384,2048]{1,0:T(8,128)(2,1)}, f32[384,2048]{1,0:T(8,128)S(1)}, f32[384,2048]{1,0:T(8,128)S(1)}) custom-call(bf16[384,2048]{1,0:T(8,128)(2,1)} %query_ref.6, bf16[384,2048]{1,0:T(8,128)(2,1)} %key_ref.11, bf16[384,2048]{1,0:T(8,128)(2,1)} %value_ref.11, bf16[384,2048]{1,0:T(8,128)(2,1)S(1)} %get-tuple-element.38.grad_ref, ...), custom_call_target="tpu_custom_call" | custom-call | tf_op jit(solution)/shard_map/pallas_call | solution.py:165
  69.8 0.0 collective-permute-done.13
  69.8 0.0 collective-permute-done.11
  69.8 0.1 broadcast_select_fusion.2
  70.0 0.6 collective-permute-start.14
  70.6 0.1 broadcast_select_fusion.3
  70.6 4.4 %collective-permute-done.14 = bf16[512,128]{1,0:T(8,128)(2,1)S(1)} collective-permute-done((bf16[512,128]{1,0:T(8,128)(2,1)S(1)}, bf16[512,128]{1,0:T(8,128)(2,1)S(1)}, u32[]{:S(2)}, u32[]{:S(2)}) %collective-permute-start.14) | collective-permute-done | bytes 131104 | tf_op jit(solution)/shard_map/ppermute | solution.py:175
  75.0 0.2 fusion.2
  75.2 0.1 collective-permute-start.15
  75.3 2.1 %collective-permute-start.16 = (f32[16,128]{1,0:T(8,128)S(1)}, f32[16,128]{1,0:T(8,128)S(1)}, u32[]{:S(2)}, u32[]{:S(2)}) collective-permute-start(f32[16,128]{1,0:T(8,128)S(1)} %add.92), channel_id=1, source_target_pairs={{0,4},{1,5},{2,6},{3,7},{4,0},{5,1},{6,2},{7,3},{8,12},{9,13},{10,... | collective-permute-start | bytes 24584 | tf_op jit(solution)/shard_map/ppermute | solution.py:175
  77.4 1.6 %collective-permute-done.16 = f32[16,128]{1,0:T(8,128)S(1)} collective-permute-done((f32[16,128]{1,0:T(8,128)S(1)}, f32[16,128]{1,0:T(8,128)S(1)}, u32[]{:S(2)}, u32[]{:S(2)}) %collective-permute-start.16) | collective-permute-done | bytes 8224 | tf_op jit(solution)/shard_map/ppermute | solution.py:175
  79.0 4.2 %collective-permute-start.17 = (f32[16,128]{1,0:T(8,128)S(1)}, f32[16,128]{1,0:T(8,128)S(1)}, u32[]{:S(2)}, u32[]{:S(2)}) collective-permute-start(f32[16,128]{1,0:T(8,128)S(1)} %add.97), channel_id=1, source_target_pairs={{0,8},{1,9},{2,10},{3,11},{4,12},{5,13},{6,14},{7,15},{8,0},{9,1},... | collective-permute-start | bytes 24584 | tf_op jit(solution)/shard_map/ppermute | solution.py:175
  83.2 4.1 %shard_map.90 = (bf16[384,2048]{1,0:T(8,128)(2,1)}, bf16[384,2048]{1,0:T(8,128)(2,1)}) custom-call(s32[1]{0:T(128)S(6)} %sub.18._, bf16[384,2048]{1,0:T(8,128)(2,1)} %key_ref.11, bf16[384,2048]{1,0:T(8,128)(2,1)} %value_ref.11, bf16[1024,128]{1,0:T(8,128)(2,1)S(1)} %get-tuple-element.50.back_ref, f32[384,2048]{1,0:T(8,128)S(1)} %get-tuple-element.40.dk_ref, ...), custom_call_target="tpu_custom_call" | custom-call | tf_op jit(solution)/shard_map/pallas_call | solution.py:165
  87.3 0.6 add_bitcast_fusion
  87.9 4.1 %shard_map.91 = (bf16[384,2048]{1,0:T(8,128)(2,1)}, bf16[384,2048]{1,0:T(8,128)(2,1)}) custom-call(s32[1]{0:T(128)} %bitcast._, bf16[384,2048]{1,0:T(8,128)(2,1)} %key_ref.11, bf16[384,2048]{1,0:T(8,128)(2,1)} %value_ref.11, bf16[1024,128]{1,0:T(8,128)(2,1)S(1)} %collective-permute-done.15.back_ref, ...), custom_call_target="tpu_custom_call", output_to_operand_aliasing={{0}: (6, {}), {1}: (7, {})} | custom-call | tf_op jit(solution)/shard_map/pallas_call | solution.py:165
  (14 shorter events, 0.1 us)
Async XLA Ops:
  3.6 3.5 %collective-permute-start = (bf16[1024,128]{1,0:T(8,128)(2,1)S(1)}, bf16[1024,128]{1,0:T(8,128)(2,1)S(1)}, u32[]{:S(2)}, u32[]{:S(2)}) collective-permute-start(bf16[1024,128]{1,0:T(8,128)(2,1)S(1)} %shard_map.85), channel_id=1, source_target_pairs={{0,1},{1,0},{2,3},{3,2},{4,5},{5,4},{6,7},{7,6},{8,9},{9,8},{10,11... | collective-permute-start | bytes 786440 | tf_op jit(solution)/shard_map/ppermute | solution.py:175
  7.2 6.7 %collective-permute-start.1 = (bf16[512,128]{1,0:T(8,128)(2,1)S(1)}, bf16[512,128]{1,0:T(8,128)(2,1)S(1)}, u32[]{:S(2)}, u32[]{:S(2)}) collective-permute-start(bf16[512,128]{1,0:T(8,128)(2,1)S(1)} %add_convert_fusion.8), channel_id=1, source_target_pairs={{0,2},{1,3},{2,0},{3,1},{4,6},{5,7},{6,4},{7,5},{8,10},{9,11},{10,... | collective-permute-start | bytes 393224 | tf_op jit(solution)/shard_map/ppermute | solution.py:175
  14.0 17.1 %collective-permute-start.4 = (bf16[512,128]{1,0:T(8,128)(2,1)S(1)}, bf16[512,128]{1,0:T(8,128)(2,1)S(1)}, u32[]{:S(2)}, u32[]{:S(2)}) collective-permute-start(bf16[512,128]{1,0:T(8,128)(2,1)S(1)} %add_convert_fusion.7), channel_id=1, source_target_pairs={{0,4},{1,5},{2,6},{3,7},{4,8},{5,9},{6,10},{7,11},{8,12},{9,13},{1... | collective-permute-start | bytes 393224 | tf_op jit(solution)/shard_map/ppermute | solution.py:175
  17.8 13.4 %collective-permute-start.3 = (bf16[512,128]{1,0:T(8,128)(2,1)S(1)}, bf16[512,128]{1,0:T(8,128)(2,1)S(1)}, u32[]{:S(2)}, u32[]{:S(2)}) collective-permute-start(bf16[512,128]{1,0:T(8,128)(2,1)S(1)} %add_convert_fusion.7), channel_id=1, source_target_pairs={{0,8},{1,9},{2,10},{3,11},{4,12},{5,13},{6,14},{7,15},{16,24},{17,... | collective-permute-start | bytes 393224 | tf_op jit(solution)/shard_map/ppermute | solution.py:175
  22.3 8.9 %collective-permute-start.2 = (bf16[512,128]{1,0:T(8,128)(2,1)S(1)}, bf16[512,128]{1,0:T(8,128)(2,1)S(1)}, u32[]{:S(2)}, u32[]{:S(2)}) collective-permute-start(bf16[512,128]{1,0:T(8,128)(2,1)S(1)} %add_convert_fusion.7), channel_id=1, source_target_pairs={{0,12},{1,13},{2,14},{3,15},{16,28},{17,29},{18,30},{19,31}} | collective-permute-start | bytes 393224 | tf_op jit(solution)/shard_map/ppermute | solution.py:175
  31.1 5.5 %copy-start = (f32[2048]{0:T(1024)S(1)}, f32[2048]{0:T(1024)}, u32[]{:S(2)}) copy-start(f32[2048]{0:T(1024)} %param.9) | copy-start | bytes 24580
  31.3 5.0 %collective-permute-start.5 = (bf16[512,128]{1,0:T(8,128)(2,1)S(1)}, bf16[512,128]{1,0:T(8,128)(2,1)S(1)}, u32[]{:S(2)}, u32[]{:S(2)}) collective-permute-start(bf16[512,128]{1,0:T(8,128)(2,1)S(1)} %get-tuple-element.58), channel_id=1, source_target_pairs={{0,2},{1,3},{2,0},{3,1},{4,6},{5,7},{6,4},{7,5},{8,10},{9,11},{10,... | collective-permute-start | bytes 393224 | tf_op jit(solution)/shard_map/ppermute | solution.py:175
  36.5 4.7 %collective-permute-start.6 = (bf16[1024,128]{1,0:T(8,128)(2,1)S(1)}, bf16[1024,128]{1,0:T(8,128)(2,1)S(1)}, u32[]{:S(2)}, u32[]{:S(2)}) collective-permute-start(bf16[1024,128]{1,0:T(8,128)(2,1)S(1)} %get-tuple-element.63), channel_id=1, source_target_pairs={{0,1},{1,0},{2,3},{3,2},{4,5},{5,4},{6,7},{7,6},{8,9},{9,8},{10,11... | collective-permute-start | bytes 786440 | tf_op jit(solution)/shard_map/ppermute | solution.py:175
  40.6 4.5 %collective-permute-start.7 = (bf16[1024,128]{1,0:T(8,128)(2,1)S(1)}, bf16[1024,128]{1,0:T(8,128)(2,1)S(1)}, u32[]{:S(2)}, u32[]{:S(2)}) collective-permute-start(bf16[1024,128]{1,0:T(8,128)(2,1)S(1)} %get-tuple-element.34), channel_id=1, source_target_pairs={{0,1},{1,0},{2,3},{3,2},{4,5},{5,4},{6,7},{7,6},{8,9},{9,8},{10,11... | collective-permute-start | bytes 786440 | tf_op jit(solution)/shard_map/ppermute | solution.py:175
  45.2 5.5 %collective-permute-start.8 = (bf16[512,128]{1,0:T(8,128)(2,1)S(1)}, bf16[512,128]{1,0:T(8,128)(2,1)S(1)}, u32[]{:S(2)}, u32[]{:S(2)}) collective-permute-start(bf16[512,128]{1,0:T(8,128)(2,1)S(1)} %add_convert_fusion.4), channel_id=1, source_target_pairs={{0,2},{1,3},{2,0},{3,1},{4,6},{5,7},{6,4},{7,5},{8,10},{9,11},{10,... | collective-permute-start | bytes 393224 | tf_op jit(solution)/shard_map/ppermute | solution.py:175
  46.8 1.2 %collective-permute-start.9 = (f32[16,128]{1,0:T(8,128)S(1)}, f32[16,128]{1,0:T(8,128)S(1)}, u32[]{:S(2)}, u32[]{:S(2)}) collective-permute-start(f32[16,128]{1,0:T(8,128)S(1)} %bitcast.7), channel_id=1, source_target_pairs={{0,1},{1,0},{2,3},{3,2},{4,5},{5,4},{6,7},{7,6},{8,9},{9,8},{10,11... | collective-permute-start | bytes 24584 | tf_op jit(solution)/shard_map/ppermute | solution.py:175
  50.8 19.0 %collective-permute-start.12 = (bf16[512,128]{1,0:T(8,128)(2,1)S(1)}, bf16[512,128]{1,0:T(8,128)(2,1)S(1)}, u32[]{:S(2)}, u32[]{:S(2)}) collective-permute-start(bf16[512,128]{1,0:T(8,128)(2,1)S(1)} %add_convert_fusion.3), channel_id=1, source_target_pairs={{4,0},{5,1},{6,2},{7,3},{8,4},{9,5},{10,6},{11,7},{12,8},{13,9},{1... | collective-permute-start | bytes 393224 | tf_op jit(solution)/shard_map/ppermute | solution.py:175
  52.1 17.7 %collective-permute-start.11 = (bf16[512,128]{1,0:T(8,128)(2,1)S(1)}, bf16[512,128]{1,0:T(8,128)(2,1)S(1)}, u32[]{:S(2)}, u32[]{:S(2)}) collective-permute-start(bf16[512,128]{1,0:T(8,128)(2,1)S(1)} %add_convert_fusion.3), channel_id=1, source_target_pairs={{8,0},{9,1},{10,2},{11,3},{12,4},{13,5},{14,6},{15,7},{24,16},{25,... | collective-permute-start | bytes 393224 | tf_op jit(solution)/shard_map/ppermute | solution.py:175
  53.4 16.4 %collective-permute-start.10 = (bf16[512,128]{1,0:T(8,128)(2,1)S(1)}, bf16[512,128]{1,0:T(8,128)(2,1)S(1)}, u32[]{:S(2)}, u32[]{:S(2)}) collective-permute-start(bf16[512,128]{1,0:T(8,128)(2,1)S(1)} %add_convert_fusion.3), channel_id=1, source_target_pairs={{12,0},{13,1},{14,2},{15,3},{28,16},{29,17},{30,18},{31,19}} | collective-permute-start | bytes 393224 | tf_op jit(solution)/shard_map/ppermute | solution.py:175
  54.7 15.1 %collective-permute-start.13 = (f32[16,128]{1,0:T(8,128)S(1)}, f32[16,128]{1,0:T(8,128)S(1)}, u32[]{:S(2)}, u32[]{:S(2)}) collective-permute-start(f32[16,128]{1,0:T(8,128)S(1)} %add.91), channel_id=1, source_target_pairs={{0,2},{1,3},{2,0},{3,1},{4,6},{5,7},{6,4},{7,5},{8,10},{9,11},{10,... | collective-permute-start | bytes 24584 | tf_op jit(solution)/shard_map/ppermute | solution.py:175
  70.0 5.0 %collective-permute-start.14 = (bf16[512,128]{1,0:T(8,128)(2,1)S(1)}, bf16[512,128]{1,0:T(8,128)(2,1)S(1)}, u32[]{:S(2)}, u32[]{:S(2)}) collective-permute-start(bf16[512,128]{1,0:T(8,128)(2,1)S(1)} %get-tuple-element.56), channel_id=1, source_target_pairs={{0,2},{1,3},{2,0},{3,1},{4,6},{5,7},{6,4},{7,5},{8,10},{9,11},{10,... | collective-permute-start | bytes 393224 | tf_op jit(solution)/shard_map/ppermute | solution.py:175
  75.2 12.7 %collective-permute-start.15 = (bf16[1024,128]{1,0:T(8,128)(2,1)S(1)}, bf16[1024,128]{1,0:T(8,128)(2,1)S(1)}, u32[]{:S(2)}, u32[]{:S(2)}) collective-permute-start(bf16[1024,128]{1,0:T(8,128)(2,1)S(1)} %get-tuple-element.61), channel_id=1, source_target_pairs={{0,1},{1,0},{2,3},{3,2},{4,5},{5,4},{6,7},{7,6},{8,9},{9,8},{10,11... | collective-permute-start | bytes 786440 | tf_op jit(solution)/shard_map/ppermute | solution.py:175
  75.3 3.7 %collective-permute-start.16 = (f32[16,128]{1,0:T(8,128)S(1)}, f32[16,128]{1,0:T(8,128)S(1)}, u32[]{:S(2)}, u32[]{:S(2)}) collective-permute-start(f32[16,128]{1,0:T(8,128)S(1)} %add.92), channel_id=1, source_target_pairs={{0,4},{1,5},{2,6},{3,7},{4,0},{5,1},{6,2},{7,3},{8,12},{9,13},{10,... | collective-permute-start | bytes 24584 | tf_op jit(solution)/shard_map/ppermute | solution.py:175
  79.0 8.3 %collective-permute-start.17 = (f32[16,128]{1,0:T(8,128)S(1)}, f32[16,128]{1,0:T(8,128)S(1)}, u32[]{:S(2)}, u32[]{:S(2)}) collective-permute-start(f32[16,128]{1,0:T(8,128)S(1)} %add.97), channel_id=1, source_target_pairs={{0,8},{1,9},{2,10},{3,11},{4,12},{5,13},{6,14},{7,15},{8,0},{9,1},... | collective-permute-start | bytes 24584 | tf_op jit(solution)/shard_map/ppermute | solution.py:175

commit v3 on v0

v3 whole, which is shorter than its diff:
```python
import functools

import jax
import jax.numpy as jnp
from jax import lax
from jax.experimental import pallas as pl
from jax.experimental.pallas import tpu as pltpu
from jax.sharding import PartitionSpec as P

HEADS = 16
HEAD = 128
TILE = 128
QUARTER = HEADS // 4
SPAN = QUARTER * HEAD
EXTRA = 16
norm_eps = 1e-05
f32 = jnp.float32
bf16 = jnp.bfloat16

VMEM = pl.BlockSpec(memory_space=pltpu.VMEM)
SMEM = pl.BlockSpec(memory_space=pltpu.SMEM)
HBM = pl.BlockSpec(memory_space=pltpu.HBM)


def decay(x):
    return jnp.exp(jnp.minimum(x, 0.0))


def feature(x):
    return jnp.where(x > 0, x + 1.0, decay(x)).astype(bf16)


def mm(a, b):
    return lax.dot_general(a, b, (((1,), (0,)), ((), ())), preferred_element_type=f32)


def mm_nt(a, b):
    return lax.dot_general(a, b, (((1,), (1,)), ((), ())), preferred_element_type=f32)


def mm_tn(a, b):
    return lax.dot_general(a, b, (((0,), (0,)), ((), ())), preferred_element_type=f32)


def own(head):
    return slice(head * HEAD, (head + 1) * HEAD)


def span(where):
    return pl.ds(pl.multiple_of((2 * where[0] + where[1]) * SPAN, SPAN), SPAN)


def place(where, head):
    start = (2 * where[0] + where[1]) * SPAN + head * HEAD
    return pl.ds(pl.multiple_of(start, HEAD), HEAD)


def lower(rows, depth, length):
    keep = lax.broadcasted_iota(jnp.int32, (TILE, TILE), 0) >= lax.broadcasted_iota(
        jnp.int32, (TILE, TILE), 1
    )
    strips = []
    for start in range(0, length, TILE):
        strip = mm_nt(rows[start : start + TILE], depth[: start + TILE])
        last = jnp.where(keep, strip[:, start:], 0.0).astype(bf16)
        if start:
            last = jnp.concatenate([strip[:, :start].astype(bf16), last], axis=1)
        strips.append(last)
    return strips


def upper(rows, depth, length):
    keep = lax.broadcasted_iota(jnp.int32, (TILE, TILE), 0) <= lax.broadcasted_iota(
        jnp.int32, (TILE, TILE), 1
    )
    strips = []
    for start in range(0, length, TILE):
        strip = mm_nt(rows[start : start + TILE], depth[start:])
        first = jnp.where(keep, strip[:, :TILE], 0.0).astype(bf16)
        if start + TILE < length:
            first = jnp.concatenate([first, strip[:, TILE:].astype(bf16)], axis=1)
        strips.append(first)
    return strips


def finish(copies):
    for copy in copies:
        copy.wait()


def state(ins, outs):
    (key_ref, value_ref), (own_ref,) = ins, outs
    for head in range(QUARTER):
        key_map = feature(key_ref[:, own(head)].astype(f32))
        own_ref[own(head), :] = mm_tn(key_map, value_ref[:, own(head)]).astype(own_ref.dtype)


def inner(ins, outs):
    (query_ref, key_ref, value_ref), (mixed_ref,) = ins, outs
    length = query_ref.shape[0]
    for head in range(QUARTER):
        query_map = feature(query_ref[:, own(head)].astype(f32))
        key_map = feature(key_ref[:, own(head)].astype(f32))
        value = value_ref[:, own(head)]
        for i, strip in enumerate(lower(query_map, key_map, length)):
            start = i * TILE
            mixed_ref[start : start + TILE, own(head)] = mm(strip, value[: start + TILE])


def loading_kernel(body, first, *refs):
    body_ins, body_outs, loads = body[1:]
    where, refs = refs[:loads], refs[loads:]
    ins, refs = refs[:body_ins], refs[body_ins:]
    sources, refs = refs[:loads], refs[loads:]
    outs, refs = refs[:body_outs], refs[body_outs:]
    targets, sems = refs[:loads], refs[-1]
    copies = [
        pltpu.make_async_copy(source.at[:, span(at)], target, sems.at[i])
        for i, (at, source, target) in enumerate(zip(where, sources, targets, strict=True))
    ]
    for copy in copies:
        copy.start()
    finish(copies[:first])
    body[0]((*targets[:first], *ins), outs)
    finish(copies[first:])


def plain_kernel(body, count, *refs):
    body(refs[:count], refs[count:])


def norm_kernel(where, query_ref, cotan_ref, gain_ref, state_ref, mixed_ref, grad_ref, own_ref):
    own_ref[SPAN:, :] = jnp.zeros_like(own_ref[SPAN:, :])
    for head in range(QUARTER):
        query_map = feature(query_ref[:, own(head)].astype(f32))
        mixed = mixed_ref[:, own(head)] + mm(query_map, state_ref[own(head), :])
        inverse = lax.rsqrt(jnp.mean(mixed * mixed, axis=1, keepdims=True) + norm_eps)
        normed = mixed * inverse
        cotan = cotan_ref[:, own(head)].astype(f32)
        part = jnp.sum(cotan * normed, axis=0, keepdims=True)
        own_ref[SPAN + head : SPAN + head + 1, :] = part.astype(own_ref.dtype)
        scaled = cotan * gain_ref[:, place(where, head)]
        along = jnp.mean(scaled * normed, axis=1, keepdims=True)
        grad = ((scaled - normed * along) * inverse).astype(bf16)
        grad_ref[:, own(head)] = grad
        own_ref[own(head), :] = mm_tn(query_map, grad).astype(own_ref.dtype)


def back_kernel(where, query_ref, key_ref, value_ref, grad_ref, state_ref, *refs):
    dk_ref, dv_ref, dq_hbm, dq_ref, sems = refs[-5:]
    length = query_ref.shape[0]
    copies = []
    for head in range(QUARTER):
        query = query_ref[:, own(head)].astype(f32)
        query_map = feature(query)
        key_map = feature(key_ref[:, own(head)].astype(f32))
        value = value_ref[:, own(head)]
        grad = grad_ref[:, own(head)]
        far = mm_nt(grad, state_ref[own(head), :])
        slope = decay(query)
        for i, strip in enumerate(lower(grad, value, length)):
            rows = slice(i * TILE, (i + 1) * TILE)
            near = mm(strip, key_map[: (i + 1) * TILE])
            dq_ref[rows, own(head)] = ((near + far[rows]) * slope[rows]).astype(bf16)
        copies.append(
            pltpu.make_async_copy(
                dq_ref.at[:, own(head)], dq_hbm.at[:, place(where, head)], sems.at[head]
            )
        )
        copies[-1].start()
        for i, strip in enumerate(upper(value, grad, length)):
            rows = slice(i * TILE, (i + 1) * TILE)
            dk_ref[rows, own(head)] = mm(strip, query_map[i * TILE :])
        for i, strip in enumerate(upper(key_map, query_map, length)):
            rows = slice(i * TILE, (i + 1) * TILE)
            dv_ref[rows, own(head)] = mm(strip, grad[i * TILE :])
    finish(copies)


def last_kernel(where, key_ref, value_ref, back_ref, dk_ref, dv_ref, so_far_ref, *refs):
    key_hbm, value_hbm, gain_ref, key_grad_ref, value_grad_ref, sems = refs[-6:]
    copies = []
    gain_ref[...] = so_far_ref[...]
    gains = back_ref[SPAN:, :].astype(f32)
    for head in range(QUARTER):
        gain_ref[:, place(where, head)] = gains[head : head + 1, :]
        key = key_ref[:, own(head)].astype(f32)
        back = back_ref[own(head), :]
        far = mm_nt(value_ref[:, own(head)], back)
        key_grad_ref[:, own(head)] = ((dk_ref[:, own(head)] + far) * decay(key)).astype(bf16)
        value_grad = dv_ref[:, own(head)] + mm(feature(key), back)
        value_grad_ref[:, own(head)] = value_grad.astype(bf16)
        for i, (held, whole) in enumerate(((key_grad_ref, key_hbm), (value_grad_ref, value_hbm))):
            copies.append(
                pltpu.make_async_copy(
                    held.at[:, own(head)], whole.at[:, place(where, head)], sems.at[i, head]
                )
            )
            copies[-1].start()
    finish(copies)


def call(kernel, ins, outs, scratch=(), kept=()):
    return pl.pallas_call(
        kernel,
        out_shape=[jax.ShapeDtypeStruct(shape, dtype) for shape, dtype, _ in outs],
        in_specs=[spec for _, spec in ins] + [spec for _, spec, _ in kept],
        out_specs=[spec for _, _, spec in outs],
        scratch_shapes=list(scratch),
        input_output_aliases={len(ins) + i: out for i, (_, _, out) in enumerate(kept)},
        compiler_params=pltpu.CompilerParams(vmem_limit_bytes=12 << 20),
        cost_estimate=pl.CostEstimate(flops=1024, bytes_accessed=1024, transcendentals=0),
    )(*[a for a, _ in ins], *[a for a, _, _ in kept])


def permute(value, pairs):
    return lax.ppermute(value, "seq", pairs)


def add(*terms):
    return functools.reduce(lambda a, b: a + b, [t.astype(f32) for t in terms])


def when(flag, wanted, value):
    value = value.astype(f32)
    return jnp.where(flag, value, 0.0) if wanted else jnp.where(flag, 0.0, value)


def after(value, *done):
    leaves, tree = jax.tree.flatten(value)
    held = lax.optimization_barrier((*leaves, *done))
    return jax.tree.unflatten(tree, held[: len(leaves)])


class Scan:
    def __init__(self, shards, reverse, odd_core, odd_chip, ends):
        self.shards = shards
        self.sign = -1 if reverse else 1
        self.second = not reverse
        self.odd_core, self.odd_chip, self.ends = odd_core, odd_chip, ends

    def swap_core(self, value):
        return permute(value, [(i, i ^ 1) for i in range(self.shards)])

    def swap_chip(self, value):
        return permute(value, [(i, i ^ 2) for i in range(self.shards)])

    def shift(self, value, fours):
        step = 4 * fours * self.sign
        if value.shape[0] > SPAN:
            moved = permute(value, [(i, (i + step) % self.shards) for i in range(self.shards)])
            rows = lax.broadcasted_iota(jnp.int32, value.shape, 0)
            return jnp.where(self.ends[fours] | (rows >= SPAN), moved, 0)
        pairs = [(i, i + step) for i in range(self.shards) if 0 <= i + step < self.shards]
        return permute(value, pairs)

    def early(self, mine, got):
        self.early_mine, self.early_got = mine, got
        send = add(mine, got).astype(bf16)
        self.other = self.swap_chip(send)
        return send

    def late(self, mine, got):
        self.late_mine, self.late_got = mine, got
        self.near = add(mine, got)

    def before(self):
        total = add(self.near, self.other).astype(bf16)
        self.total = total
        count = self.shards // 4
        if count <= 4:
            return total, [self.shift(total, k) for k in range(1, count)]
        running, step = self.shift(total, 1), 1
        while step < count:
            running = add(running, self.shift(running, step)).astype(bf16)
            step *= 2
        return total, [running]

    def alone(self, value, wanted):
        rows = lax.broadcasted_iota(jnp.int32, value.shape, 0)
        return jnp.where((rows >= SPAN) if wanted else (rows < SPAN), value, 0)

    def state(self, base, mine, got):
        if base.shape[0] > SPAN:
            mine, got = self.alone(mine, False), self.alone(got, False)
        here = add(base, when(self.odd_core, self.second, got)).astype(bf16)
        there = add(base, when(self.odd_core, not self.second, mine)).astype(bf16)
        return here, self.swap_core(there)

    def late_state(self, earlier):
        base = add(*earlier)
        near, other = self.near, self.other
        if base.shape[0] > SPAN:
            if self.shards // 4 <= 4:
                base = base + self.alone(self.total, True).astype(f32)
            near, other = self.alone(near, False), self.alone(other, False)
        send = add(base, when(self.odd_chip, not self.second, near)).astype(bf16)
        self.back = self.swap_chip(send)
        base = add(base, when(self.odd_chip, self.second, other))
        return self.state(base, self.late_mine, self.late_got)

    def early_state(self):
        return self.state(self.back, self.early_mine, self.early_got)


def on_device(queries, key_vectors, value_vectors, out_cotangent, norm_gain):
    queries, key_vectors, value_vectors, out_cotangent = (
        pltpu.with_memory_space_constraint(a, pltpu.HBM)
        for a in (queries, key_vectors, value_vectors, out_cotangent)
    )
    length, width = queries.shape
    shards = lax.axis_size("seq")
    index = lax.axis_index("seq").astype(jnp.int32)
    core, chip, four = index % 2, index // 2 % 2, index // 4
    gain = norm_gain.reshape(1, width)
    where = {
        (a, b): jnp.stack([1 - core if a else core, 1 - chip if b else chip])
        for a in (0, 1)
        for b in (0, 1)
    }
    count = shards // 4
    ends = {k: four + k < count for k in range(1, count)}
    where, odd_core, odd_chip, ends = after((where, core == 1, chip == 1, ends))
    state_low = ((SPAN, HEAD), bf16, VMEM)
    state_wide = ((SPAN, HEAD), f32, VMEM)
    sums_low = ((SPAN + EXTRA, HEAD), bf16, VMEM)
    sums_wide = ((SPAN + EXTRA, HEAD), f32, VMEM)
    wide = ((length, SPAN), f32, VMEM)
    low = ((length, SPAN), bf16, VMEM)
    whole = ((length, width), bf16, HBM)
    row = ((1, width), f32, VMEM)
    held = lambda *arrays: [(a, VMEM) for a in arrays]
    sems = lambda *shape: pltpu.SemaphoreType.DMA(shape)
    wholes = {"q": queries, "k": key_vectors, "v": value_vectors, "c": out_cotangent}
    tile = {}

    def loading(body, ins, outs, fetch, first=0):
        kernel = functools.partial(
            loading_kernel, (body, len(ins), len(outs), len(fetch)), first
        )
        result = call(
            kernel,
            [(where[which], SMEM) for _, which in fetch]
            + held(*ins)
            + [(wholes[name], HBM) for name, _ in fetch],
            outs + [low] * len(fetch),
            [sems(len(fetch))],
        )
        for key, value in zip(fetch, result[len(outs) :], strict=True):
            tile[key] = value
        return result[: len(outs)]

    def tiles(names, which):
        return [tile[name, which] for name in names]

    fore = Scan(shards, False, odd_core, odd_chip, ends)
    (sent,) = loading(
        state, [], [state_low], [("k", (1, 1)), ("v", (1, 1)), ("k", (0, 1)), ("v", (0, 1))], 2
    )
    got = fore.swap_core(sent)
    (mine,) = loading(
        state, after(tiles("kv", (0, 1)), sent), [state_wide], [("k", (1, 0)), ("v", (1, 0))]
    )
    send = fore.early(mine, got)
    (sent,) = loading(
        state, after(tiles("kv", (1, 0)), send), [state_low], [("k", (0, 0)), ("v", (0, 0))]
    )
    got = fore.swap_core(sent)
    (mine,) = loading(
        state, after(tiles("kv", (0, 0)), sent), [state_wide], [("q", (0, 0)), ("q", (1, 0))]
    )
    fore.late(mine, got)

    mixed = {}
    (mixed[0, 0],) = loading(
        inner, tiles("qkv", (0, 0)), [wide], [("q", (0, 1)), ("q", (1, 1))]
    )
    fore.near = after(fore.near, mixed[0, 0])
    total, earlier = fore.before()
    (mixed[1, 0],) = loading(
        inner, after(tiles("qkv", (1, 0)), total), [wide], [("c", (0, 0)), ("c", (1, 0))]
    )
    (mixed[0, 1],) = loading(
        inner, after(tiles("qkv", (0, 1)), mixed[1, 0]), [wide], [("c", (0, 1)), ("c", (1, 1))]
    )
    (mixed[1, 1],) = call(
        functools.partial(plain_kernel, inner, 3),
        held(*after(tiles("qkv", (1, 1)), mixed[0, 1])),
        [wide],
    )
    earlier = after(earlier, mixed[1, 1])

    grads, seen = {}, {}
    aft = Scan(shards, True, odd_core, odd_chip, ends)

    def norm(which, state, kind, *done):
        query, cotan = tiles("qc", which)
        (cotan,) = after([cotan], *done) if done else [cotan]
        ins = [(where[which], SMEM)] + held(query, cotan, gain, state, mixed[which])
        return call(norm_kernel, ins, [low, kind])

    seen[0, 0], seen[1, 0] = fore.late_state(earlier)
    grads[0, 0], sent = norm((0, 0), seen[0, 0], sums_low)
    got = aft.swap_core(sent)
    grads[1, 0], mine = norm((1, 0), seen[1, 0], sums_wide)
    send = aft.early(mine, got)
    fore.back = after(fore.back, send)
    seen[0, 1], seen[1, 1] = fore.early_state()
    grads[0, 1], sent = norm((0, 1), seen[0, 1], sums_low, send)
    got = aft.swap_core(sent)
    grads[1, 1], mine = norm((1, 1), seen[1, 1], sums_wide)
    aft.late(mine, got)
    total, later = aft.before()

    inner_grads = {}
    query_grad = None

    def back(which, query_grad, *done):
        grad = after(grads[which], *done)
        return call(
            back_kernel,
            [(where[which], SMEM)] + held(*tiles("qkv", which), grad, seen[which]),
            [wide, wide, whole],
            [pltpu.VMEM((length, SPAN), bf16), sems(QUARTER)],
            [] if query_grad is None else [(query_grad, HBM, 2)],
        )

    done = total
    for which in ((1, 1), (0, 1), (1, 0)):
        *inner_grads[which], query_grad = back(which, query_grad, done)
        done = inner_grads[which][0]
    later = after(later, done)

    def last(which, back, outs):
        so_far = outs[2] if outs else gain
        ins = [(where[which], SMEM)]
        ins += held(*tiles("kv", which), back, *inner_grads[which], so_far)
        scratch = [pltpu.VMEM((length, SPAN), bf16)] * 2 + [sems(2, QUARTER)]
        kept = [(a, HBM, i) for i, a in enumerate(outs[:2])]
        return call(last_kernel, ins, [whole, whole, row], scratch, kept)

    here, there = aft.late_state(later)
    outs = last((1, 1), here, ())
    *inner_grads[0, 0], query_grad = back((0, 0), query_grad, outs[2])
    inner_grads[0, 1][0] = after(inner_grads[0, 1][0], inner_grads[0, 0][0])
    outs = last((0, 1), there, outs)
    aft.back = after(aft.back, outs[2])
    here, there = aft.early_state()
    outs = last((1, 0), here, outs)
    key_grad, value_grad, gain_grad = last((0, 0), there, outs)
    return query_grad, key_grad, value_grad, gain_grad.reshape(width)


def solution(mesh):
    tokens = P(("groups", "seq"), None)
    return jax.shard_map(
        on_device,
        mesh=mesh,
        in_specs=(tokens, tokens, tokens, tokens, P()),
        out_specs=(tokens, tokens, tokens, P("groups")),
        check_vma=False,
    )
```

time: 293 us -> 74.4 us (0.25)
  the two profiles are of different devices: /device:TPU:16 before, /device:TPU:0 now
where the time goes in v3:
time: 74.4 us; the launch traced here: 74.1 us
  Pallas kernels  44.4 us (60%)
  starting transfers between devices  25.2 us (34%)
  waiting for transfers between devices  1.65 us (2%)
  other arithmetic  1.54 us (2%)
  between operations  1.25 us (2%)
    pallas_call x20, Pallas kernels, call(): pl.pallas_call(kernel, out_shape=[jax.ShapeDtypeStruct(shape, dtype) for...  44.4 us
    ppermute x18, starting transfers between devices, permute(): return lax.ppermute(value, 'seq', pairs)  25.2 us
    ppermute x18, waiting for transfers between devices, permute(): return lax.ppermute(value, 'seq', pairs)  1.65 us
  transfers between devices with their start and end apart: 18, of which 1 were waited for; matrix products, arithmetic and copies ran while one was open for 1% of the time, Pallas kernels for 49%

profile of v3, /device:TPU:0, one launch (start us, length us, event | category | flops | bytes accessed | tf_op | source)
XLA Modules:
  0.0 74.1 jit_solution(4401745267170006910)
XLA Ops:
  0.7 0.1 pad_add_fusion.2
  0.8 0.1 pad_add_fusion
  0.8 2.1 %shard_map.84 = (bf16[512,128]{1,0:T(8,128)(2,1)S(1)}, bf16[384,512]{1,0:T(8,128)(2,1)S(1)}, bf16[384,512]{1,0:T(8,128)(2,1)S(1)}, bf16[384,512]{1,0:T(8,128)(2,1)S(1)}, bf16[384,512]{1,0:T(8,128)(2,1)S(1)}) custom-call(s32[2]{0:T(128)S(1)} %get-tuple-element.100.refs_0_.refs_1_.where, s32[2]{0:T(128)S(1)} %get-tuple-element.100.refs_0_.refs_1_.where, ...), custom_call_target="tpu_custom_call" | custom-call | flops 1024 | bytes 1024 | tf_op jit(solution)/shard_map/pallas_call | solution.py:204
  2.9 0.5 collective-permute-start
  3.5 1.9 %shard_map.85 = (f32[512,128]{1,0:T(8,128)S(1)}, bf16[384,512]{1,0:T(8,128)(2,1)S(1)}, bf16[384,512]{1,0:T(8,128)(2,1)S(1)}) custom-call(s32[2]{0:T(128)S(1)} %get-tuple-element.99.refs_0_.refs_1_.where, s32[2]{0:T(128)S(1)} %get-tuple-element.99.refs_0_.refs_1_.where, bf16[384,512]{1,0:T(8,128)(2,1)S(1)} %get-tuple-element.132.refs_2_.refs_3_.key_ref, ...), custom_call_target="tpu_custom_call" | custom-call | flops 1024 | bytes 1024 | tf_op jit(solution)/shard_map/pallas_call | solution.py:204
  5.4 1.9 %shard_map.86 = (bf16[512,128]{1,0:T(8,128)(2,1)S(1)}, bf16[384,512]{1,0:T(8,128)(2,1)S(1)}, bf16[384,512]{1,0:T(8,128)(2,1)S(1)}) custom-call(s32[2]{0:T(128)S(1)} %get-tuple-element.98.refs_0_.refs_1_.where, s32[2]{0:T(128)S(1)} %get-tuple-element.98.refs_0_.refs_1_.where, bf16[384,512]{1,0:T(8,128)(2,1)S(1)} %get-tuple-element.123.refs_2_.refs_3_.key_ref, ...), custom_call_target="tpu_custom_call" | custom-call | flops 1024 | bytes 1024 | tf_op jit(solution)/shard_map/pallas_call | solution.py:204
  7.3 0.1 collective-permute-start.1
  7.4 2.9 %collective-permute-start.2 = (bf16[512,128]{1,0:T(8,128)(2,1)S(1)}, bf16[512,128]{1,0:T(8,128)(2,1)S(1)}, u32[]{:S(2)}, u32[]{:S(2)}) collective-permute-start(bf16[512,128]{1,0:T(8,128)(2,1)S(1)} %fusion.2), channel_id=1, source_target_pairs={{0,2},{1,3},{2,0},{3,1},{4,6},{5,7},{6,4},{7,5},{8,10},{9,11},{10,... | collective-permute-start | bytes 393224 | tf_op jit(solution)/shard_map/ppermute | solution.py:217
  10.3 1.9 %shard_map.87 = (f32[512,128]{1,0:T(8,128)S(1)}, bf16[384,512]{1,0:T(8,128)(2,1)S(1)}, bf16[384,512]{1,0:T(8,128)(2,1)S(1)}) custom-call(s32[2]{0:T(128)S(1)} %get-tuple-element.98.refs_0_.refs_1_.where, s32[2]{0:T(128)S(1)} %get-tuple-element.99.refs_0_.refs_1_.where, bf16[384,512]{1,0:T(8,128)(2,1)S(1)} %get-tuple-element.115.refs_2_.refs_3_.key_ref, ...), custom_call_target="tpu_custom_call" | custom-call | flops 1024 | bytes 1024 | tf_op jit(solution)/shard_map/pallas_call | solution.py:204
  12.2 2.4 %shard_map.88 = (f32[384,512]{1,0:T(8,128)S(1)}, bf16[384,512]{1,0:T(8,128)(2,1)S(1)}, bf16[384,512]{1,0:T(8,128)(2,1)S(1)}) custom-call(s32[2]{0:T(128)S(1)} %get-tuple-element.101.refs_2_.refs_3_.refs_0_.where, s32[2]{0:T(128)S(1)} %get-tuple-element.100.refs_0_.refs_1_.where, bf16[384,512]{1,0:T(8,128)(2,1)S(1)} %get-tuple-element.117.refs_2_.query_ref, ...), custom_call_target="tpu_custom_call" | custom-call | flops 1024 | bytes 1024 | tf_op jit(solution)/shard_map/pallas_call | solution.py:204
  14.7 5.5 %collective-permute-start.5 = (bf16[512,128]{1,0:T(8,128)(2,1)S(1)}, bf16[512,128]{1,0:T(8,128)(2,1)S(1)}, u32[]{:S(2)}, u32[]{:S(2)}) collective-permute-start(bf16[512,128]{1,0:T(8,128)(2,1)S(1)} %fusion.5), channel_id=1, source_target_pairs={{0,12},{1,13},{2,14},{3,15},{16,28},{17,29},{18,30},{19,31}} | collective-permute-start | bytes 393224 | tf_op jit(solution)/shard_map/ppermute | solution.py:217
  20.2 1.3 %collective-permute-start.4 = (bf16[512,128]{1,0:T(8,128)(2,1)S(1)}, bf16[512,128]{1,0:T(8,128)(2,1)S(1)}, u32[]{:S(2)}, u32[]{:S(2)}) collective-permute-start(bf16[512,128]{1,0:T(8,128)(2,1)S(1)} %fusion.5), channel_id=1, source_target_pairs={{0,8},{1,9},{2,10},{3,11},{4,12},{5,13},{6,14},{7,15},{16,24},{17,... | collective-permute-start | bytes 393224 | tf_op jit(solution)/shard_map/ppermute | solution.py:217
  21.5 2.5 %collective-permute-start.3 = (bf16[512,128]{1,0:T(8,128)(2,1)S(1)}, bf16[512,128]{1,0:T(8,128)(2,1)S(1)}, u32[]{:S(2)}, u32[]{:S(2)}) collective-permute-start(bf16[512,128]{1,0:T(8,128)(2,1)S(1)} %fusion.5), channel_id=1, source_target_pairs={{0,4},{1,5},{2,6},{3,7},{4,8},{5,9},{6,10},{7,11},{8,12},{9,13},{1... | collective-permute-start | bytes 393224 | tf_op jit(solution)/shard_map/ppermute | solution.py:217
  24.0 2.4 %shard_map.89 = (f32[384,512]{1,0:T(8,128)S(1)}, bf16[384,512]{1,0:T(8,128)(2,1)S(1)}, bf16[384,512]{1,0:T(8,128)(2,1)S(1)}) custom-call(s32[2]{0:T(128)S(1)} %get-tuple-element.98.refs_0_.refs_1_.where, s32[2]{0:T(128)S(1)} %get-tuple-element.99.refs_0_.refs_1_.where, bf16[384,512]{1,0:T(8,128)(2,1)S(1)} %get-tuple-element.122.refs_2_.query_ref, ...), custom_call_target="tpu_custom_call" | custom-call | flops 1024 | bytes 1024 | tf_op jit(solution)/shard_map/pallas_call | solution.py:204
  26.4 2.4 %shard_map.90 = (f32[384,512]{1,0:T(8,128)S(1)}, bf16[384,512]{1,0:T(8,128)(2,1)S(1)}, bf16[384,512]{1,0:T(8,128)(2,1)S(1)}) custom-call(s32[2]{0:T(128)S(1)} %get-tuple-element.101.refs_2_.refs_3_.refs_0_.where, s32[2]{0:T(128)S(1)} %get-tuple-element.100.refs_0_.refs_1_.where, bf16[384,512]{1,0:T(8,128)(2,1)S(1)} %get-tuple-element.131.refs_2_.query_ref, ...), custom_call_target="tpu_custom_call" | custom-call | flops 1024 | bytes 1024 | tf_op jit(solution)/shard_map/pallas_call | solution.py:204
  28.8 1.0 %shard_map.91.mixed_ref = f32[384,512]{1,0:T(8,128)S(1)} custom-call(bf16[384,512]{1,0:T(8,128)(2,1)S(1)} %get-tuple-element.135.refs_0_.query_ref, bf16[384,512]{1,0:T(8,128)(2,1)S(1)} %get-tuple-element.136.refs_1_.key_ref, bf16[384,512]{1,0:T(8,128)(2,1)S(1)} %get-tuple-element.137.refs_2_.value_ref), custom_call_target="tpu_custom_call" | custom-call | flops 1024 | bytes 1024 | tf_op jit(solution)/shard_map/pallas_call | solution.py:204
  29.8 0.2 add_convert_fusion.5
  30.0 1.5 %shard_map.92 = (bf16[384,512]{1,0:T(8,128)(2,1)S(1)}, bf16[528,128]{1,0:T(8,128)(2,1)S(1)}) custom-call(s32[2]{0:T(128)S(1)} %get-tuple-element.98.refs_0_.refs_1_.where, bf16[384,512]{1,0:T(8,128)(2,1)S(1)} %get-tuple-element.117.refs_2_.query_ref, bf16[384,512]{1,0:T(8,128)(2,1)S(1)} %get-tuple-element.125.cotan_ref, f32[1,2048]{1,0:T(1,128)S(1)} %bitcast.6, ...), custom_call_target="tpu_custom_call" | custom-call | flops 1024 | bytes 1024 | tf_op jit(solution)/shard_map/pallas_call | solution.py:204
  31.5 0.1 collective-permute-start.8
  31.6 0.5 collective-permute-start.7
  32.1 1.2 %collective-permute-start.6 = (bf16[512,128]{1,0:T(8,128)(2,1)S(1)}, bf16[512,128]{1,0:T(8,128)(2,1)S(1)}, u32[]{:S(2)}, u32[]{:S(2)}) collective-permute-start(bf16[512,128]{1,0:T(8,128)(2,1)S(1)} %get-tuple-element.197), channel_id=1, source_target_pairs={{0,2},{1,3},{2,0},{3,1},{4,6},{5,7},{6,4},{7,5},{8,10},{9,11},{10,... | collective-permute-start | bytes 393224 | tf_op jit(solution)/shard_map/ppermute | solution.py:217
  33.3 1.6 %shard_map.93 = (bf16[384,512]{1,0:T(8,128)(2,1)S(1)}, f32[528,128]{1,0:T(8,128)S(1)}) custom-call(s32[2]{0:T(128)S(1)} %get-tuple-element.99.refs_0_.refs_1_.where, bf16[384,512]{1,0:T(8,128)(2,1)S(1)} %get-tuple-element.122.refs_2_.query_ref, bf16[384,512]{1,0:T(8,128)(2,1)S(1)} %get-tuple-element.146.cotan_ref, f32[1,2048]{1,0:T(1,128)S(1)} %bitcast.7, ...), custom_call_target="tpu_custom_call" | custom-call | flops 1024 | bytes 1024 | tf_op jit(solution)/shard_map/pallas_call | solution.py:204
  34.9 1.1 %collective-permute-start.11 = (bf16[528,128]{1,0:T(8,128)(2,1)S(1)}, bf16[528,128]{1,0:T(8,128)(2,1)S(1)}, u32[]{:S(2)}, u32[]{:S(2)}) collective-permute-start(bf16[528,128]{1,0:T(8,128)(2,1)S(1)} %add_convert_fusion.4), channel_id=1, source_target_pairs={{0,2},{1,3},{2,0},{3,1},{4,6},{5,7},{6,4},{7,5},{8,10},{9,11},{10,... | collective-permute-start | bytes 405512 | tf_op jit(solution)/shard_map/ppermute | solution.py:217
  36.0 1.6 %collective-permute-done.6 = bf16[512,128]{1,0:T(8,128)(2,1)S(1)} collective-permute-done((bf16[512,128]{1,0:T(8,128)(2,1)S(1)}, bf16[512,128]{1,0:T(8,128)(2,1)S(1)}, u32[]{:S(2)}, u32[]{:S(2)}) %collective-permute-start.6) | collective-permute-done | bytes 131104 | tf_op jit(solution)/shard_map/ppermute | solution.py:217
  37.6 0.1 fusion.7
  37.7 0.1 collective-permute-start.9
  37.8 1.5 %shard_map.95 = (bf16[384,512]{1,0:T(8,128)(2,1)S(1)}, bf16[528,128]{1,0:T(8,128)(2,1)S(1)}) custom-call(s32[2]{0:T(128)S(1)} %get-tuple-element.101.refs_2_.refs_3_.refs_0_.where, bf16[384,512]{1,0:T(8,128)(2,1)S(1)} %get-tuple-element.131.refs_2_.query_ref, bf16[384,512]{1,0:T(8,128)(2,1)S(1)} %get-tuple-element.152.cotan_ref, f32[1,2048]{1,0:T(1,128)S(1)} %bitcast.8, ...), custom_call_target="tpu_custom_call" | custom-call | flops 1024 | bytes 1024 | tf_op jit(solution)/shard_map/pallas_call | solution.py:204
  39.3 0.6 collective-permute-start.10
  39.9 1.6 %shard_map.94 = (bf16[384,512]{1,0:T(8,128)(2,1)S(1)}, f32[528,128]{1,0:T(8,128)S(1)}) custom-call(s32[2]{0:T(128)S(1)} %get-tuple-element.100.refs_0_.refs_1_.where, bf16[384,512]{1,0:T(8,128)(2,1)S(1)} %get-tuple-element.135.refs_0_.query_ref, bf16[384,512]{1,0:T(8,128)(2,1)S(1)} %get-tuple-element.145.cotan_ref, f32[1,2048]{1,0:T(1,128)S(1)} %bitcast.9, ...), custom_call_target="tpu_custom_call" | custom-call | flops 1024 | bytes 1024 | tf_op jit(solution)/shard_map/pallas_call | solution.py:204
  41.5 3.0 %collective-permute-start.14 = (bf16[528,128]{1,0:T(8,128)(2,1)S(1)}, bf16[528,128]{1,0:T(8,128)(2,1)S(1)}, u32[]{:S(2)}, u32[]{:S(2)}) collective-permute-start(bf16[528,128]{1,0:T(8,128)(2,1)S(1)} %add_convert_fusion.3), channel_id=1, source_target_pairs={{0,4},{1,5},{2,6},{3,7},{4,8},{5,9},{6,10},{7,11},{8,12},{9,13},{1... | collective-permute-start | bytes 405512 | tf_op jit(solution)/shard_map/ppermute | solution.py:217
  44.6 2.0 %collective-permute-start.13 = (bf16[528,128]{1,0:T(8,128)(2,1)S(1)}, bf16[528,128]{1,0:T(8,128)(2,1)S(1)}, u32[]{:S(2)}, u32[]{:S(2)}) collective-permute-start(bf16[528,128]{1,0:T(8,128)(2,1)S(1)} %add_convert_fusion.3), channel_id=1, source_target_pairs={{0,8},{1,9},{2,10},{3,11},{4,12},{5,13},{6,14},{7,15},{8,0},{9,1},... | collective-permute-start | bytes 405512 | tf_op jit(solution)/shard_map/ppermute | solution.py:217
  46.6 2.9 %collective-permute-start.12 = (bf16[528,128]{1,0:T(8,128)(2,1)S(1)}, bf16[528,128]{1,0:T(8,128)(2,1)S(1)}, u32[]{:S(2)}, u32[]{:S(2)}) collective-permute-start(bf16[528,128]{1,0:T(8,128)(2,1)S(1)} %add_convert_fusion.3), channel_id=1, source_target_pairs={{0,12},{1,13},{2,14},{3,15},{4,0},{5,1},{6,2},{7,3},{8,4},{9,5},{1... | collective-permute-start | bytes 405512 | tf_op jit(solution)/shard_map/ppermute | solution.py:217
  49.5 3.7 %shard_map.96 = (f32[384,512]{1,0:T(8,128)S(1)}, f32[384,512]{1,0:T(8,128)S(1)}, bf16[384,2048]{1,0:T(8,128)(2,1)}) custom-call(s32[2]{0:T(128)S(1)} %get-tuple-element.100.refs_0_.refs_1_.where, bf16[384,512]{1,0:T(8,128)(2,1)S(1)} %get-tuple-element.135.refs_0_.query_ref, bf16[384,512]{1,0:T(8,128)(2,1)S(1)} %get-tuple-element.136.refs_1_.key_ref, ...), custom_call_target="tpu_custom_call" | custom-call | flops 1024 | bytes 1024 | tf_op jit(solution)/shard_map/pallas_call | solution.py:204
  53.2 3.7 %shard_map.97 = (f32[384,512]{1,0:T(8,128)S(1)}, f32[384,512]{1,0:T(8,128)S(1)}, bf16[384,2048]{1,0:T(8,128)(2,1)}) custom-call(s32[2]{0:T(128)S(1)} %get-tuple-element.101.refs_2_.refs_3_.refs_0_.where, bf16[384,512]{1,0:T(8,128)(2,1)S(1)} %get-tuple-element.131.refs_2_.query_ref, ...), custom_call_target="tpu_custom_call", output_to_operand_aliasing={{2}: (6, {})} | custom-call | flops 1024 | bytes 1024 | tf_op jit(solution)/shard_map/pallas_call | solution.py:204
  56.9 3.7 %shard_map.98 = (f32[384,512]{1,0:T(8,128)S(1)}, f32[384,512]{1,0:T(8,128)S(1)}, bf16[384,2048]{1,0:T(8,128)(2,1)}) custom-call(s32[2]{0:T(128)S(1)} %get-tuple-element.99.refs_0_.refs_1_.where, bf16[384,512]{1,0:T(8,128)(2,1)S(1)} %get-tuple-element.122.refs_2_.query_ref, ...), custom_call_target="tpu_custom_call", output_to_operand_aliasing={{2}: (6, {})} | custom-call | flops 1024 | bytes 1024 | tf_op jit(solution)/shard_map/pallas_call | solution.py:204
  60.7 0.1 broadcast_select_fusion.1
  60.8 0.1 broadcast_select_fusion.2
  61.0 0.1 broadcast_select_fusion.3
  61.1 0.3 add_convert_fusion
  61.4 0.1 collective-permute-start.16
  61.5 0.7 collective-permute-start.15
  62.2 1.7 %shard_map.99 = (bf16[384,2048]{1,0:T(8,128)(2,1)}, bf16[384,2048]{1,0:T(8,128)(2,1)}, f32[1,2048]{1,0:T(1,128)S(1)}) custom-call(s32[2]{0:T(128)S(1)} %get-tuple-element.100.refs_0_.refs_1_.where, bf16[384,512]{1,0:T(8,128)(2,1)S(1)} %get-tuple-element.136.refs_1_.key_ref, bf16[384,512]{1,0:T(8,128)(2,1)S(1)} %get-tuple-element.137.refs_2_.value_ref, ...), custom_call_target="tpu_custom_call" | custom-call | flops 1024 | bytes 1024 | tf_op jit(solution)/shard_map/pallas_call | solution.py:204
  63.9 3.7 %shard_map.100 = (f32[384,512]{1,0:T(8,128)S(1)}, f32[384,512]{1,0:T(8,128)S(1)}, bf16[384,2048]{1,0:T(8,128)(2,1)}) custom-call(s32[2]{0:T(128)S(1)} %get-tuple-element.98.refs_0_.refs_1_.where, bf16[384,512]{1,0:T(8,128)(2,1)S(1)} %get-tuple-element.117.refs_2_.query_ref, ...), custom_call_target="tpu_custom_call", output_to_operand_aliasing={{2}: (6, {})} | custom-call | flops 1024 | bytes 1024 | tf_op jit(solution)/shard_map/pallas_call | solution.py:204
  67.6 1.7 %shard_map.101 = (bf16[384,2048]{1,0:T(8,128)(2,1)}, bf16[384,2048]{1,0:T(8,128)(2,1)}, f32[1,2048]{1,0:T(1,128)S(1)}) custom-call(s32[2]{0:T(128)S(1)} %get-tuple-element.101.refs_2_.refs_3_.refs_0_.where, bf16[384,512]{1,0:T(8,128)(2,1)S(1)} %get-tuple-element.132.refs_2_.refs_3_.key_ref, ...), custom_call_target="tpu_custom_call", output_to_operand_aliasing={{0}: (7, {}), {1}: (8, {})} | custom-call | flops 1024 | bytes 1024 | tf_op jit(solution)/shard_map/pallas_call | solution.py:204
  69.4 0.2 fusion.1
  69.6 0.3 collective-permute-start.17
  69.8 1.7 %shard_map.102 = (bf16[384,2048]{1,0:T(8,128)(2,1)}, bf16[384,2048]{1,0:T(8,128)(2,1)}, f32[1,2048]{1,0:T(1,128)S(1)}) custom-call(s32[2]{0:T(128)S(1)} %get-tuple-element.99.refs_0_.refs_1_.where, bf16[384,512]{1,0:T(8,128)(2,1)S(1)} %get-tuple-element.123.refs_2_.refs_3_.key_ref, ...), custom_call_target="tpu_custom_call", output_to_operand_aliasing={{0}: (7, {}), {1}: (8, {})} | custom-call | flops 1024 | bytes 1024 | tf_op jit(solution)/shard_map/pallas_call | solution.py:204
  71.6 2.3 %shard_map.103 = (bf16[384,2048]{1,0:T(8,128)(2,1)}, bf16[384,2048]{1,0:T(8,128)(2,1)}, f32[1,2048]{1,0:T(1,128)}) custom-call(s32[2]{0:T(128)S(1)} %get-tuple-element.98.refs_0_.refs_1_.where, bf16[384,512]{1,0:T(8,128)(2,1)S(1)} %get-tuple-element.115.refs_2_.refs_3_.key_ref, ...), custom_call_target="tpu_custom_call", output_to_operand_aliasing={{0}: (7, {}), {1}: (8, {})} | custom-call | flops 1024 | bytes 1024 | tf_op jit(solution)/shard_map/pallas_call | solution.py:204
  (28 shorter events, 0.3 us)
Async XLA Ops:
  2.9 2.4 %collective-permute-start = (bf16[512,128]{1,0:T(8,128)(2,1)S(1)}, bf16[512,128]{1,0:T(8,128)(2,1)S(1)}, u32[]{:S(2)}, u32[]{:S(2)}) collective-permute-start(bf16[512,128]{1,0:T(8,128)(2,1)S(1)} %get-tuple-element.104), channel_id=1, source_target_pairs={{0,1},{1,0},{2,3},{3,2},{4,5},{5,4},{6,7},{7,6},{8,9},{9,8},{10,11... | collective-permute-start | bytes 393224 | tf_op jit(solution)/shard_map/ppermute | solution.py:217
  7.3 7.3 %collective-permute-start.1 = (bf16[512,128]{1,0:T(8,128)(2,1)S(1)}, bf16[512,128]{1,0:T(8,128)(2,1)S(1)}, u32[]{:S(2)}, u32[]{:S(2)}) collective-permute-start(bf16[512,128]{1,0:T(8,128)(2,1)S(1)} %get-tuple-element.114), channel_id=1, source_target_pairs={{0,1},{1,0},{2,3},{3,2},{4,5},{5,4},{6,7},{7,6},{8,9},{9,8},{10,11... | collective-permute-start | bytes 393224 | tf_op jit(solution)/shard_map/ppermute | solution.py:217
  7.4 7.3 %collective-permute-start.2 = (bf16[512,128]{1,0:T(8,128)(2,1)S(1)}, bf16[512,128]{1,0:T(8,128)(2,1)S(1)}, u32[]{:S(2)}, u32[]{:S(2)}) collective-permute-start(bf16[512,128]{1,0:T(8,128)(2,1)S(1)} %fusion.2), channel_id=1, source_target_pairs={{0,2},{1,3},{2,0},{3,1},{4,6},{5,7},{6,4},{7,5},{8,10},{9,11},{10,... | collective-permute-start | bytes 393224 | tf_op jit(solution)/shard_map/ppermute | solution.py:217
  14.7 15.1 %collective-permute-start.5 = (bf16[512,128]{1,0:T(8,128)(2,1)S(1)}, bf16[512,128]{1,0:T(8,128)(2,1)S(1)}, u32[]{:S(2)}, u32[]{:S(2)}) collective-permute-start(bf16[512,128]{1,0:T(8,128)(2,1)S(1)} %fusion.5), channel_id=1, source_target_pairs={{0,12},{1,13},{2,14},{3,15},{16,28},{17,29},{18,30},{19,31}} | collective-permute-start | bytes 393224 | tf_op jit(solution)/shard_map/ppermute | solution.py:217
  20.2 9.6 %collective-permute-start.4 = (bf16[512,128]{1,0:T(8,128)(2,1)S(1)}, bf16[512,128]{1,0:T(8,128)(2,1)S(1)}, u32[]{:S(2)}, u32[]{:S(2)}) collective-permute-start(bf16[512,128]{1,0:T(8,128)(2,1)S(1)} %fusion.5), channel_id=1, source_target_pairs={{0,8},{1,9},{2,10},{3,11},{4,12},{5,13},{6,14},{7,15},{16,24},{17,... | collective-permute-start | bytes 393224 | tf_op jit(solution)/shard_map/ppermute | solution.py:217
  21.5 8.3 %collective-permute-start.3 = (bf16[512,128]{1,0:T(8,128)(2,1)S(1)}, bf16[512,128]{1,0:T(8,128)(2,1)S(1)}, u32[]{:S(2)}, u32[]{:S(2)}) collective-permute-start(bf16[512,128]{1,0:T(8,128)(2,1)S(1)} %fusion.5), channel_id=1, source_target_pairs={{0,4},{1,5},{2,6},{3,7},{4,8},{5,9},{6,10},{7,11},{8,12},{9,13},{1... | collective-permute-start | bytes 393224 | tf_op jit(solution)/shard_map/ppermute | solution.py:217
  28.8 1.2 %copy-start = (f32[2048]{0:T(1024)S(1)}, f32[2048]{0:T(1024)}, u32[]{:S(2)}) copy-start(f32[2048]{0:T(1024)} %param.9) | copy-start | bytes 24580
  31.5 3.3 %collective-permute-start.8 = (bf16[528,128]{1,0:T(8,128)(2,1)S(1)}, bf16[528,128]{1,0:T(8,128)(2,1)S(1)}, u32[]{:S(2)}, u32[]{:S(2)}) collective-permute-start(bf16[528,128]{1,0:T(8,128)(2,1)S(1)} %get-tuple-element.148), channel_id=1, source_target_pairs={{0,1},{1,0},{2,3},{3,2},{4,5},{5,4},{6,7},{7,6},{8,9},{9,8},{10,11... | collective-permute-start | bytes 405512 | tf_op jit(solution)/shard_map/ppermute | solution.py:217
  31.6 1.7 %collective-permute-start.7 = (bf16[512,128]{1,0:T(8,128)(2,1)S(1)}, bf16[512,128]{1,0:T(8,128)(2,1)S(1)}, u32[]{:S(2)}, u32[]{:S(2)}) collective-permute-start(bf16[512,128]{1,0:T(8,128)(2,1)S(1)} %get-tuple-element.195), channel_id=1, source_target_pairs={{0,1},{1,0},{2,3},{3,2},{4,5},{5,4},{6,7},{7,6},{8,9},{9,8},{10,11... | collective-permute-start | bytes 393224 | tf_op jit(solution)/shard_map/ppermute | solution.py:217
  32.1 5.5 %collective-permute-start.6 = (bf16[512,128]{1,0:T(8,128)(2,1)S(1)}, bf16[512,128]{1,0:T(8,128)(2,1)S(1)}, u32[]{:S(2)}, u32[]{:S(2)}) collective-permute-start(bf16[512,128]{1,0:T(8,128)(2,1)S(1)} %get-tuple-element.197), channel_id=1, source_target_pairs={{0,2},{1,3},{2,0},{3,1},{4,6},{5,7},{6,4},{7,5},{8,10},{9,11},{10,... | collective-permute-start | bytes 393224 | tf_op jit(solution)/shard_map/ppermute | solution.py:217
  34.9 6.5 %collective-permute-start.11 = (bf16[528,128]{1,0:T(8,128)(2,1)S(1)}, bf16[528,128]{1,0:T(8,128)(2,1)S(1)}, u32[]{:S(2)}, u32[]{:S(2)}) collective-permute-start(bf16[528,128]{1,0:T(8,128)(2,1)S(1)} %add_convert_fusion.4), channel_id=1, source_target_pairs={{0,2},{1,3},{2,0},{3,1},{4,6},{5,7},{6,4},{7,5},{8,10},{9,11},{10,... | collective-permute-start | bytes 405512 | tf_op jit(solution)/shard_map/ppermute | solution.py:217
  37.7 2.2 %collective-permute-start.9 = (bf16[512,128]{1,0:T(8,128)(2,1)S(1)}, bf16[512,128]{1,0:T(8,128)(2,1)S(1)}, u32[]{:S(2)}, u32[]{:S(2)}) collective-permute-start(bf16[512,128]{1,0:T(8,128)(2,1)S(1)} %get-tuple-element.200), channel_id=1, source_target_pairs={{0,1},{1,0},{2,3},{3,2},{4,5},{5,4},{6,7},{7,6},{8,9},{9,8},{10,11... | collective-permute-start | bytes 393224 | tf_op jit(solution)/shard_map/ppermute | solution.py:217
  39.3 2.2 %collective-permute-start.10 = (bf16[528,128]{1,0:T(8,128)(2,1)S(1)}, bf16[528,128]{1,0:T(8,128)(2,1)S(1)}, u32[]{:S(2)}, u32[]{:S(2)}) collective-permute-start(bf16[528,128]{1,0:T(8,128)(2,1)S(1)} %get-tuple-element.153), channel_id=1, source_target_pairs={{0,1},{1,0},{2,3},{3,2},{4,5},{5,4},{6,7},{7,6},{8,9},{9,8},{10,11... | collective-permute-start | bytes 405512 | tf_op jit(solution)/shard_map/ppermute | solution.py:217
  41.5 19.1 %collective-permute-start.14 = (bf16[528,128]{1,0:T(8,128)(2,1)S(1)}, bf16[528,128]{1,0:T(8,128)(2,1)S(1)}, u32[]{:S(2)}, u32[]{:S(2)}) collective-permute-start(bf16[528,128]{1,0:T(8,128)(2,1)S(1)} %add_convert_fusion.3), channel_id=1, source_target_pairs={{0,4},{1,5},{2,6},{3,7},{4,8},{5,9},{6,10},{7,11},{8,12},{9,13},{1... | collective-permute-start | bytes 405512 | tf_op jit(solution)/shard_map/ppermute | solution.py:217
  44.6 16.2 %collective-permute-start.13 = (bf16[528,128]{1,0:T(8,128)(2,1)S(1)}, bf16[528,128]{1,0:T(8,128)(2,1)S(1)}, u32[]{:S(2)}, u32[]{:S(2)}) collective-permute-start(bf16[528,128]{1,0:T(8,128)(2,1)S(1)} %add_convert_fusion.3), channel_id=1, source_target_pairs={{0,8},{1,9},{2,10},{3,11},{4,12},{5,13},{6,14},{7,15},{8,0},{9,1},... | collective-permute-start | bytes 405512 | tf_op jit(solution)/shard_map/ppermute | solution.py:217
  46.6 14.4 %collective-permute-start.12 = (bf16[528,128]{1,0:T(8,128)(2,1)S(1)}, bf16[528,128]{1,0:T(8,128)(2,1)S(1)}, u32[]{:S(2)}, u32[]{:S(2)}) collective-permute-start(bf16[528,128]{1,0:T(8,128)(2,1)S(1)} %add_convert_fusion.3), channel_id=1, source_target_pairs={{0,12},{1,13},{2,14},{3,15},{4,0},{5,1},{6,2},{7,3},{8,4},{9,5},{1... | collective-permute-start | bytes 405512 | tf_op jit(solution)/shard_map/ppermute | solution.py:217
  61.4 6.2 %collective-permute-start.16 = (bf16[528,128]{1,0:T(8,128)(2,1)S(1)}, bf16[528,128]{1,0:T(8,128)(2,1)S(1)}, u32[]{:S(2)}, u32[]{:S(2)}) collective-permute-start(bf16[528,128]{1,0:T(8,128)(2,1)S(1)} %get-tuple-element.192), channel_id=1, source_target_pairs={{0,1},{1,0},{2,3},{3,2},{4,5},{5,4},{6,7},{7,6},{8,9},{9,8},{10,11... | collective-permute-start | bytes 405512 | tf_op jit(solution)/shard_map/ppermute | solution.py:217
  61.5 7.9 %collective-permute-start.15 = (bf16[528,128]{1,0:T(8,128)(2,1)S(1)}, bf16[528,128]{1,0:T(8,128)(2,1)S(1)}, u32[]{:S(2)}, u32[]{:S(2)}) collective-permute-start(bf16[528,128]{1,0:T(8,128)(2,1)S(1)} %get-tuple-element.193), channel_id=1, source_target_pairs={{0,2},{1,3},{2,0},{3,1},{4,6},{5,7},{6,4},{7,5},{8,10},{9,11},{10,... | collective-permute-start | bytes 405512 | tf_op jit(solution)/shard_map/ppermute | solution.py:217
  69.6 2.0 %collective-permute-start.17 = (bf16[528,128]{1,0:T(8,128)(2,1)S(1)}, bf16[528,128]{1,0:T(8,128)(2,1)S(1)}, u32[]{:S(2)}, u32[]{:S(2)}) collective-permute-start(bf16[528,128]{1,0:T(8,128)(2,1)S(1)} %get-tuple-element.199), channel_id=1, source_target_pairs={{0,1},{1,0},{2,3},{3,2},{4,5},{5,4},{6,7},{7,6},{8,9},{9,8},{10,11... | collective-permute-start | bytes 405512 | tf_op jit(solution)/shard_map/ppermute | solution.py:217

commit v4 on v3

v4 whole, which is shorter than its diff:
```python
import functools

import jax
import jax.numpy as jnp
from jax import lax
from jax.experimental import pallas as pl
from jax.experimental.pallas import tpu as pltpu
from jax.sharding import PartitionSpec as P

HEADS = 16
HEAD = 128
TILE = 128
QUARTER = HEADS // 4
SPAN = QUARTER * HEAD
WORK, LIGHT = 2_000_000_000, 300_000_000
PIECES = 2
EXTRA = 16
norm_eps = 1e-05
f32 = jnp.float32
bf16 = jnp.bfloat16

VMEM = pl.BlockSpec(memory_space=pltpu.VMEM)
SMEM = pl.BlockSpec(memory_space=pltpu.SMEM)
HBM = pl.BlockSpec(memory_space=pltpu.HBM)


def decay(x):
    return jnp.exp(jnp.minimum(x, 0.0))


def feature(x):
    return jnp.where(x > 0, x + 1.0, decay(x)).astype(bf16)


def mm(a, b):
    return lax.dot_general(a, b, (((1,), (0,)), ((), ())), preferred_element_type=f32)


def mm_nt(a, b):
    return lax.dot_general(a, b, (((1,), (1,)), ((), ())), preferred_element_type=f32)


def mm_tn(a, b):
    return lax.dot_general(a, b, (((0,), (0,)), ((), ())), preferred_element_type=f32)


def own(head):
    return slice(head * HEAD, (head + 1) * HEAD)


def span(where):
    return pl.ds(pl.multiple_of((2 * where[0] + where[1]) * SPAN, SPAN), SPAN)


def place(where, head):
    start = (2 * where[0] + where[1]) * SPAN + head * HEAD
    return pl.ds(pl.multiple_of(start, HEAD), HEAD)


def lower(rows, depth, length):
    keep = lax.broadcasted_iota(jnp.int32, (TILE, TILE), 0) >= lax.broadcasted_iota(
        jnp.int32, (TILE, TILE), 1
    )
    strips = []
    for start in range(0, length, TILE):
        strip = mm_nt(rows[start : start + TILE], depth[: start + TILE])
        last = jnp.where(keep, strip[:, start:], 0.0).astype(bf16)
        if start:
            last = jnp.concatenate([strip[:, :start].astype(bf16), last], axis=1)
        strips.append(last)
    return strips


def upper(rows, depth, length):
    keep = lax.broadcasted_iota(jnp.int32, (TILE, TILE), 0) <= lax.broadcasted_iota(
        jnp.int32, (TILE, TILE), 1
    )
    strips = []
    for start in range(0, length, TILE):
        strip = mm_nt(rows[start : start + TILE], depth[start:])
        first = jnp.where(keep, strip[:, :TILE], 0.0).astype(bf16)
        if start + TILE < length:
            first = jnp.concatenate([first, strip[:, TILE:].astype(bf16)], axis=1)
        strips.append(first)
    return strips


def finish(copies):
    for copy in copies:
        copy.wait()


def state(key_ref, value_ref, own_ref):
    for head in range(QUARTER):
        key_map = feature(key_ref[:, own(head)].astype(f32))
        own_ref[own(head), :] = mm_tn(key_map, value_ref[:, own(head)]).astype(own_ref.dtype)


def inner(query_ref, key_ref, value_ref, mixed_ref):
    length = query_ref.shape[0]
    for head in range(QUARTER):
        query_map = feature(query_ref[:, own(head)].astype(f32))
        key_map = feature(key_ref[:, own(head)].astype(f32))
        value = value_ref[:, own(head)]
        for i, strip in enumerate(lower(query_map, key_map, length)):
            start = i * TILE
            mixed_ref[start : start + TILE, own(head)] = mm(strip, value[: start + TILE])


def chunked(source, target, sem, pieces):
    rows = source.shape[0] // pieces
    return [
        pltpu.make_async_copy(
            source.at[pl.ds(i * rows, rows)], target.at[pl.ds(i * rows, rows)], sem.at[i]
        )
        for i in range(pieces)
    ]


def moving_kernel(body, counts, first, *refs):
    loads, store_to, body_ins, body_outs, wholes, scratch, named = counts
    stores = len(store_to)
    refs = list(refs)

    def take(number):
        taken = refs[:number]
        del refs[:number]
        return taken

    load_at, store_at = take(loads), take(stores)
    ins, sources, ready = take(body_ins), take(loads), take(stores)
    take(wholes)
    outs, targets, results = take(body_outs), take(loads), take(named)
    rest, (sems,) = take(scratch), take(1)
    copies = []
    for i, (at, source, target) in enumerate(zip(load_at, sources, targets, strict=True)):
        copies.append(chunked(source.at[:, span(at)], target, sems.at[i], PIECES))
    for i, (at, source, to) in enumerate(zip(store_at, ready, store_to, strict=True)):
        target = results[to].at[:, span(at)]
        copies.append(chunked(source, target, sems.at[loads + i], PIECES))
    for copy in copies:
        for piece in copy:
            piece.start()
    for copy in copies[:first]:
        finish(copy)
    body(*targets[:first], *ins, *outs, *results, *rest)
    for copy in copies[first:]:
        finish(copy)


def norm_kernel(where, query_ref, cotan_ref, gain_ref, state_ref, mixed_ref, grad_ref, own_ref):
    own_ref[SPAN:, :] = jnp.zeros_like(own_ref[SPAN:, :])
    for head in range(QUARTER):
        query_map = feature(query_ref[:, own(head)].astype(f32))
        mixed = mixed_ref[:, own(head)] + mm(query_map, state_ref[own(head), :])
        inverse = lax.rsqrt(jnp.mean(mixed * mixed, axis=1, keepdims=True) + norm_eps)
        normed = mixed * inverse
        cotan = cotan_ref[:, own(head)].astype(f32)
        part = jnp.sum(cotan * normed, axis=0, keepdims=True)
        own_ref[SPAN + head : SPAN + head + 1, :] = part.astype(own_ref.dtype)
        scaled = cotan * gain_ref[:, place(where, head)]
        along = jnp.mean(scaled * normed, axis=1, keepdims=True)
        grad = ((scaled - normed * along) * inverse).astype(bf16)
        grad_ref[:, own(head)] = grad
        own_ref[own(head), :] = mm_tn(query_map, grad).astype(own_ref.dtype)


def back(query_ref, key_ref, value_ref, grad_ref, state_ref, dk_ref, dv_ref, dq_ref, *_):
    length = query_ref.shape[0]
    for head in range(QUARTER):
        query = query_ref[:, own(head)].astype(f32)
        query_map = feature(query)
        key_map = feature(key_ref[:, own(head)].astype(f32))
        value = value_ref[:, own(head)]
        grad = grad_ref[:, own(head)]
        far = mm_nt(grad, state_ref[own(head), :])
        slope = decay(query)
        for i, strip in enumerate(lower(grad, value, length)):
            rows = slice(i * TILE, (i + 1) * TILE)
            near = mm(strip, key_map[: (i + 1) * TILE])
            dq_ref[rows, own(head)] = ((near + far[rows]) * slope[rows]).astype(bf16)
        for i, strip in enumerate(upper(value, grad, length)):
            rows = slice(i * TILE, (i + 1) * TILE)
            dk_ref[rows, own(head)] = mm(strip, query_map[i * TILE :])
        for i, strip in enumerate(upper(key_map, query_map, length)):
            rows = slice(i * TILE, (i + 1) * TILE)
            dv_ref[rows, own(head)] = mm(strip, grad[i * TILE :])


def last_head(head, key_ref, value_ref, back_ref, dk_ref, dv_ref, key_grad_ref, value_grad_ref):
    key = key_ref[:, own(head)].astype(f32)
    back = back_ref[own(head), :]
    far = mm_nt(value_ref[:, own(head)], back)
    key_grad_ref[:, own(head)] = ((dk_ref[:, own(head)] + far) * decay(key)).astype(bf16)
    value_grad = dv_ref[:, own(head)] + mm(feature(key), back)
    value_grad_ref[:, own(head)] = value_grad.astype(bf16)


def last(key_ref, value_ref, back_ref, dk_ref, dv_ref, key_grad_ref, value_grad_ref, *_):
    for head in range(QUARTER):
        last_head(
            head, key_ref, value_ref, back_ref, dk_ref, dv_ref, key_grad_ref, value_grad_ref
        )


def very_last(*refs):
    wheres, refs = refs[:4], refs[4:]
    key_ref, value_ref, dk_ref, dv_ref, *backs = refs[:8]
    gain_ref, key_hbm, value_hbm, key_grad_ref, value_grad_ref, sems = refs[8:]
    for where, back_ref in zip(wheres, backs, strict=True):
        gains = back_ref[SPAN:, :].astype(f32)
        for head in range(QUARTER):
            gain_ref[:, place(where, head)] = gains[head : head + 1, :]
    copies = []
    for head in range(QUARTER):
        last_head(
            head, key_ref, value_ref, backs[0], dk_ref, dv_ref, key_grad_ref, value_grad_ref
        )
        for i, (held, whole) in enumerate(((key_grad_ref, key_hbm), (value_grad_ref, value_hbm))):
            copies.append(
                pltpu.make_async_copy(
                    held.at[:, own(head)], whole.at[:, place(wheres[0], head)], sems.at[i, head]
                )
            )
            copies[-1].start()
    finish(copies)


def call(kernel, ins, outs, scratch=(), kept=(), flops=WORK):
    return pl.pallas_call(
        kernel,
        out_shape=[jax.ShapeDtypeStruct(shape, dtype) for shape, dtype, _ in outs],
        in_specs=[spec for _, spec in ins] + [spec for _, spec, _ in kept],
        out_specs=[spec for _, _, spec in outs],
        scratch_shapes=list(scratch),
        input_output_aliases={len(ins) + i: out for i, (_, _, out) in enumerate(kept)},
        compiler_params=pltpu.CompilerParams(vmem_limit_bytes=12 << 20),
        cost_estimate=pl.CostEstimate(flops=flops, bytes_accessed=4 << 20, transcendentals=0),
    )(*[a for a, _ in ins], *[a for a, _, _ in kept])


def permute(value, pairs):
    return lax.ppermute(value, "seq", pairs)


def add(*terms):
    return functools.reduce(lambda a, b: a + b, [t.astype(f32) for t in terms])


def when(flag, wanted, value):
    value = value.astype(f32)
    return jnp.where(flag, value, 0.0) if wanted else jnp.where(flag, 0.0, value)


def after(value, *done):
    leaves, tree = jax.tree.flatten(value)
    held = lax.optimization_barrier((*leaves, *done))
    return jax.tree.unflatten(tree, held[: len(leaves)])


class Scan:
    def __init__(self, shards, reverse, odd_core, odd_chip, bits):
        self.shards = shards
        self.sign = -1 if reverse else 1
        self.second = not reverse
        self.odd_core, self.odd_chip, self.bits = odd_core, odd_chip, bits

    def swap_core(self, value):
        return permute(value, [(i, i ^ 1) for i in range(self.shards)])

    def swap_chip(self, value):
        return permute(value, [(i, i ^ 2) for i in range(self.shards)])

    def early(self, mine, got):
        self.early_mine, self.early_got = mine, got
        send = add(mine, got).astype(bf16)
        self.other = self.swap_chip(send)
        return send

    def late(self, mine, got):
        self.late_mine, self.late_got = mine, got
        self.near = add(mine, got)

    def open(self):
        self.total = add(self.near, self.other).astype(bf16)
        self.base = 0.0
        return self.total

    def exchange(self, level):
        step = 4 << level
        return permute(self.total, [(i, i ^ step) for i in range(self.shards)])

    def absorb(self, level, other):
        self.base = self.base + when(self.bits[level], self.second, other)
        self.total = add(self.total, other).astype(bf16)
        return self.total

    def alone(self, value, wanted):
        rows = lax.broadcasted_iota(jnp.int32, value.shape, 0)
        return jnp.where((rows >= SPAN) if wanted else (rows < SPAN), value, 0)

    def state(self, base, mine, got):
        if base.shape[0] > SPAN:
            mine, got = self.alone(mine, False), self.alone(got, False)
        here = add(base, when(self.odd_core, self.second, got)).astype(bf16)
        there = add(base, when(self.odd_core, not self.second, mine)).astype(bf16)
        return here, self.swap_core(there)

    def late_state(self):
        base, near, other = self.base, self.near, self.other
        if base.shape[0] > SPAN:
            base = self.alone(base, False) + self.alone(self.total, True).astype(f32)
            near, other = self.alone(near, False), self.alone(other, False)
        send = add(base, when(self.odd_chip, not self.second, near)).astype(bf16)
        self.back = self.swap_chip(send)
        base = add(base, when(self.odd_chip, self.second, other))
        return self.state(base, self.late_mine, self.late_got)

    def early_state(self):
        return self.state(self.back, self.early_mine, self.early_got)


def on_device(queries, key_vectors, value_vectors, out_cotangent, norm_gain):
    queries, key_vectors, value_vectors, out_cotangent = (
        pltpu.with_memory_space_constraint(a, pltpu.HBM)
        for a in (queries, key_vectors, value_vectors, out_cotangent)
    )
    length, width = queries.shape
    shards = lax.axis_size("seq")
    index = lax.axis_index("seq").astype(jnp.int32)
    core, chip, four = index % 2, index // 2 % 2, index // 4
    gain = norm_gain.reshape(1, width)
    where = {
        (a, b): jnp.stack([1 - core if a else core, 1 - chip if b else chip])
        for a in (0, 1)
        for b in (0, 1)
    }
    levels = range((shards // 4 - 1).bit_length())
    bits = [four // (1 << level) % 2 == 1 for level in levels]
    where, odd_core, odd_chip, bits = after((where, core == 1, chip == 1, bits))
    state_low = ((SPAN, HEAD), bf16, VMEM)
    state_wide = ((SPAN, HEAD), f32, VMEM)
    sums_low = ((SPAN + EXTRA, HEAD), bf16, VMEM)
    sums_wide = ((SPAN + EXTRA, HEAD), f32, VMEM)
    wide = ((length, SPAN), f32, VMEM)
    low = ((length, SPAN), bf16, VMEM)
    whole = ((length, width), bf16, HBM)
    row = ((1, width), f32, VMEM)
    held = lambda *arrays: [(a, VMEM) for a in arrays]
    sems = lambda *shape: pltpu.SemaphoreType.DMA(shape)
    wholes = {"q": queries, "k": key_vectors, "v": value_vectors, "c": out_cotangent}
    tile, results = {}, {}

    def moving(body, ins, outs, fetch=(), first=0, put=(), scratch=(), flops=WORK):
        names = list(dict.fromkeys(name for _, _, name in put))
        old = [(name, results[name]) for name in names if name in results]
        store_to = tuple(names.index(name) for _, _, name in put)
        counts = (len(fetch), store_to, len(ins), len(outs), len(old), len(scratch), len(names))
        result = call(
            functools.partial(moving_kernel, body, counts, first),
            [(where[which], SMEM) for _, which in fetch]
            + [(where[which], SMEM) for which, _, _ in put]
            + ins
            + [(wholes[name], HBM) for name, _ in fetch]
            + held(*[a for _, a, _ in put]),
            outs + [low] * len(fetch) + [whole] * len(names),
            [*scratch, sems(max(1, len(fetch) + len(put)), PIECES)],
            [(a, HBM, len(outs) + len(fetch) + names.index(name)) for name, a in old],
            flops,
        )
        for key, value in zip(fetch, result[len(outs) : len(outs) + len(fetch)], strict=True):
            tile[key] = value
        for name, value in zip(names, result[len(outs) + len(fetch) :], strict=True):
            results[name] = value
        return result[: len(outs)]

    def loading(body, ins, outs, fetch=(), first=0):
        return moving(body, held(*ins), outs, fetch, first)

    def tiles(names, which):
        return [tile[name, which] for name in names]

    every = [(1, 1), (0, 1), (1, 0), (0, 0)]
    fore = Scan(shards, False, odd_core, odd_chip, bits)
    (sent,) = loading(state, [], [state_low], [(name, w) for w in every for name in "kv"], 2)
    got = fore.swap_core(sent)
    (mine,) = loading(state, after(tiles("kv", (0, 1)), sent), [state_wide])
    send = fore.early(mine, got)
    (sent,) = loading(state, after(tiles("kv", (1, 0)), send), [state_low])
    got = fore.swap_core(sent)
    (mine,) = loading(
        state, after(tiles("kv", (0, 0)), sent), [state_wide], [("q", w) for w in every]
    )
    fore.late(mine, got)

    mixed = {}
    (mixed[0, 0],) = loading(inner, tiles("qkv", (0, 0)), [wide])
    fore.near = after(fore.near, mixed[0, 0])
    done = fore.open()
    plan = {0: [(1, 0)], 1: [(0, 1), (1, 1)]}
    fetched = {(1, 0): [("c", w) for w in every]}
    for level in levels:
        moved = fore.exchange(level)
        for which in plan.get(level, []):
            (done,) = loading(
                inner, after(tiles("qkv", which), done), [wide], fetched.get(which, [])
            )
            mixed[which] = done
        done = fore.absorb(level, after(moved, done))

    grads, seen = {}, {}
    aft = Scan(shards, True, odd_core, odd_chip, bits)

    def norm(which, state, kind, *done):
        query, cotan = tiles("qc", which)
        (cotan,) = after([cotan], *done) if done else [cotan]
        ins = [(where[which], SMEM)] + held(query, cotan, gain, state, mixed[which])
        return call(norm_kernel, ins, [low, kind])

    seen[0, 0], seen[1, 0] = fore.late_state()
    grads[0, 0], sent = norm((0, 0), seen[0, 0], sums_low)
    got = aft.swap_core(sent)
    grads[1, 0], mine = norm((1, 0), seen[1, 0], sums_wide)
    send = aft.early(mine, got)
    fore.back = after(fore.back, send)
    seen[0, 1], seen[1, 1] = fore.early_state()
    grads[0, 1], sent = norm((0, 1), seen[0, 1], sums_low, send)
    got = aft.swap_core(sent)
    grads[1, 1], mine = norm((1, 1), seen[1, 1], sums_wide)
    aft.late(mine, got)

    inner_grads, ready = {}, []

    def back_of(which, done, flops=WORK):
        grad = after(grads[which], done)
        *inner_grads[which], query_grad = moving(
            back, held(*tiles("qkv", which), grad, seen[which]), [wide, wide, low], flops=flops
        )
        ready.append((which, query_grad, "query"))
        return inner_grads[which][0]

    done = aft.open()
    plan = {0: [(1, 1)], 1: [(0, 1), (1, 0)]}
    for level in levels:
        moved = aft.exchange(level)
        for which in plan.get(level, []):
            done = back_of(which, done)
        done = aft.absorb(level, after(moved, done))

    def last_of(which, back_state):
        put = [ready.pop(0) for _ in range(len(ready))]
        key_grad, value_grad = moving(
            last,
            held(*tiles("kv", which), back_state, *inner_grads[which]),
            [low, low],
            put=put,
            flops=LIGHT,
        )
        ready.extend([(which, key_grad, "key"), (which, value_grad, "value")])
        return key_grad

    backs = {}
    backs[1, 1], backs[0, 1] = aft.late_state()
    done = last_of((1, 1), backs[1, 1])
    done = back_of((0, 0), done, LIGHT)
    inner_grads[0, 1][0] = after(inner_grads[0, 1][0], done)
    done = last_of((0, 1), backs[0, 1])
    aft.back = after(aft.back, done)
    backs[1, 0], backs[0, 0] = aft.early_state()
    last_of((1, 0), backs[1, 0])
    order = ((0, 0), (1, 0), (0, 1), (1, 1))
    (gain_grad,) = moving(
        very_last,
        [(where[which], SMEM) for which in order]
        + held(*tiles("kv", (0, 0)), *inner_grads[0, 0], *[backs[which] for which in order]),
        [row],
        put=list(ready),
        scratch=[pltpu.VMEM((length, SPAN), bf16)] * 2 + [sems(2, QUARTER)],
    )
    return results["query"], results["key"], results["value"], gain_grad.reshape(width)


def solution(mesh):
    tokens = P(("groups", "seq"), None)
    return jax.shard_map(
        on_device,
        mesh=mesh,
        in_specs=(tokens, tokens, tokens, tokens, P()),
        out_specs=(tokens, tokens, tokens, P("groups")),
        check_vma=False,
    )
```

time: 74.4 us -> 63.6 us (0.85)
  starting transfers between devices: 25.2 us -> 14.5 us
  waiting for transfers between devices: 1.65 us -> 9.43 us
  Pallas kernels: 44.4 us -> 37 us
    ppermute x18 -> x16, starting transfers between devices: 25.2 us -> 14.5 us  [permute(): return lax.ppermute(value, 'seq', pairs)]
    ppermute x18 -> x16, waiting for transfers between devices: 1.65 us -> 9.43 us  [permute(): return lax.ppermute(value, 'seq', pairs)]
    pallas_call x20, Pallas kernels: 44.4 us -> 37 us  [call(): pl.pallas_call(kernel, out_shape=[jax.ShapeDtypeStruct(shape, dtype) for...]
  transfers between devices with their start and end apart: 18 -> 16, of which waited for: 1 -> 6; matrix products, arithmetic and copies ran while one was open for 1% -> 0% of each run, Pallas kernels for 49% -> 50%
where the time goes in v4:
time: 63.6 us; the launch traced here: 63.4 us
  Pallas kernels  37 us (58%)
  starting transfers between devices  14.5 us (23%)
  waiting for transfers between devices  9.43 us (15%)
  between operations  1.21 us (2%)
  other arithmetic  1.18 us (2%)
    pallas_call x20, Pallas kernels, call(): pl.pallas_call(kernel, out_shape=[jax.ShapeDtypeStruct(shape, dtype) for...  37 us
    ppermute x16, starting transfers between devices, permute(): return lax.ppermute(value, 'seq', pairs)  14.5 us
    ppermute x16, waiting for transfers between devices, permute(): return lax.ppermute(value, 'seq', pairs)  9.43 us
  transfers between devices with their start and end apart: 16, of which 6 were waited for; matrix products, arithmetic and copies ran while one was open for 0% of the time, Pallas kernels for 50%

profile of v4, /device:TPU:0, one launch (start us, length us, event | category | flops | bytes accessed | tf_op | source)
XLA Modules:
  0.0 63.4 jit_solution(14433432661196368331)
XLA Ops:
  0.7 0.1 pad_add_fusion.2
  0.8 0.1 pad_add_fusion
  0.9 2.7 %shard_map.84 = (bf16[512,128]{1,0:T(8,128)(2,1)S(1)}, bf16[384,512]{1,0:T(8,128)(2,1)S(1)}, bf16[384,512]{1,0:T(8,128)(2,1)S(1)}, bf16[384,512]{1,0:T(8,128)(2,...) custom-call(s32[2]{0:T(128)S(1)} %get-tuple-element.94.refs_0_.refs_, ...), custom_call_target="tpu_custom_call" | custom-call | flops 2000000000 | bytes 4194304 | tf_op jit(solution)/shard_map/pallas_call | solution.py:230
  3.6 0.5 collective-permute-start
  4.1 0.4 shard_map.85
  4.5 0.6 collective-permute-done
  5.1 2.9 %collective-permute-start.2 = (bf16[512,128]{1,0:T(8,128)(2,1)S(1)}, bf16[512,128]{1,0:T(8,128)(2,1)S(1)}, u32[]{:S(2)}, u32[]{:S(2)}) collective-permute-start(bf16[512,128]{1,0:T(8,128)(2,1)S(1)} %fusion.7), channel_id=1, source_target_pairs={{0,2},{1,3},{2,0},{3,1},{4,6},{5,7},{6,4},{7,5},{8,10},{9,11},{10,... | collective-permute-start | bytes 393224 | tf_op jit(solution)/shard_map/ppermute | solution.py:243
  8.0 0.4 shard_map.86
  8.5 0.1 collective-permute-start.1
  8.5 2.3 %shard_map.87 = (f32[512,128]{1,0:T(8,128)S(1)}, bf16[384,512]{1,0:T(8,128)(2,1)S(1)}, bf16[384,512]{1,0:T(8,128)(2,1)S(1)}, bf16[384,512]{1,0:T(8,128)(2,1)S(1)}, bf16[384,512]{1,0:T(8,128)(2,1)S(1)}) custom-call(s32[2]{0:T(128)S(1)} %get-tuple-element.94.refs_0_.refs_1_.where.refs_5_, s32[2]{0:T(128)S(1)} %get-tuple-element.96.refs_2_.refs_3_.refs_1_.where.refs_0_.refs_4_, ...), custom_call_target="tpu_custom_call" | custom-call | flops 2000000000 | bytes 4194304 | tf_op jit(solution)/shard_map/pallas_call | solution.py:230
  10.8 1.0 %shard_map.88.mixed_ref = f32[384,512]{1,0:T(8,128)S(1)} custom-call(bf16[384,512]{1,0:T(8,128)(2,1)S(1)} %get-tuple-element.115.refs_0_.query_ref, bf16[384,512]{1,0:T(8,128)(2,1)S(1)} %get-tuple-element.110.refs_4_.refs_1_.refs_6_, bf16[384,512]{1,0:T(8,128)(2,1)S(1)} %get-tuple-element.111.refs_5_.refs_2_.refs_7_), custom_call_target="tpu_custom_call" | custom-call | flops 2000000000 | bytes 4194304 | tf_op jit(solution)/shard_map/pallas_call | solution.py:230
  12.0 1.8 %collective-permute-start.3 = (bf16[512,128]{1,0:T(8,128)(2,1)S(1)}, bf16[512,128]{1,0:T(8,128)(2,1)S(1)}, u32[]{:S(2)}, u32[]{:S(2)}) collective-permute-start(bf16[512,128]{1,0:T(8,128)(2,1)S(1)} %fusion.10), channel_id=1, source_target_pairs={{0,4},{1,5},{2,6},{3,7},{4,0},{5,1},{6,2},{7,3},{8,12},{9,13},{10,... | collective-permute-start | bytes 393224 | tf_op jit(solution)/shard_map/ppermute | solution.py:243
  13.8 2.9 %shard_map.89 = (f32[384,512]{1,0:T(8,128)S(1)}, bf16[384,512]{1,0:T(8,128)(2,1)S(1)}, bf16[384,512]{1,0:T(8,128)(2,1)S(1)}, bf16[384,512]{1,0:T(8,128)(2,1)S(1)}, bf16[384,512]{1,0:T(8,128)(2,1)S(1)}) custom-call(s32[2]{0:T(128)S(1)} %get-tuple-element.94.refs_0_.refs_1_.where.refs_5_, s32[2]{0:T(128)S(1)} %get-tuple-element.96.refs_2_.refs_3_.refs_1_.where.refs_0_.refs_4_, ...), custom_call_target="tpu_custom_call" | custom-call | flops 2000000000 | bytes 4194304 | tf_op jit(solution)/shard_map/pallas_call | solution.py:230
  16.7 1.2 %collective-permute-done.3 = bf16[512,128]{1,0:T(8,128)(2,1)S(1)} collective-permute-done((bf16[512,128]{1,0:T(8,128)(2,1)S(1)}, bf16[512,128]{1,0:T(8,128)(2,1)S(1)}, u32[]{:S(2)}, u32[]{:S(2)}) %collective-permute-start.3) | collective-permute-done | bytes 131104 | tf_op jit(solution)/shard_map/ppermute | solution.py:243
  18.0 2.7 %collective-permute-start.4 = (bf16[512,128]{1,0:T(8,128)(2,1)S(1)}, bf16[512,128]{1,0:T(8,128)(2,1)S(1)}, u32[]{:S(2)}, u32[]{:S(2)}) collective-permute-start(bf16[512,128]{1,0:T(8,128)(2,1)S(1)} %fusion.13), channel_id=1, source_target_pairs={{0,8},{1,9},{2,10},{3,11},{4,12},{5,13},{6,14},{7,15},{8,0},{9,1},... | collective-permute-start | bytes 393224 | tf_op jit(solution)/shard_map/ppermute | solution.py:243
  20.6 1.0 %shard_map.90.mixed_ref = f32[384,512]{1,0:T(8,128)S(1)} custom-call(bf16[384,512]{1,0:T(8,128)(2,1)S(1)} %get-tuple-element.127.refs_0_.query_ref, bf16[384,512]{1,0:T(8,128)(2,1)S(1)} %get-tuple-element.128.refs_0_.refs_1_.refs_3_, bf16[384,512]{1,0:T(8,128)(2,1)S(1)} %get-tuple-element.129.refs_1_.refs_2_.refs_4_), custom_call_target="tpu_custom_call" | custom-call | flops 2000000000 | bytes 4194304 | tf_op jit(solution)/shard_map/pallas_call | solution.py:230
  21.7 1.0 %shard_map.91.mixed_ref = f32[384,512]{1,0:T(8,128)S(1)} custom-call(bf16[384,512]{1,0:T(8,128)(2,1)S(1)} %get-tuple-element.130.refs_0_.query_ref, bf16[384,512]{1,0:T(8,128)(2,1)S(1)} %get-tuple-element.131.refs_1_.refs_3_, bf16[384,512]{1,0:T(8,128)(2,1)S(1)} %get-tuple-element.132.refs_2_.refs_4_), custom_call_target="tpu_custom_call" | custom-call | flops 2000000000 | bytes 4194304 | tf_op jit(solution)/shard_map/pallas_call | solution.py:230
  22.7 4.2 %collective-permute-done.4 = bf16[512,128]{1,0:T(8,128)(2,1)S(1)} collective-permute-done((bf16[512,128]{1,0:T(8,128)(2,1)S(1)}, bf16[512,128]{1,0:T(8,128)(2,1)S(1)}, u32[]{:S(2)}, u32[]{:S(2)}) %collective-permute-start.4) | collective-permute-done | bytes 131104 | tf_op jit(solution)/shard_map/ppermute | solution.py:243
  26.8 0.2 fusion.9
  27.0 0.1 collective-permute-start.6
  27.1 0.1 collective-permute-start.5
  27.2 1.5 %shard_map.93 = (bf16[384,512]{1,0:T(8,128)(2,1)S(1)}, bf16[528,128]{1,0:T(8,128)(2,1)S(1)}) custom-call(s32[2]{0:T(128)S(1)} %get-tuple-element.95.refs_6_.refs_7_.refs_3_.where.refs_2_, bf16[384,512]{1,0:T(8,128)(2,1)S(1)} %get-tuple-element.115.refs_0_.query_ref, bf16[384,512]{1,0:T(8,128)(2,1)S(1)} %get-tuple-element.138.cotan_ref, ...), custom_call_target="tpu_custom_call" | custom-call | flops 2000000000 | bytes 4194304 | tf_op jit(solution)/shard_map/pallas_call | solution.py:230
  28.7 0.5 collective-permute-start.7
  29.2 1.6 %shard_map.92 = (bf16[384,512]{1,0:T(8,128)(2,1)S(1)}, f32[528,128]{1,0:T(8,128)S(1)}) custom-call(s32[2]{0:T(128)S(1)} %get-tuple-element.97.refs_4_.refs_5_.refs_2_.where.refs_0_.refs_1_.refs_3_, bf16[384,512]{1,0:T(8,128)(2,1)S(1)} %get-tuple-element.117.refs_4_.query_ref.refs_0_, bf16[384,512]{1,0:T(8,128)(2,1)S(1)} %get-tuple-element.135.cotan_ref, ...), custom_call_target="tpu_custom_call" | custom-call | flops 2000000000 | bytes 4194304 | tf_op jit(solution)/shard_map/pallas_call | solution.py:230
  30.8 1.8 %collective-permute-start.10 = (bf16[528,128]{1,0:T(8,128)(2,1)S(1)}, bf16[528,128]{1,0:T(8,128)(2,1)S(1)}, u32[]{:S(2)}, u32[]{:S(2)}) collective-permute-start(bf16[528,128]{1,0:T(8,128)(2,1)S(1)} %add_convert_fusion.4), channel_id=1, source_target_pairs={{0,2},{1,3},{2,0},{3,1},{4,6},{5,7},{6,4},{7,5},{8,10},{9,11},{10,... | collective-permute-start | bytes 405512 | tf_op jit(solution)/shard_map/ppermute | solution.py:243
  32.6 0.4 collective-permute-done.5
  33.0 0.1 fusion.15
  33.1 0.1 collective-permute-start.8
  33.2 1.5 %shard_map.95 = (bf16[384,512]{1,0:T(8,128)(2,1)S(1)}, bf16[528,128]{1,0:T(8,128)(2,1)S(1)}) custom-call(s32[2]{0:T(128)S(1)} %get-tuple-element.96.refs_2_.refs_3_.refs_1_.where.refs_0_.refs_4_, bf16[384,512]{1,0:T(8,128)(2,1)S(1)} %get-tuple-element.127.refs_0_.query_ref, bf16[384,512]{1,0:T(8,128)(2,1)S(1)} %get-tuple-element.143.cotan_ref, ...), custom_call_target="tpu_custom_call" | custom-call | flops 2000000000 | bytes 4194304 | tf_op jit(solution)/shard_map/pallas_call | solution.py:230
  34.7 0.6 collective-permute-start.9
  35.2 1.6 %shard_map.94 = (bf16[384,512]{1,0:T(8,128)(2,1)S(1)}, f32[528,128]{1,0:T(8,128)S(1)}) custom-call(s32[2]{0:T(128)S(1)} %get-tuple-element.94.refs_0_.refs_1_.where.refs_5_, bf16[384,512]{1,0:T(8,128)(2,1)S(1)} %get-tuple-element.130.refs_0_.query_ref, bf16[384,512]{1,0:T(8,128)(2,1)S(1)} %get-tuple-element.120.cotan_ref, f32[1,2048]{1,0:T(1,128)S(1)} %bitcast.9, ...), custom_call_target="tpu_custom_call" | custom-call | flops 2000000000 | bytes 4194304 | tf_op jit(solution)/shard_map/pallas_call | solution.py:230
  36.9 0.5 collective-permute-start.11
  37.4 2.9 %shard_map.96 = (f32[384,512]{1,0:T(8,128)S(1)}, f32[384,512]{1,0:T(8,128)S(1)}, bf16[384,512]{1,0:T(8,128)(2,1)S(1)}) custom-call(bf16[384,512]{1,0:T(8,128)(2,1)S(1)} %get-tuple-element.130.refs_0_.query_ref, bf16[384,512]{1,0:T(8,128)(2,1)S(1)} %get-tuple-element.131.refs_1_.refs_3_, bf16[384,512]{1,0:T(8,128)(2,1)S(1)} %get-tuple-element.132.refs_2_.refs_4_, ...), custom_call_target="tpu_custom_call" | custom-call | flops 2000000000 | bytes 4194304 | tf_op jit(solution)/shard_map/pallas_call | solution.py:230
  40.3 2.2 %collective-permute-done.11 = bf16[528,128]{1,0:T(8,128)(2,1)S(1)} collective-permute-done((bf16[528,128]{1,0:T(8,128)(2,1)S(1)}, bf16[528,128]{1,0:T(8,128)(2,1)S(1)}, u32[]{:S(2)}, u32[]{:S(2)}) %collective-permute-start.11) | collective-permute-done | bytes 135200 | tf_op jit(solution)/shard_map/ppermute | solution.py:243
  42.5 2.2 %collective-permute-start.12 = (bf16[528,128]{1,0:T(8,128)(2,1)S(1)}, bf16[528,128]{1,0:T(8,128)(2,1)S(1)}, u32[]{:S(2)}, u32[]{:S(2)}) collective-permute-start(bf16[528,128]{1,0:T(8,128)(2,1)S(1)} %fusion.3), channel_id=1, source_target_pairs={{0,8},{1,9},{2,10},{3,11},{4,12},{5,13},{6,14},{7,15},{8,0},{9,1},... | collective-permute-start | bytes 405512 | tf_op jit(solution)/shard_map/ppermute | solution.py:243
  44.7 2.7 %shard_map.97 = (f32[384,512]{1,0:T(8,128)S(1)}, f32[384,512]{1,0:T(8,128)S(1)}, bf16[384,512]{1,0:T(8,128)(2,1)S(1)}) custom-call(bf16[384,512]{1,0:T(8,128)(2,1)S(1)} %get-tuple-element.127.refs_0_.query_ref, bf16[384,512]{1,0:T(8,128)(2,1)S(1)} %get-tuple-element.128.refs_0_.refs_1_.refs_3_, ...), custom_call_target="tpu_custom_call" | custom-call | flops 2000000000 | bytes 4194304 | tf_op jit(solution)/shard_map/pallas_call | solution.py:230
  47.4 2.7 %shard_map.98 = (f32[384,512]{1,0:T(8,128)S(1)}, f32[384,512]{1,0:T(8,128)S(1)}, bf16[384,512]{1,0:T(8,128)(2,1)S(1)}) custom-call(bf16[384,512]{1,0:T(8,128)(2,1)S(1)} %get-tuple-element.117.refs_4_.query_ref.refs_0_, bf16[384,512]{1,0:T(8,128)(2,1)S(1)} %get-tuple-element.118.refs_0_.refs_5_.refs_1_.refs_2_, ...), custom_call_target="tpu_custom_call" | custom-call | flops 2000000000 | bytes 4194304 | tf_op jit(solution)/shard_map/pallas_call | solution.py:230
  50.1 0.9 %collective-permute-done.12 = bf16[528,128]{1,0:T(8,128)(2,1)S(1)} collective-permute-done((bf16[528,128]{1,0:T(8,128)(2,1)S(1)}, bf16[528,128]{1,0:T(8,128)(2,1)S(1)}, u32[]{:S(2)}, u32[]{:S(2)}) %collective-permute-start.12) | collective-permute-done | bytes 135200 | tf_op jit(solution)/shard_map/ppermute | solution.py:243
  51.0 0.3 add_convert_fusion
  51.3 0.1 collective-permute-start.13
  51.4 0.4 collective-permute-start.14
  51.9 2.0 %shard_map.99 = (bf16[384,512]{1,0:T(8,128)(2,1)S(1)}, bf16[384,512]{1,0:T(8,128)(2,1)S(1)}, bf16[384,2048]{1,0:T(8,128)(2,1)}) custom-call(s32[2]{0:T(128)S(1)} %get-tuple-element.94.refs_0_.refs_1_.where.refs_5_, s32[2]{0:T(128)S(1)} %get-tuple-element.96.refs_2_.refs_3_.refs_1_.where.refs_0_.refs_4_, ...), custom_call_target="tpu_custom_call" | custom-call | flops 300000000 | bytes 4194304 | tf_op jit(solution)/shard_map/pallas_call | solution.py:230
  53.8 2.7 %shard_map.100 = (f32[384,512]{1,0:T(8,128)S(1)}, f32[384,512]{1,0:T(8,128)S(1)}, bf16[384,512]{1,0:T(8,128)(2,1)S(1)}) custom-call(bf16[384,512]{1,0:T(8,128)(2,1)S(1)} %get-tuple-element.115.refs_0_.query_ref, bf16[384,512]{1,0:T(8,128)(2,1)S(1)} %get-tuple-element.110.refs_4_.refs_1_.refs_6_, ...), custom_call_target="tpu_custom_call" | custom-call | flops 300000000 | bytes 4194304 | tf_op jit(solution)/shard_map/pallas_call | solution.py:230
  56.5 2.0 %shard_map.101 = (bf16[384,512]{1,0:T(8,128)(2,1)S(1)}, bf16[384,512]{1,0:T(8,128)(2,1)S(1)}, bf16[384,2048]{1,0:T(8,128)(2,1)}, bf16[384,2048]{1,0:T(8,128)(2,1)}, bf16[384,2048]{1,0:T(8,128)(2,1)}) custom-call(s32[2]{0:T(128)S(1)} %get-tuple-element.94.refs_0_.refs_1_.where.refs_5_, ...), custom_call_target="tpu_custom_call", output_to_operand_aliasing={{4}: (11, {})} | custom-call | flops 300000000 | bytes 4194304 | tf_op jit(solution)/shard_map/pallas_call | solution.py:230
  58.5 0.2 fusion.6
  58.7 0.2 collective-permute-start.15
  59.0 1.8 %shard_map.102 = (bf16[384,512]{1,0:T(8,128)(2,1)S(1)}, bf16[384,512]{1,0:T(8,128)(2,1)S(1)}, bf16[384,2048]{1,0:T(8,128)(2,1)}, bf16[384,2048]{1,0:T(8,128)(2,1)}) custom-call(s32[2]{0:T(128)S(1)} %get-tuple-element.96.refs_2_.refs_3_.refs_1_.where.refs_0_.refs_4_, ...), custom_call_target="tpu_custom_call", output_to_operand_aliasing={{2}: (9, {}), {3}: (10, {})} | custom-call | flops 300000000 | bytes 4194304 | tf_op jit(solution)/shard_map/pallas_call | solution.py:230
  60.7 2.5 %shard_map.103 = (f32[1,2048]{1,0:T(1,128)}, bf16[384,2048]{1,0:T(8,128)(2,1)}, bf16[384,2048]{1,0:T(8,128)(2,1)}) custom-call(s32[2]{0:T(128)S(1)} %get-tuple-element.97.refs_4_.refs_5_.refs_2_.where.refs_0_.refs_1_.refs_3_, ...), custom_call_target="tpu_custom_call", output_to_operand_aliasing={{1}: (16, {}), {2}: (17, {})} | custom-call | flops 2000000000 | bytes 4194304 | tf_op jit(solution)/shard_map/pallas_call | solution.py:230
  (20 shorter events, 0.3 us)
Async XLA Ops:
  3.6 1.5 %collective-permute-start = (bf16[512,128]{1,0:T(8,128)(2,1)S(1)}, bf16[512,128]{1,0:T(8,128)(2,1)S(1)}, u32[]{:S(2)}, u32[]{:S(2)}) collective-permute-start(bf16[512,128]{1,0:T(8,128)(2,1)S(1)} %get-tuple-element.105), channel_id=1, source_target_pairs={{0,1},{1,0},{2,3},{3,2},{4,5},{5,4},{6,7},{7,6},{8,9},{9,8},{10,11... | collective-permute-start | bytes 393224 | tf_op jit(solution)/shard_map/ppermute | solution.py:243
  5.1 6.8 %collective-permute-start.2 = (bf16[512,128]{1,0:T(8,128)(2,1)S(1)}, bf16[512,128]{1,0:T(8,128)(2,1)S(1)}, u32[]{:S(2)}, u32[]{:S(2)}) collective-permute-start(bf16[512,128]{1,0:T(8,128)(2,1)S(1)} %fusion.7), channel_id=1, source_target_pairs={{0,2},{1,3},{2,0},{3,1},{4,6},{5,7},{6,4},{7,5},{8,10},{9,11},{10,... | collective-permute-start | bytes 393224 | tf_op jit(solution)/shard_map/ppermute | solution.py:243
  8.5 3.4 %collective-permute-start.1 = (bf16[512,128]{1,0:T(8,128)(2,1)S(1)}, bf16[512,128]{1,0:T(8,128)(2,1)S(1)}, u32[]{:S(2)}, u32[]{:S(2)}) collective-permute-start(bf16[512,128]{1,0:T(8,128)(2,1)S(1)} %shard_map.86), channel_id=1, source_target_pairs={{0,1},{1,0},{2,3},{3,2},{4,5},{5,4},{6,7},{7,6},{8,9},{9,8},{10,11... | collective-permute-start | bytes 393224 | tf_op jit(solution)/shard_map/ppermute | solution.py:243
  12.0 6.0 %collective-permute-start.3 = (bf16[512,128]{1,0:T(8,128)(2,1)S(1)}, bf16[512,128]{1,0:T(8,128)(2,1)S(1)}, u32[]{:S(2)}, u32[]{:S(2)}) collective-permute-start(bf16[512,128]{1,0:T(8,128)(2,1)S(1)} %fusion.10), channel_id=1, source_target_pairs={{0,4},{1,5},{2,6},{3,7},{4,0},{5,1},{6,2},{7,3},{8,12},{9,13},{10,... | collective-permute-start | bytes 393224 | tf_op jit(solution)/shard_map/ppermute | solution.py:243
  18.0 8.9 %collective-permute-start.4 = (bf16[512,128]{1,0:T(8,128)(2,1)S(1)}, bf16[512,128]{1,0:T(8,128)(2,1)S(1)}, u32[]{:S(2)}, u32[]{:S(2)}) collective-permute-start(bf16[512,128]{1,0:T(8,128)(2,1)S(1)} %fusion.13), channel_id=1, source_target_pairs={{0,8},{1,9},{2,10},{3,11},{4,12},{5,13},{6,14},{7,15},{8,0},{9,1},... | collective-permute-start | bytes 393224 | tf_op jit(solution)/shard_map/ppermute | solution.py:243
  21.6 5.5 %copy-start = (f32[2048]{0:T(1024)S(1)}, f32[2048]{0:T(1024)}, u32[]{:S(2)}) copy-start(f32[2048]{0:T(1024)} %param.9) | copy-start | bytes 24580
  27.0 2.2 %collective-permute-start.6 = (bf16[512,128]{1,0:T(8,128)(2,1)S(1)}, bf16[512,128]{1,0:T(8,128)(2,1)S(1)}, u32[]{:S(2)}, u32[]{:S(2)}) collective-permute-start(bf16[512,128]{1,0:T(8,128)(2,1)S(1)} %get-tuple-element.188), channel_id=1, source_target_pairs={{0,1},{1,0},{2,3},{3,2},{4,5},{5,4},{6,7},{7,6},{8,9},{9,8},{10,11... | collective-permute-start | bytes 393224 | tf_op jit(solution)/shard_map/ppermute | solution.py:243
  27.1 5.9 %collective-permute-start.5 = (bf16[512,128]{1,0:T(8,128)(2,1)S(1)}, bf16[512,128]{1,0:T(8,128)(2,1)S(1)}, u32[]{:S(2)}, u32[]{:S(2)}) collective-permute-start(bf16[512,128]{1,0:T(8,128)(2,1)S(1)} %get-tuple-element.189), channel_id=1, source_target_pairs={{0,2},{1,3},{2,0},{3,1},{4,6},{5,7},{6,4},{7,5},{8,10},{9,11},{10,... | collective-permute-start | bytes 393224 | tf_op jit(solution)/shard_map/ppermute | solution.py:243
  28.7 2.0 %collective-permute-start.7 = (bf16[528,128]{1,0:T(8,128)(2,1)S(1)}, bf16[528,128]{1,0:T(8,128)(2,1)S(1)}, u32[]{:S(2)}, u32[]{:S(2)}) collective-permute-start(bf16[528,128]{1,0:T(8,128)(2,1)S(1)} %get-tuple-element.139), channel_id=1, source_target_pairs={{0,1},{1,0},{2,3},{3,2},{4,5},{5,4},{6,7},{7,6},{8,9},{9,8},{10,11... | collective-permute-start | bytes 405512 | tf_op jit(solution)/shard_map/ppermute | solution.py:243
  30.8 6.0 %collective-permute-start.10 = (bf16[528,128]{1,0:T(8,128)(2,1)S(1)}, bf16[528,128]{1,0:T(8,128)(2,1)S(1)}, u32[]{:S(2)}, u32[]{:S(2)}) collective-permute-start(bf16[528,128]{1,0:T(8,128)(2,1)S(1)} %add_convert_fusion.4), channel_id=1, source_target_pairs={{0,2},{1,3},{2,0},{3,1},{4,6},{5,7},{6,4},{7,5},{8,10},{9,11},{10,... | collective-permute-start | bytes 405512 | tf_op jit(solution)/shard_map/ppermute | solution.py:243
  33.1 2.1 %collective-permute-start.8 = (bf16[512,128]{1,0:T(8,128)(2,1)S(1)}, bf16[512,128]{1,0:T(8,128)(2,1)S(1)}, u32[]{:S(2)}, u32[]{:S(2)}) collective-permute-start(bf16[512,128]{1,0:T(8,128)(2,1)S(1)} %get-tuple-element.193), channel_id=1, source_target_pairs={{0,1},{1,0},{2,3},{3,2},{4,5},{5,4},{6,7},{7,6},{8,9},{9,8},{10,11... | collective-permute-start | bytes 393224 | tf_op jit(solution)/shard_map/ppermute | solution.py:243
  34.7 2.1 %collective-permute-start.9 = (bf16[528,128]{1,0:T(8,128)(2,1)S(1)}, bf16[528,128]{1,0:T(8,128)(2,1)S(1)}, u32[]{:S(2)}, u32[]{:S(2)}) collective-permute-start(bf16[528,128]{1,0:T(8,128)(2,1)S(1)} %get-tuple-element.144), channel_id=1, source_target_pairs={{0,1},{1,0},{2,3},{3,2},{4,5},{5,4},{6,7},{7,6},{8,9},{9,8},{10,11... | collective-permute-start | bytes 405512 | tf_op jit(solution)/shard_map/ppermute | solution.py:243
  36.9 5.6 %collective-permute-start.11 = (bf16[528,128]{1,0:T(8,128)(2,1)S(1)}, bf16[528,128]{1,0:T(8,128)(2,1)S(1)}, u32[]{:S(2)}, u32[]{:S(2)}) collective-permute-start(bf16[528,128]{1,0:T(8,128)(2,1)S(1)} %add_convert_fusion.3), channel_id=1, source_target_pairs={{0,4},{1,5},{2,6},{3,7},{4,0},{5,1},{6,2},{7,3},{8,12},{9,13},{10,... | collective-permute-start | bytes 405512 | tf_op jit(solution)/shard_map/ppermute | solution.py:243
  42.5 8.5 %collective-permute-start.12 = (bf16[528,128]{1,0:T(8,128)(2,1)S(1)}, bf16[528,128]{1,0:T(8,128)(2,1)S(1)}, u32[]{:S(2)}, u32[]{:S(2)}) collective-permute-start(bf16[528,128]{1,0:T(8,128)(2,1)S(1)} %fusion.3), channel_id=1, source_target_pairs={{0,8},{1,9},{2,10},{3,11},{4,12},{5,13},{6,14},{7,15},{8,0},{9,1},... | collective-permute-start | bytes 405512 | tf_op jit(solution)/shard_map/ppermute | solution.py:243
  51.3 5.2 %collective-permute-start.13 = (bf16[528,128]{1,0:T(8,128)(2,1)S(1)}, bf16[528,128]{1,0:T(8,128)(2,1)S(1)}, u32[]{:S(2)}, u32[]{:S(2)}) collective-permute-start(bf16[528,128]{1,0:T(8,128)(2,1)S(1)} %get-tuple-element.185), channel_id=1, source_target_pairs={{0,1},{1,0},{2,3},{3,2},{4,5},{5,4},{6,7},{7,6},{8,9},{9,8},{10,11... | collective-permute-start | bytes 405512 | tf_op jit(solution)/shard_map/ppermute | solution.py:243
  51.4 7.1 %collective-permute-start.14 = (bf16[528,128]{1,0:T(8,128)(2,1)S(1)}, bf16[528,128]{1,0:T(8,128)(2,1)S(1)}, u32[]{:S(2)}, u32[]{:S(2)}) collective-permute-start(bf16[528,128]{1,0:T(8,128)(2,1)S(1)} %get-tuple-element.184), channel_id=1, source_target_pairs={{0,2},{1,3},{2,0},{3,1},{4,6},{5,7},{6,4},{7,5},{8,10},{9,11},{10,... | collective-permute-start | bytes 405512 | tf_op jit(solution)/shard_map/ppermute | solution.py:243
  58.7 2.0 %collective-permute-start.15 = (bf16[528,128]{1,0:T(8,128)(2,1)S(1)}, bf16[528,128]{1,0:T(8,128)(2,1)S(1)}, u32[]{:S(2)}, u32[]{:S(2)}) collective-permute-start(bf16[528,128]{1,0:T(8,128)(2,1)S(1)} %get-tuple-element.191), channel_id=1, source_target_pairs={{0,1},{1,0},{2,3},{3,2},{4,5},{5,4},{6,7},{7,6},{8,9},{9,8},{10,11... | collective-permute-start | bytes 405512 | tf_op jit(solution)/shard_map/ppermute | solution.py:243

commit v5 on v4

--- a/solution.py
+++ b/solution.py
@@ -48,6 +48,15 @@
     return slice(head * HEAD, (head + 1) * HEAD)
 
 
+class Quarter:
+    def __init__(self, index_ref, which):
+        self.index_ref, self.which = index_ref, which
+
+    def __getitem__(self, axis):
+        bit = (self.index_ref[0] >> axis) & 1
+        return 1 - bit if self.which[axis] else bit
+
+
 def span(where):
     return pl.ds(pl.multiple_of((2 * where[0] + where[1]) * SPAN, SPAN), SPAN)
 
@@ -71,20 +80,6 @@
     return strips
 
 
-def upper(rows, depth, length):
-    keep = lax.broadcasted_iota(jnp.int32, (TILE, TILE), 0) <= lax.broadcasted_iota(
-        jnp.int32, (TILE, TILE), 1
-    )
-    strips = []
-    for start in range(0, length, TILE):
-        strip = mm_nt(rows[start : start + TILE], depth[start:])
-        first = jnp.where(keep, strip[:, :TILE], 0.0).astype(bf16)
-        if start + TILE < length:
-            first = jnp.concatenate([first, strip[:, TILE:].astype(bf16)], axis=1)
-        strips.append(first)
-    return strips
-
-
 def finish(copies):
     for copy in copies:
         copy.wait()
@@ -118,8 +113,8 @@
 
 
 def moving_kernel(body, counts, first, *refs):
-    loads, store_to, body_ins, body_outs, wholes, scratch, named = counts
-    stores = len(store_to)
+    load_at, store_at, store_to, body_ins, body_outs, wholes, scratch, named = counts
+    loads, stores = len(load_at), len(store_to)
     refs = list(refs)
 
     def take(number):
@@ -127,7 +122,9 @@
         del refs[:number]
         return taken
 
-    load_at, store_at = take(loads), take(stores)
+    (index_ref,) = take(1)
+    load_at = [Quarter(index_ref, which) for which in load_at]
+    store_at = [Quarter(index_ref, which) for which in store_at]
     ins, sources, ready = take(body_ins), take(loads), take(stores)
     take(wholes)
     outs, targets, results = take(body_outs), take(loads), take(named)
@@ -148,7 +145,8 @@
         finish(copy)
 
 
-def norm_kernel(where, query_ref, cotan_ref, gain_ref, state_ref, mixed_ref, grad_ref, own_ref):
+def norm_kernel(which, index_ref, query_ref, cotan_ref, gain_ref, state_ref, mixed_ref, grad_ref, own_ref):
+    where = Quarter(index_ref, which)
     own_ref[SPAN:, :] = jnp.zeros_like(own_ref[SPAN:, :])
     for head in range(QUARTER):
         query_map = feature(query_ref[:, own(head)].astype(f32))
@@ -175,16 +173,18 @@
         grad = grad_ref[:, own(head)]
         far = mm_nt(grad, state_ref[own(head), :])
         slope = decay(query)
-        for i, strip in enumerate(lower(grad, value, length)):
+        inside = lower(grad, value, length)
+        for i, strip in enumerate(inside):
             rows = slice(i * TILE, (i + 1) * TILE)
             near = mm(strip, key_map[: (i + 1) * TILE])
             dq_ref[rows, own(head)] = ((near + far[rows]) * slope[rows]).astype(bf16)
-        for i, strip in enumerate(upper(value, grad, length)):
-            rows = slice(i * TILE, (i + 1) * TILE)
-            dk_ref[rows, own(head)] = mm(strip, query_map[i * TILE :])
-        for i, strip in enumerate(upper(key_map, query_map, length)):
-            rows = slice(i * TILE, (i + 1) * TILE)
-            dv_ref[rows, own(head)] = mm(strip, grad[i * TILE :])
+        weights = lower(query_map, key_map, length)
+        for i in range(len(inside)):
+            rows, below = slice(i * TILE, (i + 1) * TILE), slice(i * TILE, length)
+            column = jnp.concatenate([strip[:, rows] for strip in inside[i:]], axis=0)
+            dk_ref[rows, own(head)] = mm_tn(column, query_map[below])
+            column = jnp.concatenate([strip[:, rows] for strip in weights[i:]], axis=0)
+            dv_ref[rows, own(head)] = mm_tn(column, grad[below])
 
 
 def last_head(head, key_ref, value_ref, back_ref, dk_ref, dv_ref, key_grad_ref, value_grad_ref):
@@ -203,8 +203,11 @@
         )
 
 
+LAST_ORDER = ((0, 0), (1, 0), (0, 1), (1, 1))
+
+
 def very_last(*refs):
-    wheres, refs = refs[:4], refs[4:]
+    wheres, refs = [Quarter(refs[0], which) for which in LAST_ORDER], refs[1:]
     key_ref, value_ref, dk_ref, dv_ref, *backs = refs[:8]
     gain_ref, key_hbm, value_hbm, key_grad_ref, value_grad_ref, sems = refs[8:]
     for where, back_ref in zip(wheres, backs, strict=True):
@@ -330,14 +333,11 @@
     index = lax.axis_index("seq").astype(jnp.int32)
     core, chip, four = index % 2, index // 2 % 2, index // 4
     gain = norm_gain.reshape(1, width)
-    where = {
-        (a, b): jnp.stack([1 - core if a else core, 1 - chip if b else chip])
-        for a in (0, 1)
-        for b in (0, 1)
-    }
     levels = range((shards // 4 - 1).bit_length())
     bits = [four // (1 << level) % 2 == 1 for level in levels]
-    where, odd_core, odd_chip, bits = after((where, core == 1, chip == 1, bits))
+    place_in_seq, odd_core, odd_chip, bits = after(
+        (index.reshape(1), core == 1, chip == 1, bits)
+    )
     state_low = ((SPAN, HEAD), bf16, VMEM)
     state_wide = ((SPAN, HEAD), f32, VMEM)
     sums_low = ((SPAN + EXTRA, HEAD), bf16, VMEM)
@@ -355,11 +355,19 @@
         names = list(dict.fromkeys(name for _, _, name in put))
         old = [(name, results[name]) for name in names if name in results]
         store_to = tuple(names.index(name) for _, _, name in put)
-        counts = (len(fetch), store_to, len(ins), len(outs), len(old), len(scratch), len(names))
+        counts = (
+            tuple(which for _, which in fetch),
+            tuple(which for which, _, _ in put),
+            store_to,
+            len(ins),
+            len(outs),
+            len(old),
+            len(scratch),
+            len(names),
+        )
         result = call(
             functools.partial(moving_kernel, body, counts, first),
-            [(where[which], SMEM) for _, which in fetch]
-            + [(where[which], SMEM) for which, _, _ in put]
+            [(place_in_seq, SMEM)]
             + ins
             + [(wholes[name], HBM) for name, _ in fetch]
             + held(*[a for _, a, _ in put]),
@@ -394,10 +402,8 @@
     fore.late(mine, got)
 
     mixed = {}
-    (mixed[0, 0],) = loading(inner, tiles("qkv", (0, 0)), [wide])
-    fore.near = after(fore.near, mixed[0, 0])
     done = fore.open()
-    plan = {0: [(1, 0)], 1: [(0, 1), (1, 1)]}
+    plan = {0: [(1, 0)], 1: [(0, 0), (0, 1), (1, 1)]}
     fetched = {(1, 0): [("c", w) for w in every]}
     for level in levels:
         moved = fore.exchange(level)
@@ -414,8 +420,8 @@
     def norm(which, state, kind, *done):
         query, cotan = tiles("qc", which)
         (cotan,) = after([cotan], *done) if done else [cotan]
-        ins = [(where[which], SMEM)] + held(query, cotan, gain, state, mixed[which])
-        return call(norm_kernel, ins, [low, kind])
+        ins = [(place_in_seq, SMEM)] + held(query, cotan, gain, state, mixed[which])
+        return call(functools.partial(norm_kernel, which), ins, [low, kind])
 
     seen[0, 0], seen[1, 0] = fore.late_state()
     grads[0, 0], sent = norm((0, 0), seen[0, 0], sums_low)
@@ -440,7 +446,7 @@
         return inner_grads[which][0]
 
     done = aft.open()
-    plan = {0: [(1, 1)], 1: [(0, 1), (1, 0)]}
+    plan = {0: [(1, 1), (0, 1)], 1: [(1, 0), (0, 0)]}
     for level in levels:
         moved = aft.exchange(level)
         for which in plan.get(level, []):
@@ -462,17 +468,15 @@
     backs = {}
     backs[1, 1], backs[0, 1] = aft.late_state()
     done = last_of((1, 1), backs[1, 1])
-    done = back_of((0, 0), done, LIGHT)
     inner_grads[0, 1][0] = after(inner_grads[0, 1][0], done)
     done = last_of((0, 1), backs[0, 1])
     aft.back = after(aft.back, done)
     backs[1, 0], backs[0, 0] = aft.early_state()
     last_of((1, 0), backs[1, 0])
-    order = ((0, 0), (1, 0), (0, 1), (1, 1))
     (gain_grad,) = moving(
         very_last,
-        [(where[which], SMEM) for which in order]
-        + held(*tiles("kv", (0, 0)), *inner_grads[0, 0], *[backs[which] for which in order]),
+        [(place_in_seq, SMEM)]
+        + held(*tiles("kv", (0, 0)), *inner_grads[0, 0], *[backs[w] for w in LAST_ORDER]),
         [row],
         put=list(ready),
         scratch=[pltpu.VMEM((length, SPAN), bf16)] * 2 + [sems(2, QUARTER)],

time: 63.6 us -> 59.7 us (0.939)
  Pallas kernels: 37 us -> 30 us
  starting transfers between devices: 14.5 us -> 16.5 us
  waiting for transfers between devices: 9.43 us -> 10.8 us
    pallas_call x20, Pallas kernels: 37 us -> 30 us  [call(): pl.pallas_call(kernel, out_shape=[jax.ShapeDtypeStruct(shape, dtype) for...]
    ppermute x16, starting transfers between devices: 14.5 us -> 16.5 us  [permute(): return lax.ppermute(value, 'seq', pairs)]
    ppermute x16, waiting for transfers between devices: 9.43 us -> 10.8 us  [permute(): return lax.ppermute(value, 'seq', pairs)]
  transfers between devices with their start and end apart: 16 -> 16, of which waited for: 6 -> 9; matrix products, arithmetic and copies ran while one was open for 0% -> 0% of each run, Pallas kernels for 50% -> 43%
where the time goes in v5:
time: 59.7 us; the launch traced here: 59.5 us
  Pallas kernels  30 us (50%)
  starting transfers between devices  16.5 us (28%)
  waiting for transfers between devices  10.8 us (18%)
  between operations  1.17 us (2%)
  other arithmetic  1.01 us (2%)
    pallas_call x20, Pallas kernels, call(): pl.pallas_call(kernel, out_shape=[jax.ShapeDtypeStruct(shape, dtype) for...  30 us
    ppermute x16, starting transfers between devices, permute(): return lax.ppermute(value, 'seq', pairs)  16.5 us
    ppermute x16, waiting for transfers between devices, permute(): return lax.ppermute(value, 'seq', pairs)  10.8 us
  transfers between devices with their start and end apart: 16, of which 9 were waited for; matrix products, arithmetic and copies ran while one was open for 0% of the time, Pallas kernels for 43%

profile of v5, /device:TPU:0, one launch (start us, length us, event | category | flops | bytes accessed | tf_op | source)
XLA Modules:
  0.0 59.5 jit_solution(5134416790769487025)
XLA Ops:
  0.7 2.1 %shard_map.84 = (bf16[512,128]{1,0:T(8,128)(2,1)S(1)}, bf16[384,512]{1,0:T(8,128)(2,1)S(1)}, bf16[384,512]{1,0:T(8,128)(2,1)S(1)}, bf16[384,512]{1,0:T(8,128)(2,...) custom-call(s32[1]{0:T(128)} %bitcast.refs_0_.index_ref.refs_1_, ...), custom_call_target="tpu_custom_call" | custom-call | flops 2000000000 | bytes 4194304 | tf_op jit(solution)/shard_map/pallas_call | solution.py:233
  2.8 0.5 collective-permute-start
  3.4 0.4 shard_map.85
  3.8 0.6 collective-permute-done
  4.4 2.9 %collective-permute-start.2 = (bf16[512,128]{1,0:T(8,128)(2,1)S(1)}, bf16[512,128]{1,0:T(8,128)(2,1)S(1)}, u32[]{:S(2)}, u32[]{:S(2)}) collective-permute-start(bf16[512,128]{1,0:T(8,128)(2,1)S(1)} %fusion.7), channel_id=1, source_target_pairs={{0,2},{1,3},{2,0},{3,1},{4,6},{5,7},{6,4},{7,5},{8,10},{9,11},{10,... | collective-permute-start | bytes 393224 | tf_op jit(solution)/shard_map/ppermute | solution.py:246
  7.3 0.4 shard_map.86
  7.7 0.1 collective-permute-start.1
  7.8 1.7 %shard_map.87 = (f32[512,128]{1,0:T(8,128)S(1)}, bf16[384,512]{1,0:T(8,128)(2,1)S(1)}, bf16[384,512]{1,0:T(8,128)(2,1)S(1)}, bf16[384,512]{1,0:T(8,128)(2,1)S(1)}, bf16[384,512]{1,0:T(8,128)(2,1)S(1)}) custom-call(s32[1]{0:T(128)} %bitcast.refs_0_.index_ref.refs_1_, bf16[384,512]{1,0:T(8,128)(2,1)S(1)} %get-tuple-element.122.refs_1_.refs_2_, ...), custom_call_target="tpu_custom_call" | custom-call | flops 2000000000 | bytes 4194304 | tf_op jit(solution)/shard_map/pallas_call | solution.py:233
  9.5 1.6 %collective-permute-done.2 = bf16[512,128]{1,0:T(8,128)(2,1)S(1)} collective-permute-done((bf16[512,128]{1,0:T(8,128)(2,1)S(1)}, bf16[512,128]{1,0:T(8,128)(2,1)S(1)}, u32[]{:S(2)}, u32[]{:S(2)}) %collective-permute-start.2) | collective-permute-done | bytes 131104 | tf_op jit(solution)/shard_map/ppermute | solution.py:246
  11.2 1.9 %collective-permute-start.3 = (bf16[512,128]{1,0:T(8,128)(2,1)S(1)}, bf16[512,128]{1,0:T(8,128)(2,1)S(1)}, u32[]{:S(2)}, u32[]{:S(2)}) collective-permute-start(bf16[512,128]{1,0:T(8,128)(2,1)S(1)} %fusion.10), channel_id=1, source_target_pairs={{0,4},{1,5},{2,6},{3,7},{4,0},{5,1},{6,2},{7,3},{8,12},{9,13},{10,... | collective-permute-start | bytes 393224 | tf_op jit(solution)/shard_map/ppermute | solution.py:246
  13.1 2.4 %shard_map.88 = (f32[384,512]{1,0:T(8,128)S(1)}, bf16[384,512]{1,0:T(8,128)(2,1)S(1)}, bf16[384,512]{1,0:T(8,128)(2,1)S(1)}, bf16[384,512]{1,0:T(8,128)(2,1)S(1)}, bf16[384,512]{1,0:T(8,128)(2,1)S(1)}) custom-call(s32[1]{0:T(128)} %bitcast.refs_0_.index_ref.refs_1_, bf16[384,512]{1,0:T(8,128)(2,1)S(1)} %get-tuple-element.112.refs_1_.query_ref, ...), custom_call_target="tpu_custom_call" | custom-call | flops 2000000000 | bytes 4194304 | tf_op jit(solution)/shard_map/pallas_call | solution.py:233
  15.4 0.9 %collective-permute-done.3 = bf16[512,128]{1,0:T(8,128)(2,1)S(1)} collective-permute-done((bf16[512,128]{1,0:T(8,128)(2,1)S(1)}, bf16[512,128]{1,0:T(8,128)(2,1)S(1)}, u32[]{:S(2)}, u32[]{:S(2)}) %collective-permute-start.3) | collective-permute-done | bytes 131104 | tf_op jit(solution)/shard_map/ppermute | solution.py:246
  16.3 2.8 %collective-permute-start.4 = (bf16[512,128]{1,0:T(8,128)(2,1)S(1)}, bf16[512,128]{1,0:T(8,128)(2,1)S(1)}, u32[]{:S(2)}, u32[]{:S(2)}) collective-permute-start(bf16[512,128]{1,0:T(8,128)(2,1)S(1)} %fusion.13), channel_id=1, source_target_pairs={{0,8},{1,9},{2,10},{3,11},{4,12},{5,13},{6,14},{7,15},{8,0},{9,1},... | collective-permute-start | bytes 393224 | tf_op jit(solution)/shard_map/ppermute | solution.py:246
  19.1 1.0 %shard_map.89.mixed_ref = f32[384,512]{1,0:T(8,128)S(1)} custom-call(s32[1]{0:T(128)} %bitcast.refs_0_.index_ref.refs_1_, bf16[384,512]{1,0:T(8,128)(2,1)S(1)} %get-tuple-element.121.refs_1_.query_ref, bf16[384,512]{1,0:T(8,128)(2,1)S(1)} %get-tuple-element.122.refs_1_.refs_2_, bf16[384,512]{1,0:T(8,128)(2,1)S(1)} %get-tuple-element.123.refs_2_.refs_3_), custom_call_target="tpu_custom_call" | custom-call | flops 2000000000 | bytes 4194304 | tf_op jit(solution)/shard_map/pallas_call | solution.py:233
  20.2 1.0 %shard_map.90.mixed_ref = f32[384,512]{1,0:T(8,128)S(1)} custom-call(s32[1]{0:T(128)} %bitcast.refs_0_.index_ref.refs_1_, bf16[384,512]{1,0:T(8,128)(2,1)S(1)} %get-tuple-element.124.refs_1_.query_ref, bf16[384,512]{1,0:T(8,128)(2,1)S(1)} %get-tuple-element.125.refs_1_.refs_2_, bf16[384,512]{1,0:T(8,128)(2,1)S(1)} %get-tuple-element.126.refs_2_.refs_3_), custom_call_target="tpu_custom_call" | custom-call | flops 2000000000 | bytes 4194304 | tf_op jit(solution)/shard_map/pallas_call | solution.py:233
  21.2 1.0 %shard_map.91.mixed_ref = f32[384,512]{1,0:T(8,128)S(1)} custom-call(s32[1]{0:T(128)} %bitcast.refs_0_.index_ref.refs_1_, bf16[384,512]{1,0:T(8,128)(2,1)S(1)} %get-tuple-element.127.refs_1_.query_ref, bf16[384,512]{1,0:T(8,128)(2,1)S(1)} %get-tuple-element.128.refs_2_.refs_1_, bf16[384,512]{1,0:T(8,128)(2,1)S(1)} %get-tuple-element.129.refs_3_.refs_2_), custom_call_target="tpu_custom_call" | custom-call | flops 2000000000 | bytes 4194304 | tf_op jit(solution)/shard_map/pallas_call | solution.py:233
  22.2 2.0 %collective-permute-done.4 = bf16[512,128]{1,0:T(8,128)(2,1)S(1)} collective-permute-done((bf16[512,128]{1,0:T(8,128)(2,1)S(1)}, bf16[512,128]{1,0:T(8,128)(2,1)S(1)}, u32[]{:S(2)}, u32[]{:S(2)}) %collective-permute-start.4) | collective-permute-done | bytes 131104 | tf_op jit(solution)/shard_map/ppermute | solution.py:246
  24.2 0.2 add_convert_fusion.6
  24.4 1.2 %collective-permute-start.5 = (bf16[512,128]{1,0:T(8,128)(2,1)S(1)}, bf16[512,128]{1,0:T(8,128)(2,1)S(1)}, u32[]{:S(2)}, u32[]{:S(2)}) collective-permute-start(bf16[512,128]{1,0:T(8,128)(2,1)S(1)} %get-tuple-element.183), channel_id=1, source_target_pairs={{0,2},{1,3},{2,0},{3,1},{4,6},{5,7},{6,4},{7,5},{8,10},{9,11},{10,... | collective-permute-start | bytes 393224 | tf_op jit(solution)/shard_map/ppermute | solution.py:246
  25.6 1.0 %shard_map.93 = (bf16[384,512]{1,0:T(8,128)(2,1)S(1)}, bf16[528,128]{1,0:T(8,128)(2,1)S(1)}) custom-call(s32[1]{0:T(128)} %bitcast.refs_0_.index_ref.refs_1_, bf16[384,512]{1,0:T(8,128)(2,1)S(1)} %get-tuple-element.121.refs_1_.query_ref, bf16[384,512]{1,0:T(8,128)(2,1)S(1)} %get-tuple-element.135.cotan_ref, f32[1,2048]{1,0:T(1,128)S(1)} %bitcast.3, ...), custom_call_target="tpu_custom_call" | custom-call | flops 2000000000 | bytes 4194304 | tf_op jit(solution)/shard_map/pallas_call | solution.py:233
  26.5 0.6 collective-permute-start.7
  27.1 1.0 %shard_map.92 = (bf16[384,512]{1,0:T(8,128)(2,1)S(1)}, f32[528,128]{1,0:T(8,128)S(1)}) custom-call(s32[1]{0:T(128)} %bitcast.refs_0_.index_ref.refs_1_, bf16[384,512]{1,0:T(8,128)(2,1)S(1)} %get-tuple-element.112.refs_1_.query_ref, bf16[384,512]{1,0:T(8,128)(2,1)S(1)} %get-tuple-element.132.cotan_ref, f32[1,2048]{1,0:T(1,128)S(1)} %bitcast.4, ...), custom_call_target="tpu_custom_call" | custom-call | flops 2000000000 | bytes 4194304 | tf_op jit(solution)/shard_map/pallas_call | solution.py:233
  28.2 1.0 %collective-permute-start.10 = (bf16[528,128]{1,0:T(8,128)(2,1)S(1)}, bf16[528,128]{1,0:T(8,128)(2,1)S(1)}, u32[]{:S(2)}, u32[]{:S(2)}) collective-permute-start(bf16[528,128]{1,0:T(8,128)(2,1)S(1)} %add_convert_fusion.4), channel_id=1, source_target_pairs={{0,2},{1,3},{2,0},{3,1},{4,6},{5,7},{6,4},{7,5},{8,10},{9,11},{10,... | collective-permute-start | bytes 405512 | tf_op jit(solution)/shard_map/ppermute | solution.py:246
  29.2 0.2 collective-permute-done.5
  29.4 0.1 fusion.14
  29.5 0.1 collective-permute-start.8
  29.6 0.9 %shard_map.95 = (bf16[384,512]{1,0:T(8,128)(2,1)S(1)}, bf16[528,128]{1,0:T(8,128)(2,1)S(1)}) custom-call(s32[1]{0:T(128)} %bitcast.refs_0_.index_ref.refs_1_, bf16[384,512]{1,0:T(8,128)(2,1)S(1)} %get-tuple-element.124.refs_1_.query_ref, bf16[384,512]{1,0:T(8,128)(2,1)S(1)} %get-tuple-element.140.cotan_ref, f32[1,2048]{1,0:T(1,128)S(1)} %bitcast.5, ...), custom_call_target="tpu_custom_call" | custom-call | flops 2000000000 | bytes 4194304 | tf_op jit(solution)/shard_map/pallas_call | solution.py:233
  30.6 0.6 collective-permute-start.9
  31.1 1.0 %shard_map.94 = (bf16[384,512]{1,0:T(8,128)(2,1)S(1)}, f32[528,128]{1,0:T(8,128)S(1)}) custom-call(s32[1]{0:T(128)} %bitcast.refs_0_.index_ref.refs_1_, bf16[384,512]{1,0:T(8,128)(2,1)S(1)} %get-tuple-element.127.refs_1_.query_ref, bf16[384,512]{1,0:T(8,128)(2,1)S(1)} %get-tuple-element.115.cotan_ref, f32[1,2048]{1,0:T(1,128)S(1)} %bitcast.6, ...), custom_call_target="tpu_custom_call" | custom-call | flops 2000000000 | bytes 4194304 | tf_op jit(solution)/shard_map/pallas_call | solution.py:233
  32.1 1.9 %collective-permute-done.10 = bf16[528,128]{1,0:T(8,128)(2,1)S(1)} collective-permute-done((bf16[528,128]{1,0:T(8,128)(2,1)S(1)}, bf16[528,128]{1,0:T(8,128)(2,1)S(1)}, u32[]{:S(2)}, u32[]{:S(2)}) %collective-permute-start.10) | collective-permute-done | bytes 135200 | tf_op jit(solution)/shard_map/ppermute | solution.py:246
  34.1 0.7 %collective-permute-start.11 = (bf16[528,128]{1,0:T(8,128)(2,1)S(1)}, bf16[528,128]{1,0:T(8,128)(2,1)S(1)}, u32[]{:S(2)}, u32[]{:S(2)}) collective-permute-start(bf16[528,128]{1,0:T(8,128)(2,1)S(1)} %add_convert_fusion.3), channel_id=1, source_target_pairs={{0,4},{1,5},{2,6},{3,7},{4,0},{5,1},{6,2},{7,3},{8,12},{9,13},{10,... | collective-permute-start | bytes 405512 | tf_op jit(solution)/shard_map/ppermute | solution.py:246
  34.9 2.4 %shard_map.96 = (f32[384,512]{1,0:T(8,128)S(1)}, f32[384,512]{1,0:T(8,128)S(1)}, bf16[384,512]{1,0:T(8,128)(2,1)S(1)}) custom-call(s32[1]{0:T(128)} %bitcast.refs_0_.index_ref.refs_1_, bf16[384,512]{1,0:T(8,128)(2,1)S(1)} %get-tuple-element.127.refs_1_.query_ref, bf16[384,512]{1,0:T(8,128)(2,1)S(1)} %get-tuple-element.128.refs_2_.refs_1_, ...), custom_call_target="tpu_custom_call" | custom-call | flops 2000000000 | bytes 4194304 | tf_op jit(solution)/shard_map/pallas_call | solution.py:233
  37.3 2.6 %shard_map.97 = (f32[384,512]{1,0:T(8,128)S(1)}, f32[384,512]{1,0:T(8,128)S(1)}, bf16[384,512]{1,0:T(8,128)(2,1)S(1)}) custom-call(s32[1]{0:T(128)} %bitcast.refs_0_.index_ref.refs_1_, bf16[384,512]{1,0:T(8,128)(2,1)S(1)} %get-tuple-element.124.refs_1_.query_ref, bf16[384,512]{1,0:T(8,128)(2,1)S(1)} %get-tuple-element.125.refs_1_.refs_2_, ...), custom_call_target="tpu_custom_call" | custom-call | flops 2000000000 | bytes 4194304 | tf_op jit(solution)/shard_map/pallas_call | solution.py:233
  40.0 3.5 %collective-permute-start.12 = (bf16[528,128]{1,0:T(8,128)(2,1)S(1)}, bf16[528,128]{1,0:T(8,128)(2,1)S(1)}, u32[]{:S(2)}, u32[]{:S(2)}) collective-permute-start(bf16[528,128]{1,0:T(8,128)(2,1)S(1)} %fusion.3), channel_id=1, source_target_pairs={{0,8},{1,9},{2,10},{3,11},{4,12},{5,13},{6,14},{7,15},{8,0},{9,1},... | collective-permute-start | bytes 405512 | tf_op jit(solution)/shard_map/ppermute | solution.py:246
  43.5 2.5 %shard_map.98 = (f32[384,512]{1,0:T(8,128)S(1)}, f32[384,512]{1,0:T(8,128)S(1)}, bf16[384,512]{1,0:T(8,128)(2,1)S(1)}) custom-call(s32[1]{0:T(128)} %bitcast.refs_0_.index_ref.refs_1_, bf16[384,512]{1,0:T(8,128)(2,1)S(1)} %get-tuple-element.112.refs_1_.query_ref, bf16[384,512]{1,0:T(8,128)(2,1)S(1)} %get-tuple-element.113.refs_1_.refs_2_, ...), custom_call_target="tpu_custom_call" | custom-call | flops 2000000000 | bytes 4194304 | tf_op jit(solution)/shard_map/pallas_call | solution.py:233
  45.9 2.5 %shard_map.99 = (f32[384,512]{1,0:T(8,128)S(1)}, f32[384,512]{1,0:T(8,128)S(1)}, bf16[384,512]{1,0:T(8,128)(2,1)S(1)}) custom-call(s32[1]{0:T(128)} %bitcast.refs_0_.index_ref.refs_1_, bf16[384,512]{1,0:T(8,128)(2,1)S(1)} %get-tuple-element.121.refs_1_.query_ref, bf16[384,512]{1,0:T(8,128)(2,1)S(1)} %get-tuple-element.122.refs_1_.refs_2_, ...), custom_call_target="tpu_custom_call" | custom-call | flops 2000000000 | bytes 4194304 | tf_op jit(solution)/shard_map/pallas_call | solution.py:233
  48.4 0.9 %collective-permute-done.12 = bf16[528,128]{1,0:T(8,128)(2,1)S(1)} collective-permute-done((bf16[528,128]{1,0:T(8,128)(2,1)S(1)}, bf16[528,128]{1,0:T(8,128)(2,1)S(1)}, u32[]{:S(2)}, u32[]{:S(2)}) %collective-permute-start.12) | collective-permute-done | bytes 135200 | tf_op jit(solution)/shard_map/ppermute | solution.py:246
  49.3 0.3 add_convert_fusion
  49.7 0.1 collective-permute-start.14
  49.7 0.6 %collective-permute-start.13 = (bf16[528,128]{1,0:T(8,128)(2,1)S(1)}, bf16[528,128]{1,0:T(8,128)(2,1)S(1)}, u32[]{:S(2)}, u32[]{:S(2)}) collective-permute-start(bf16[528,128]{1,0:T(8,128)(2,1)S(1)} %get-tuple-element.181), channel_id=1, source_target_pairs={{0,2},{1,3},{2,0},{3,1},{4,6},{5,7},{6,4},{7,5},{8,10},{9,11},{10,... | collective-permute-start | bytes 405512 | tf_op jit(solution)/shard_map/ppermute | solution.py:246
  50.4 1.5 %shard_map.100 = (bf16[384,512]{1,0:T(8,128)(2,1)S(1)}, bf16[384,512]{1,0:T(8,128)(2,1)S(1)}, bf16[384,2048]{1,0:T(8,128)(2,1)}) custom-call(s32[1]{0:T(128)} %bitcast.refs_0_.index_ref.refs_1_, bf16[384,512]{1,0:T(8,128)(2,1)S(1)} %get-tuple-element.128.refs_2_.refs_1_, bf16[384,512]{1,0:T(8,128)(2,1)S(1)} %get-tuple-element.129.refs_3_.refs_2_, ...), custom_call_target="tpu_custom_call" | custom-call | flops 300000000 | bytes 4194304 | tf_op jit(solution)/shard_map/pallas_call | solution.py:233
  51.9 1.2 %shard_map.101 = (bf16[384,512]{1,0:T(8,128)(2,1)S(1)}, bf16[384,512]{1,0:T(8,128)(2,1)S(1)}, bf16[384,2048]{1,0:T(8,128)(2,1)}, bf16[384,2048]{1,0:T(8,128)(2,1)}) custom-call(s32[1]{0:T(128)} %bitcast.refs_0_.index_ref.refs_1_, bf16[384,512]{1,0:T(8,128)(2,1)S(1)} %get-tuple-element.125.refs_1_.refs_2_, ...), custom_call_target="tpu_custom_call" | custom-call | flops 300000000 | bytes 4194304 | tf_op jit(solution)/shard_map/pallas_call | solution.py:233
  53.1 2.6 %collective-permute-done.13 = bf16[528,128]{1,0:T(8,128)(2,1)S(1)} collective-permute-done((bf16[528,128]{1,0:T(8,128)(2,1)S(1)}, bf16[528,128]{1,0:T(8,128)(2,1)S(1)}, u32[]{:S(2)}, u32[]{:S(2)}) %collective-permute-start.13) | collective-permute-done | bytes 135200 | tf_op jit(solution)/shard_map/ppermute | solution.py:246
  55.8 0.2 fusion.6
  55.9 0.1 collective-permute-start.15
  56.0 1.2 %shard_map.102 = (bf16[384,512]{1,0:T(8,128)(2,1)S(1)}, bf16[384,512]{1,0:T(8,128)(2,1)S(1)}, bf16[384,2048]{1,0:T(8,128)(2,1)}, bf16[384,2048]{1,0:T(8,128)(2,1)}) custom-call(s32[1]{0:T(128)} %bitcast.refs_0_.index_ref.refs_1_, bf16[384,512]{1,0:T(8,128)(2,1)S(1)} %get-tuple-element.113.refs_1_.refs_2_, ...), custom_call_target="tpu_custom_call", output_to_operand_aliasing={{2}: (8, {}), {3}: (9, {})} | custom-call | flops 300000000 | bytes 4194304 | tf_op jit(solution)/shard_map/pallas_call | solution.py:233
  57.3 0.1 collective-permute-done.15.refs_6_
  57.4 2.0 %shard_map.103 = (f32[1,2048]{1,0:T(1,128)}, bf16[384,2048]{1,0:T(8,128)(2,1)}, bf16[384,2048]{1,0:T(8,128)(2,1)}) custom-call(s32[1]{0:T(128)} %bitcast.refs_0_.index_ref.refs_1_, s32[1]{0:T(128)} %bitcast.refs_0_.index_ref.refs_1_, bf16[384,512]{1,0:T(8,128)(2,1)S(1)} %get-tuple-element.122.refs_1_.refs_2_, ...), custom_call_target="tpu_custom_call", output_to_operand_aliasing={{1}: (12, {}), {2}: (13, {})} | custom-call | flops 2000000000 | bytes 4194304 | tf_op jit(solution)/shard_map/pallas_call | solution.py:233
  (17 shorter events, 0.3 us)
Async XLA Ops:
  2.8 1.5 %collective-permute-start = (bf16[512,128]{1,0:T(8,128)(2,1)S(1)}, bf16[512,128]{1,0:T(8,128)(2,1)S(1)}, u32[]{:S(2)}, u32[]{:S(2)}) collective-permute-start(bf16[512,128]{1,0:T(8,128)(2,1)S(1)} %get-tuple-element.102), channel_id=1, source_target_pairs={{0,1},{1,0},{2,3},{3,2},{4,5},{5,4},{6,7},{7,6},{8,9},{9,8},{10,11... | collective-permute-start | bytes 393224 | tf_op jit(solution)/shard_map/ppermute | solution.py:246
  4.4 6.7 %collective-permute-start.2 = (bf16[512,128]{1,0:T(8,128)(2,1)S(1)}, bf16[512,128]{1,0:T(8,128)(2,1)S(1)}, u32[]{:S(2)}, u32[]{:S(2)}) collective-permute-start(bf16[512,128]{1,0:T(8,128)(2,1)S(1)} %fusion.7), channel_id=1, source_target_pairs={{0,2},{1,3},{2,0},{3,1},{4,6},{5,7},{6,4},{7,5},{8,10},{9,11},{10,... | collective-permute-start | bytes 393224 | tf_op jit(solution)/shard_map/ppermute | solution.py:246
  7.7 3.4 %collective-permute-start.1 = (bf16[512,128]{1,0:T(8,128)(2,1)S(1)}, bf16[512,128]{1,0:T(8,128)(2,1)S(1)}, u32[]{:S(2)}, u32[]{:S(2)}) collective-permute-start(bf16[512,128]{1,0:T(8,128)(2,1)S(1)} %shard_map.86), channel_id=1, source_target_pairs={{0,1},{1,0},{2,3},{3,2},{4,5},{5,4},{6,7},{7,6},{8,9},{9,8},{10,11... | collective-permute-start | bytes 393224 | tf_op jit(solution)/shard_map/ppermute | solution.py:246
  11.2 5.1 %collective-permute-start.3 = (bf16[512,128]{1,0:T(8,128)(2,1)S(1)}, bf16[512,128]{1,0:T(8,128)(2,1)S(1)}, u32[]{:S(2)}, u32[]{:S(2)}) collective-permute-start(bf16[512,128]{1,0:T(8,128)(2,1)S(1)} %fusion.10), channel_id=1, source_target_pairs={{0,4},{1,5},{2,6},{3,7},{4,0},{5,1},{6,2},{7,3},{8,12},{9,13},{10,... | collective-permute-start | bytes 393224 | tf_op jit(solution)/shard_map/ppermute | solution.py:246
  16.3 7.9 %collective-permute-start.4 = (bf16[512,128]{1,0:T(8,128)(2,1)S(1)}, bf16[512,128]{1,0:T(8,128)(2,1)S(1)}, u32[]{:S(2)}, u32[]{:S(2)}) collective-permute-start(bf16[512,128]{1,0:T(8,128)(2,1)S(1)} %fusion.13), channel_id=1, source_target_pairs={{0,8},{1,9},{2,10},{3,11},{4,12},{5,13},{6,14},{7,15},{8,0},{9,1},... | collective-permute-start | bytes 393224 | tf_op jit(solution)/shard_map/ppermute | solution.py:246
  21.2 4.4 %copy-start = (f32[2048]{0:T(1024)S(1)}, f32[2048]{0:T(1024)}, u32[]{:S(2)}) copy-start(f32[2048]{0:T(1024)} %param.9) | copy-start | bytes 24580
  24.4 5.0 %collective-permute-start.5 = (bf16[512,128]{1,0:T(8,128)(2,1)S(1)}, bf16[512,128]{1,0:T(8,128)(2,1)S(1)}, u32[]{:S(2)}, u32[]{:S(2)}) collective-permute-start(bf16[512,128]{1,0:T(8,128)(2,1)S(1)} %get-tuple-element.183), channel_id=1, source_target_pairs={{0,2},{1,3},{2,0},{3,1},{4,6},{5,7},{6,4},{7,5},{8,10},{9,11},{10,... | collective-permute-start | bytes 393224 | tf_op jit(solution)/shard_map/ppermute | solution.py:246
  25.6 1.6 %collective-permute-start.6 = (bf16[512,128]{1,0:T(8,128)(2,1)S(1)}, bf16[512,128]{1,0:T(8,128)(2,1)S(1)}, u32[]{:S(2)}, u32[]{:S(2)}) collective-permute-start(bf16[512,128]{1,0:T(8,128)(2,1)S(1)} %get-tuple-element.184), channel_id=1, source_target_pairs={{0,1},{1,0},{2,3},{3,2},{4,5},{5,4},{6,7},{7,6},{8,9},{9,8},{10,11... | collective-permute-start | bytes 393224 | tf_op jit(solution)/shard_map/ppermute | solution.py:246
  26.5 1.6 %collective-permute-start.7 = (bf16[528,128]{1,0:T(8,128)(2,1)S(1)}, bf16[528,128]{1,0:T(8,128)(2,1)S(1)}, u32[]{:S(2)}, u32[]{:S(2)}) collective-permute-start(bf16[528,128]{1,0:T(8,128)(2,1)S(1)} %get-tuple-element.136), channel_id=1, source_target_pairs={{0,1},{1,0},{2,3},{3,2},{4,5},{5,4},{6,7},{7,6},{8,9},{9,8},{10,11... | collective-permute-start | bytes 405512 | tf_op jit(solution)/shard_map/ppermute | solution.py:246
  28.2 5.9 %collective-permute-start.10 = (bf16[528,128]{1,0:T(8,128)(2,1)S(1)}, bf16[528,128]{1,0:T(8,128)(2,1)S(1)}, u32[]{:S(2)}, u32[]{:S(2)}) collective-permute-start(bf16[528,128]{1,0:T(8,128)(2,1)S(1)} %add_convert_fusion.4), channel_id=1, source_target_pairs={{0,2},{1,3},{2,0},{3,1},{4,6},{5,7},{6,4},{7,5},{8,10},{9,11},{10,... | collective-permute-start | bytes 405512 | tf_op jit(solution)/shard_map/ppermute | solution.py:246
  29.5 1.6 %collective-permute-start.8 = (bf16[512,128]{1,0:T(8,128)(2,1)S(1)}, bf16[512,128]{1,0:T(8,128)(2,1)S(1)}, u32[]{:S(2)}, u32[]{:S(2)}) collective-permute-start(bf16[512,128]{1,0:T(8,128)(2,1)S(1)} %get-tuple-element.188), channel_id=1, source_target_pairs={{0,1},{1,0},{2,3},{3,2},{4,5},{5,4},{6,7},{7,6},{8,9},{9,8},{10,11... | collective-permute-start | bytes 393224 | tf_op jit(solution)/shard_map/ppermute | solution.py:246
  30.6 3.5 %collective-permute-start.9 = (bf16[528,128]{1,0:T(8,128)(2,1)S(1)}, bf16[528,128]{1,0:T(8,128)(2,1)S(1)}, u32[]{:S(2)}, u32[]{:S(2)}) collective-permute-start(bf16[528,128]{1,0:T(8,128)(2,1)S(1)} %get-tuple-element.141), channel_id=1, source_target_pairs={{0,1},{1,0},{2,3},{3,2},{4,5},{5,4},{6,7},{7,6},{8,9},{9,8},{10,11... | collective-permute-start | bytes 405512 | tf_op jit(solution)/shard_map/ppermute | solution.py:246
  34.1 5.8 %collective-permute-start.11 = (bf16[528,128]{1,0:T(8,128)(2,1)S(1)}, bf16[528,128]{1,0:T(8,128)(2,1)S(1)}, u32[]{:S(2)}, u32[]{:S(2)}) collective-permute-start(bf16[528,128]{1,0:T(8,128)(2,1)S(1)} %add_convert_fusion.3), channel_id=1, source_target_pairs={{0,4},{1,5},{2,6},{3,7},{4,0},{5,1},{6,2},{7,3},{8,12},{9,13},{10,... | collective-permute-start | bytes 405512 | tf_op jit(solution)/shard_map/ppermute | solution.py:246
  40.0 9.3 %collective-permute-start.12 = (bf16[528,128]{1,0:T(8,128)(2,1)S(1)}, bf16[528,128]{1,0:T(8,128)(2,1)S(1)}, u32[]{:S(2)}, u32[]{:S(2)}) collective-permute-start(bf16[528,128]{1,0:T(8,128)(2,1)S(1)} %fusion.3), channel_id=1, source_target_pairs={{0,8},{1,9},{2,10},{3,11},{4,12},{5,13},{6,14},{7,15},{8,0},{9,1},... | collective-permute-start | bytes 405512 | tf_op jit(solution)/shard_map/ppermute | solution.py:246
  49.7 2.2 %collective-permute-start.14 = (bf16[528,128]{1,0:T(8,128)(2,1)S(1)}, bf16[528,128]{1,0:T(8,128)(2,1)S(1)}, u32[]{:S(2)}, u32[]{:S(2)}) collective-permute-start(bf16[528,128]{1,0:T(8,128)(2,1)S(1)} %get-tuple-element.180), channel_id=1, source_target_pairs={{0,1},{1,0},{2,3},{3,2},{4,5},{5,4},{6,7},{7,6},{8,9},{9,8},{10,11... | collective-permute-start | bytes 405512 | tf_op jit(solution)/shard_map/ppermute | solution.py:246
  49.7 6.0 %collective-permute-start.13 = (bf16[528,128]{1,0:T(8,128)(2,1)S(1)}, bf16[528,128]{1,0:T(8,128)(2,1)S(1)}, u32[]{:S(2)}, u32[]{:S(2)}) collective-permute-start(bf16[528,128]{1,0:T(8,128)(2,1)S(1)} %get-tuple-element.181), channel_id=1, source_target_pairs={{0,2},{1,3},{2,0},{3,1},{4,6},{5,7},{6,4},{7,5},{8,10},{9,11},{10,... | collective-permute-start | bytes 405512 | tf_op jit(solution)/shard_map/ppermute | solution.py:246
  55.9 1.4 %collective-permute-start.15 = (bf16[528,128]{1,0:T(8,128)(2,1)S(1)}, bf16[528,128]{1,0:T(8,128)(2,1)S(1)}, u32[]{:S(2)}, u32[]{:S(2)}) collective-permute-start(bf16[528,128]{1,0:T(8,128)(2,1)S(1)} %get-tuple-element.187), channel_id=1, source_target_pairs={{0,1},{1,0},{2,3},{3,2},{4,5},{5,4},{6,7},{7,6},{8,9},{9,8},{10,11... | collective-permute-start | bytes 405512 | tf_op jit(solution)/shard_map/ppermute | solution.py:246

commit v6 on v5

--- a/solution.py
+++ b/solution.py
@@ -210,10 +210,6 @@
     wheres, refs = [Quarter(refs[0], which) for which in LAST_ORDER], refs[1:]
     key_ref, value_ref, dk_ref, dv_ref, *backs = refs[:8]
     gain_ref, key_hbm, value_hbm, key_grad_ref, value_grad_ref, sems = refs[8:]
-    for where, back_ref in zip(wheres, backs, strict=True):
-        gains = back_ref[SPAN:, :].astype(f32)
-        for head in range(QUARTER):
-            gain_ref[:, place(where, head)] = gains[head : head + 1, :]
     copies = []
     for head in range(QUARTER):
         last_head(
@@ -226,6 +222,10 @@
                 )
             )
             copies[-1].start()
+    for where, back_ref in zip(wheres, backs, strict=True):
+        gains = back_ref[SPAN:, :].astype(f32)
+        for head in range(QUARTER):
+            gain_ref[:, place(where, head)] = gains[head : head + 1, :]
     finish(copies)
 
 
@@ -331,13 +331,10 @@
     length, width = queries.shape
     shards = lax.axis_size("seq")
     index = lax.axis_index("seq").astype(jnp.int32)
-    core, chip, four = index % 2, index // 2 % 2, index // 4
+    odd = [(index >> bit) & 1 == 1 for bit in range((shards - 1).bit_length())]
     gain = norm_gain.reshape(1, width)
     levels = range((shards // 4 - 1).bit_length())
-    bits = [four // (1 << level) % 2 == 1 for level in levels]
-    place_in_seq, odd_core, odd_chip, bits = after(
-        (index.reshape(1), core == 1, chip == 1, bits)
-    )
+    place_in_seq, (odd_core, odd_chip, *bits) = after((index.reshape(1), odd))
     state_low = ((SPAN, HEAD), bf16, VMEM)
     state_wide = ((SPAN, HEAD), f32, VMEM)
     sums_low = ((SPAN + EXTRA, HEAD), bf16, VMEM)
@@ -351,7 +348,9 @@
     wholes = {"q": queries, "k": key_vectors, "v": value_vectors, "c": out_cotangent}
     tile, results = {}, {}
 
-    def moving(body, ins, outs, fetch=(), first=0, put=(), scratch=(), flops=WORK):
+    def moving(
+        body, ins, outs, fetch=(), first=0, put=(), scratch=(), flops=WORK, wholes=wholes
+    ):
         names = list(dict.fromkeys(name for _, _, name in put))
         old = [(name, results[name]) for name in names if name in results]
         store_to = tuple(names.index(name) for _, _, name in put)
@@ -382,35 +381,37 @@
             results[name] = value
         return result[: len(outs)]
 
-    def loading(body, ins, outs, fetch=(), first=0):
-        return moving(body, held(*ins), outs, fetch, first)
+    def loading(body, ins, outs, fetch=(), first=0, wholes=wholes):
+        return moving(body, held(*ins), outs, fetch, first, wholes=wholes)
+
+    def fetch(names, quarters):
+        return [(name, which) for which in quarters for name in names]
 
     def tiles(names, which):
         return [tile[name, which] for name in names]
 
     every = [(1, 1), (0, 1), (1, 0), (0, 0)]
     fore = Scan(shards, False, odd_core, odd_chip, bits)
-    (sent,) = loading(state, [], [state_low], [(name, w) for w in every for name in "kv"], 2)
+    (sent,) = loading(state, [], [state_low], fetch("kv", every[:2]), 2)
     got = fore.swap_core(sent)
     (mine,) = loading(state, after(tiles("kv", (0, 1)), sent), [state_wide])
     send = fore.early(mine, got)
-    (sent,) = loading(state, after(tiles("kv", (1, 0)), send), [state_low])
+    late = after(wholes, send)
+    (sent,) = loading(state, [], [state_low], fetch("kv", every[2:]), 2, late)
     got = fore.swap_core(sent)
-    (mine,) = loading(
-        state, after(tiles("kv", (0, 0)), sent), [state_wide], [("q", w) for w in every]
-    )
+    (mine,) = loading(state, after(tiles("kv", (0, 0)), sent), [state_wide])
     fore.late(mine, got)
 
     mixed = {}
     done = fore.open()
     plan = {0: [(1, 0)], 1: [(0, 0), (0, 1), (1, 1)]}
-    fetched = {(1, 0): [("c", w) for w in every]}
+    fetched = {(1, 0): fetch("q", every[2:] + every[:2]), (0, 0): fetch("c", every)}
     for level in levels:
         moved = fore.exchange(level)
         for which in plan.get(level, []):
-            (done,) = loading(
-                inner, after(tiles("qkv", which), done), [wide], fetched.get(which, [])
-            )
+            first = 0 if ("q", which) in tile else 1
+            ins = after(tiles("qkv"[first:], which), done)
+            (done,) = loading(inner, ins, [wide], fetched.get(which, []), first)
             mixed[which] = done
         done = fore.absorb(level, after(moved, done))
 

time: 59.7 us -> 59.3 us (level)
  waiting for transfers between devices: 10.8 us -> 9.82 us
  Pallas kernels: 30 us -> 30.6 us
    ppermute x16, waiting for transfers between devices: 10.8 us -> 9.82 us  [permute(): return lax.ppermute(value, 'seq', pairs)]
    pallas_call x20, Pallas kernels: 30 us -> 30.6 us  [call(): pl.pallas_call(kernel, out_shape=[jax.ShapeDtypeStruct(shape, dtype) for...]
  transfers between devices with their start and end apart: 16 -> 16, of which waited for: 9 -> 9; matrix products, arithmetic and copies ran while one was open for 0% -> 0% of each run, Pallas kernels for 43% -> 46%
where the time goes in v6:
time: 59.3 us; the launch traced here: 59 us
  Pallas kernels  30.6 us (52%)
  starting transfers between devices  16.5 us (28%)
  waiting for transfers between devices  9.82 us (17%)
  between operations  1.08 us (2%)
  other arithmetic  1.01 us (2%)
    pallas_call x20, Pallas kernels, call(): pl.pallas_call(kernel, out_shape=[jax.ShapeDtypeStruct(shape, dtype) for...  30.6 us
    ppermute x16, starting transfers between devices, permute(): return lax.ppermute(value, 'seq', pairs)  16.5 us
    ppermute x16, waiting for transfers between devices, permute(): return lax.ppermute(value, 'seq', pairs)  9.82 us
  transfers between devices with their start and end apart: 16, of which 9 were waited for; matrix products, arithmetic and copies ran while one was open for 0% of the time, Pallas kernels for 46%

profile of v6, /device:TPU:0, one launch (start us, length us, event | category | flops | bytes accessed | tf_op | source)
XLA Modules:
  0.0 59.0 jit_solution(11768106305676460414)
XLA Ops:
  0.6 1.7 %shard_map.84 = (bf16[512,128]{1,0:T(8,128)(2,1)S(1)}, bf16[384,512]{1,0:T(8,128)(2,1)S(1)}, bf16[384,512]{1,0:T(8,128)(2,1)S(1)}, bf16[384,512]{1,0:T(8,128)(2,1)S(1)}, bf16[384,512]{1,0:T(8,128)(2,1)S(1)}) custom-call(s32[1]{0:T(128)} %bitcast.refs_0_.index_ref.refs_1_, bf16[384,2048]{1,0:T(8,128)(2,1)} %refs_3_.3, bf16[384,2048]{1,0:T(8,128)(2,1)} %refs_4_.4, ...), custom_call_target="tpu_custom_call" | custom-call | flops 2000000000 | bytes 4194304 | tf_op jit(solution)/shard_map/pallas_call | solution.py:233
  2.3 0.5 collective-permute-start
  2.9 0.4 shard_map.85
  3.3 0.6 collective-permute-done
  3.9 2.9 %collective-permute-start.2 = (bf16[512,128]{1,0:T(8,128)(2,1)S(1)}, bf16[512,128]{1,0:T(8,128)(2,1)S(1)}, u32[]{:S(2)}, u32[]{:S(2)}) collective-permute-start(bf16[512,128]{1,0:T(8,128)(2,1)S(1)} %fusion.7), channel_id=1, source_target_pairs={{0,2},{1,3},{2,0},{3,1},{4,6},{5,7},{6,4},{7,5},{8,10},{9,11},{10,... | collective-permute-start | bytes 393224 | tf_op jit(solution)/shard_map/ppermute | solution.py:246
  6.8 1.7 %shard_map.86 = (bf16[512,128]{1,0:T(8,128)(2,1)S(1)}, bf16[384,512]{1,0:T(8,128)(2,1)S(1)}, bf16[384,512]{1,0:T(8,128)(2,1)S(1)}, bf16[384,512]{1,0:T(8,128)(2,1)S(1)}, bf16[384,512]{1,0:T(8,128)(2,1)S(1)}) custom-call(s32[1]{0:T(128)} %bitcast.refs_0_.index_ref.refs_1_, bf16[384,2048]{1,0:T(8,128)(2,1)} %refs_3_.3, bf16[384,2048]{1,0:T(8,128)(2,1)} %refs_4_.4, ...), custom_call_target="tpu_custom_call" | custom-call | flops 2000000000 | bytes 4194304 | tf_op jit(solution)/shard_map/pallas_call | solution.py:233
  8.5 0.1 collective-permute-start.1
  8.6 0.4 shard_map.87
  9.0 1.6 %collective-permute-done.2 = bf16[512,128]{1,0:T(8,128)(2,1)S(1)} collective-permute-done((bf16[512,128]{1,0:T(8,128)(2,1)S(1)}, bf16[512,128]{1,0:T(8,128)(2,1)S(1)}, u32[]{:S(2)}, u32[]{:S(2)}) %collective-permute-start.2) | collective-permute-done | bytes 131104 | tf_op jit(solution)/shard_map/ppermute | solution.py:246
  10.7 1.9 %collective-permute-start.3 = (bf16[512,128]{1,0:T(8,128)(2,1)S(1)}, bf16[512,128]{1,0:T(8,128)(2,1)S(1)}, u32[]{:S(2)}, u32[]{:S(2)}) collective-permute-start(bf16[512,128]{1,0:T(8,128)(2,1)S(1)} %fusion.10), channel_id=1, source_target_pairs={{0,4},{1,5},{2,6},{3,7},{4,0},{5,1},{6,2},{7,3},{8,12},{9,13},{10,... | collective-permute-start | bytes 393224 | tf_op jit(solution)/shard_map/ppermute | solution.py:246
  12.6 2.1 %shard_map.88 = (f32[384,512]{1,0:T(8,128)S(1)}, bf16[384,512]{1,0:T(8,128)(2,1)S(1)}, bf16[384,512]{1,0:T(8,128)(2,1)S(1)}, bf16[384,512]{1,0:T(8,128)(2,1)S(1)}, bf16[384,512]{1,0:T(8,128)(2,1)S(1)}) custom-call(s32[1]{0:T(128)} %bitcast.refs_0_.index_ref.refs_1_, bf16[384,512]{1,0:T(8,128)(2,1)S(1)} %get-tuple-element.110.refs_1_.refs_2_, ...), custom_call_target="tpu_custom_call" | custom-call | flops 2000000000 | bytes 4194304 | tf_op jit(solution)/shard_map/pallas_call | solution.py:233
  14.7 1.1 %collective-permute-done.3 = bf16[512,128]{1,0:T(8,128)(2,1)S(1)} collective-permute-done((bf16[512,128]{1,0:T(8,128)(2,1)S(1)}, bf16[512,128]{1,0:T(8,128)(2,1)S(1)}, u32[]{:S(2)}, u32[]{:S(2)}) %collective-permute-start.3) | collective-permute-done | bytes 131104 | tf_op jit(solution)/shard_map/ppermute | solution.py:246
  15.8 2.8 %collective-permute-start.4 = (bf16[512,128]{1,0:T(8,128)(2,1)S(1)}, bf16[512,128]{1,0:T(8,128)(2,1)S(1)}, u32[]{:S(2)}, u32[]{:S(2)}) collective-permute-start(bf16[512,128]{1,0:T(8,128)(2,1)S(1)} %fusion.12), channel_id=1, source_target_pairs={{0,8},{1,9},{2,10},{3,11},{4,12},{5,13},{6,14},{7,15},{8,0},{9,1},... | collective-permute-start | bytes 393224 | tf_op jit(solution)/shard_map/ppermute | solution.py:246
  18.6 2.4 %shard_map.89 = (f32[384,512]{1,0:T(8,128)S(1)}, bf16[384,512]{1,0:T(8,128)(2,1)S(1)}, bf16[384,512]{1,0:T(8,128)(2,1)S(1)}, bf16[384,512]{1,0:T(8,128)(2,1)S(1)}, bf16[384,512]{1,0:T(8,128)(2,1)S(1)}) custom-call(s32[1]{0:T(128)} %bitcast.refs_0_.index_ref.refs_1_, bf16[384,512]{1,0:T(8,128)(2,1)S(1)} %get-tuple-element.116.refs_1_.query_ref, ...), custom_call_target="tpu_custom_call" | custom-call | flops 2000000000 | bytes 4194304 | tf_op jit(solution)/shard_map/pallas_call | solution.py:233
  21.0 1.0 %shard_map.90.mixed_ref = f32[384,512]{1,0:T(8,128)S(1)} custom-call(s32[1]{0:T(128)} %bitcast.refs_0_.index_ref.refs_1_, bf16[384,512]{1,0:T(8,128)(2,1)S(1)} %get-tuple-element.123.refs_1_.query_ref, bf16[384,512]{1,0:T(8,128)(2,1)S(1)} %get-tuple-element.124.refs_1_.refs_2_, bf16[384,512]{1,0:T(8,128)(2,1)S(1)} %get-tuple-element.125.refs_2_.refs_3_), custom_call_target="tpu_custom_call" | custom-call | flops 2000000000 | bytes 4194304 | tf_op jit(solution)/shard_map/pallas_call | solution.py:233
  22.0 1.0 %shard_map.91.mixed_ref = f32[384,512]{1,0:T(8,128)S(1)} custom-call(s32[1]{0:T(128)} %bitcast.refs_0_.index_ref.refs_1_, bf16[384,512]{1,0:T(8,128)(2,1)S(1)} %get-tuple-element.126.refs_1_.query_ref, bf16[384,512]{1,0:T(8,128)(2,1)S(1)} %get-tuple-element.127.refs_2_.refs_1_, bf16[384,512]{1,0:T(8,128)(2,1)S(1)} %get-tuple-element.128.refs_3_.refs_2_), custom_call_target="tpu_custom_call" | custom-call | flops 2000000000 | bytes 4194304 | tf_op jit(solution)/shard_map/pallas_call | solution.py:233
  23.1 0.7 %collective-permute-done.4 = bf16[512,128]{1,0:T(8,128)(2,1)S(1)} collective-permute-done((bf16[512,128]{1,0:T(8,128)(2,1)S(1)}, bf16[512,128]{1,0:T(8,128)(2,1)S(1)}, u32[]{:S(2)}, u32[]{:S(2)}) %collective-permute-start.4) | collective-permute-done | bytes 131104 | tf_op jit(solution)/shard_map/ppermute | solution.py:246
  23.7 0.2 add_convert_fusion.6
  23.9 1.2 %collective-permute-start.5 = (bf16[512,128]{1,0:T(8,128)(2,1)S(1)}, bf16[512,128]{1,0:T(8,128)(2,1)S(1)}, u32[]{:S(2)}, u32[]{:S(2)}) collective-permute-start(bf16[512,128]{1,0:T(8,128)(2,1)S(1)} %get-tuple-element.183), channel_id=1, source_target_pairs={{0,2},{1,3},{2,0},{3,1},{4,6},{5,7},{6,4},{7,5},{8,10},{9,11},{10,... | collective-permute-start | bytes 393224 | tf_op jit(solution)/shard_map/ppermute | solution.py:246
  25.1 1.0 %shard_map.93 = (bf16[384,512]{1,0:T(8,128)(2,1)S(1)}, bf16[528,128]{1,0:T(8,128)(2,1)S(1)}) custom-call(s32[1]{0:T(128)} %bitcast.refs_0_.index_ref.refs_1_, bf16[384,512]{1,0:T(8,128)(2,1)S(1)} %get-tuple-element.116.refs_1_.query_ref, bf16[384,512]{1,0:T(8,128)(2,1)S(1)} %get-tuple-element.135.cotan_ref, f32[1,2048]{1,0:T(1,128)S(1)} %bitcast.3, ...), custom_call_target="tpu_custom_call" | custom-call | flops 2000000000 | bytes 4194304 | tf_op jit(solution)/shard_map/pallas_call | solution.py:233
  26.0 0.6 collective-permute-start.7
  26.6 1.0 %shard_map.92 = (bf16[384,512]{1,0:T(8,128)(2,1)S(1)}, f32[528,128]{1,0:T(8,128)S(1)}) custom-call(s32[1]{0:T(128)} %bitcast.refs_0_.index_ref.refs_1_, bf16[384,512]{1,0:T(8,128)(2,1)S(1)} %get-tuple-element.131.query_ref.refs_1_, bf16[384,512]{1,0:T(8,128)(2,1)S(1)} %get-tuple-element.132.cotan_ref, f32[1,2048]{1,0:T(1,128)S(1)} %bitcast.4, ...), custom_call_target="tpu_custom_call" | custom-call | flops 2000000000 | bytes 4194304 | tf_op jit(solution)/shard_map/pallas_call | solution.py:233
  27.7 1.0 %collective-permute-start.10 = (bf16[528,128]{1,0:T(8,128)(2,1)S(1)}, bf16[528,128]{1,0:T(8,128)(2,1)S(1)}, u32[]{:S(2)}, u32[]{:S(2)}) collective-permute-start(bf16[528,128]{1,0:T(8,128)(2,1)S(1)} %add_convert_fusion.4), channel_id=1, source_target_pairs={{0,2},{1,3},{2,0},{3,1},{4,6},{5,7},{6,4},{7,5},{8,10},{9,11},{10,... | collective-permute-start | bytes 405512 | tf_op jit(solution)/shard_map/ppermute | solution.py:246
  28.7 0.2 collective-permute-done.5
  28.9 0.1 fusion.14
  29.0 0.1 collective-permute-start.8
  29.1 1.0 %shard_map.95 = (bf16[384,512]{1,0:T(8,128)(2,1)S(1)}, bf16[528,128]{1,0:T(8,128)(2,1)S(1)}) custom-call(s32[1]{0:T(128)} %bitcast.refs_0_.index_ref.refs_1_, bf16[384,512]{1,0:T(8,128)(2,1)S(1)} %get-tuple-element.123.refs_1_.query_ref, bf16[384,512]{1,0:T(8,128)(2,1)S(1)} %get-tuple-element.140.cotan_ref, f32[1,2048]{1,0:T(1,128)S(1)} %bitcast.5, ...), custom_call_target="tpu_custom_call" | custom-call | flops 2000000000 | bytes 4194304 | tf_op jit(solution)/shard_map/pallas_call | solution.py:233
  30.1 0.6 collective-permute-start.9
  30.6 1.0 %shard_map.94 = (bf16[384,512]{1,0:T(8,128)(2,1)S(1)}, f32[528,128]{1,0:T(8,128)S(1)}) custom-call(s32[1]{0:T(128)} %bitcast.refs_0_.index_ref.refs_1_, bf16[384,512]{1,0:T(8,128)(2,1)S(1)} %get-tuple-element.126.refs_1_.query_ref, bf16[384,512]{1,0:T(8,128)(2,1)S(1)} %get-tuple-element.119.cotan_ref, f32[1,2048]{1,0:T(1,128)S(1)} %bitcast.6, ...), custom_call_target="tpu_custom_call" | custom-call | flops 2000000000 | bytes 4194304 | tf_op jit(solution)/shard_map/pallas_call | solution.py:233
  31.6 1.9 %collective-permute-done.10 = bf16[528,128]{1,0:T(8,128)(2,1)S(1)} collective-permute-done((bf16[528,128]{1,0:T(8,128)(2,1)S(1)}, bf16[528,128]{1,0:T(8,128)(2,1)S(1)}, u32[]{:S(2)}, u32[]{:S(2)}) %collective-permute-start.10) | collective-permute-done | bytes 135200 | tf_op jit(solution)/shard_map/ppermute | solution.py:246
  33.6 1.4 %collective-permute-start.11 = (bf16[528,128]{1,0:T(8,128)(2,1)S(1)}, bf16[528,128]{1,0:T(8,128)(2,1)S(1)}, u32[]{:S(2)}, u32[]{:S(2)}) collective-permute-start(bf16[528,128]{1,0:T(8,128)(2,1)S(1)} %add_convert_fusion.3), channel_id=1, source_target_pairs={{0,4},{1,5},{2,6},{3,7},{4,0},{5,1},{6,2},{7,3},{8,12},{9,13},{10,... | collective-permute-start | bytes 405512 | tf_op jit(solution)/shard_map/ppermute | solution.py:246
  35.0 2.4 %shard_map.96 = (f32[384,512]{1,0:T(8,128)S(1)}, f32[384,512]{1,0:T(8,128)S(1)}, bf16[384,512]{1,0:T(8,128)(2,1)S(1)}) custom-call(s32[1]{0:T(128)} %bitcast.refs_0_.index_ref.refs_1_, bf16[384,512]{1,0:T(8,128)(2,1)S(1)} %get-tuple-element.126.refs_1_.query_ref, bf16[384,512]{1,0:T(8,128)(2,1)S(1)} %get-tuple-element.127.refs_2_.refs_1_, ...), custom_call_target="tpu_custom_call" | custom-call | flops 2000000000 | bytes 4194304 | tf_op jit(solution)/shard_map/pallas_call | solution.py:233
  37.5 2.6 %shard_map.97 = (f32[384,512]{1,0:T(8,128)S(1)}, f32[384,512]{1,0:T(8,128)S(1)}, bf16[384,512]{1,0:T(8,128)(2,1)S(1)}) custom-call(s32[1]{0:T(128)} %bitcast.refs_0_.index_ref.refs_1_, bf16[384,512]{1,0:T(8,128)(2,1)S(1)} %get-tuple-element.123.refs_1_.query_ref, bf16[384,512]{1,0:T(8,128)(2,1)S(1)} %get-tuple-element.124.refs_1_.refs_2_, ...), custom_call_target="tpu_custom_call" | custom-call | flops 2000000000 | bytes 4194304 | tf_op jit(solution)/shard_map/pallas_call | solution.py:233
  40.2 2.8 %collective-permute-start.12 = (bf16[528,128]{1,0:T(8,128)(2,1)S(1)}, bf16[528,128]{1,0:T(8,128)(2,1)S(1)}, u32[]{:S(2)}, u32[]{:S(2)}) collective-permute-start(bf16[528,128]{1,0:T(8,128)(2,1)S(1)} %fusion.3), channel_id=1, source_target_pairs={{0,8},{1,9},{2,10},{3,11},{4,12},{5,13},{6,14},{7,15},{8,0},{9,1},... | collective-permute-start | bytes 405512 | tf_op jit(solution)/shard_map/ppermute | solution.py:246
  43.0 2.5 %shard_map.98 = (f32[384,512]{1,0:T(8,128)S(1)}, f32[384,512]{1,0:T(8,128)S(1)}, bf16[384,512]{1,0:T(8,128)(2,1)S(1)}) custom-call(s32[1]{0:T(128)} %bitcast.refs_0_.index_ref.refs_1_, bf16[384,512]{1,0:T(8,128)(2,1)S(1)} %get-tuple-element.131.query_ref.refs_1_, bf16[384,512]{1,0:T(8,128)(2,1)S(1)} %get-tuple-element.110.refs_1_.refs_2_, ...), custom_call_target="tpu_custom_call" | custom-call | flops 2000000000 | bytes 4194304 | tf_op jit(solution)/shard_map/pallas_call | solution.py:233
  45.4 2.5 %shard_map.99 = (f32[384,512]{1,0:T(8,128)S(1)}, f32[384,512]{1,0:T(8,128)S(1)}, bf16[384,512]{1,0:T(8,128)(2,1)S(1)}) custom-call(s32[1]{0:T(128)} %bitcast.refs_0_.index_ref.refs_1_, bf16[384,512]{1,0:T(8,128)(2,1)S(1)} %get-tuple-element.116.refs_1_.query_ref, bf16[384,512]{1,0:T(8,128)(2,1)S(1)} %get-tuple-element.117.refs_1_.refs_2_, ...), custom_call_target="tpu_custom_call" | custom-call | flops 2000000000 | bytes 4194304 | tf_op jit(solution)/shard_map/pallas_call | solution.py:233
  47.9 0.9 %collective-permute-done.12 = bf16[528,128]{1,0:T(8,128)(2,1)S(1)} collective-permute-done((bf16[528,128]{1,0:T(8,128)(2,1)S(1)}, bf16[528,128]{1,0:T(8,128)(2,1)S(1)}, u32[]{:S(2)}, u32[]{:S(2)}) %collective-permute-start.12) | collective-permute-done | bytes 135200 | tf_op jit(solution)/shard_map/ppermute | solution.py:246
  48.8 0.3 add_convert_fusion
  49.2 0.1 collective-permute-start.14
  49.2 0.6 %collective-permute-start.13 = (bf16[528,128]{1,0:T(8,128)(2,1)S(1)}, bf16[528,128]{1,0:T(8,128)(2,1)S(1)}, u32[]{:S(2)}, u32[]{:S(2)}) collective-permute-start(bf16[528,128]{1,0:T(8,128)(2,1)S(1)} %get-tuple-element.181), channel_id=1, source_target_pairs={{0,2},{1,3},{2,0},{3,1},{4,6},{5,7},{6,4},{7,5},{8,10},{9,11},{10,... | collective-permute-start | bytes 405512 | tf_op jit(solution)/shard_map/ppermute | solution.py:246
  49.9 1.5 %shard_map.100 = (bf16[384,512]{1,0:T(8,128)(2,1)S(1)}, bf16[384,512]{1,0:T(8,128)(2,1)S(1)}, bf16[384,2048]{1,0:T(8,128)(2,1)}) custom-call(s32[1]{0:T(128)} %bitcast.refs_0_.index_ref.refs_1_, bf16[384,512]{1,0:T(8,128)(2,1)S(1)} %get-tuple-element.127.refs_2_.refs_1_, bf16[384,512]{1,0:T(8,128)(2,1)S(1)} %get-tuple-element.128.refs_3_.refs_2_, ...), custom_call_target="tpu_custom_call" | custom-call | flops 300000000 | bytes 4194304 | tf_op jit(solution)/shard_map/pallas_call | solution.py:233
  51.4 1.2 %shard_map.101 = (bf16[384,512]{1,0:T(8,128)(2,1)S(1)}, bf16[384,512]{1,0:T(8,128)(2,1)S(1)}, bf16[384,2048]{1,0:T(8,128)(2,1)}, bf16[384,2048]{1,0:T(8,128)(2,1)}) custom-call(s32[1]{0:T(128)} %bitcast.refs_0_.index_ref.refs_1_, bf16[384,512]{1,0:T(8,128)(2,1)S(1)} %get-tuple-element.124.refs_1_.refs_2_, ...), custom_call_target="tpu_custom_call" | custom-call | flops 300000000 | bytes 4194304 | tf_op jit(solution)/shard_map/pallas_call | solution.py:233
  52.6 2.6 %collective-permute-done.13 = bf16[528,128]{1,0:T(8,128)(2,1)S(1)} collective-permute-done((bf16[528,128]{1,0:T(8,128)(2,1)S(1)}, bf16[528,128]{1,0:T(8,128)(2,1)S(1)}, u32[]{:S(2)}, u32[]{:S(2)}) %collective-permute-start.13) | collective-permute-done | bytes 135200 | tf_op jit(solution)/shard_map/ppermute | solution.py:246
  55.2 0.2 fusion.6
  55.4 0.1 collective-permute-start.15
  55.5 1.2 %shard_map.102 = (bf16[384,512]{1,0:T(8,128)(2,1)S(1)}, bf16[384,512]{1,0:T(8,128)(2,1)S(1)}, bf16[384,2048]{1,0:T(8,128)(2,1)}, bf16[384,2048]{1,0:T(8,128)(2,1)}) custom-call(s32[1]{0:T(128)} %bitcast.refs_0_.index_ref.refs_1_, bf16[384,512]{1,0:T(8,128)(2,1)S(1)} %get-tuple-element.110.refs_1_.refs_2_, ...), custom_call_target="tpu_custom_call", output_to_operand_aliasing={{2}: (8, {}), {3}: (9, {})} | custom-call | flops 300000000 | bytes 4194304 | tf_op jit(solution)/shard_map/pallas_call | solution.py:233
  56.8 0.1 collective-permute-done.15.refs_6_
  56.9 2.0 %shard_map.103 = (f32[1,2048]{1,0:T(1,128)}, bf16[384,2048]{1,0:T(8,128)(2,1)}, bf16[384,2048]{1,0:T(8,128)(2,1)}) custom-call(s32[1]{0:T(128)} %bitcast.refs_0_.index_ref.refs_1_, s32[1]{0:T(128)} %bitcast.refs_0_.index_ref.refs_1_, bf16[384,512]{1,0:T(8,128)(2,1)S(1)} %get-tuple-element.117.refs_1_.refs_2_, ...), custom_call_target="tpu_custom_call", output_to_operand_aliasing={{1}: (12, {}), {2}: (13, {})} | custom-call | flops 2000000000 | bytes 4194304 | tf_op jit(solution)/shard_map/pallas_call | solution.py:233
  (17 shorter events, 0.3 us)
Async XLA Ops:
  2.3 1.5 %collective-permute-start = (bf16[512,128]{1,0:T(8,128)(2,1)S(1)}, bf16[512,128]{1,0:T(8,128)(2,1)S(1)}, u32[]{:S(2)}, u32[]{:S(2)}) collective-permute-start(bf16[512,128]{1,0:T(8,128)(2,1)S(1)} %get-tuple-element.98), channel_id=1, source_target_pairs={{0,1},{1,0},{2,3},{3,2},{4,5},{5,4},{6,7},{7,6},{8,9},{9,8},{10,11... | collective-permute-start | bytes 393224 | tf_op jit(solution)/shard_map/ppermute | solution.py:246
  3.9 6.7 %collective-permute-start.2 = (bf16[512,128]{1,0:T(8,128)(2,1)S(1)}, bf16[512,128]{1,0:T(8,128)(2,1)S(1)}, u32[]{:S(2)}, u32[]{:S(2)}) collective-permute-start(bf16[512,128]{1,0:T(8,128)(2,1)S(1)} %fusion.7), channel_id=1, source_target_pairs={{0,2},{1,3},{2,0},{3,1},{4,6},{5,7},{6,4},{7,5},{8,10},{9,11},{10,... | collective-permute-start | bytes 393224 | tf_op jit(solution)/shard_map/ppermute | solution.py:246
  8.5 2.1 %collective-permute-start.1 = (bf16[512,128]{1,0:T(8,128)(2,1)S(1)}, bf16[512,128]{1,0:T(8,128)(2,1)S(1)}, u32[]{:S(2)}, u32[]{:S(2)}) collective-permute-start(bf16[512,128]{1,0:T(8,128)(2,1)S(1)} %get-tuple-element.107), channel_id=1, source_target_pairs={{0,1},{1,0},{2,3},{3,2},{4,5},{5,4},{6,7},{7,6},{8,9},{9,8},{10,11... | collective-permute-start | bytes 393224 | tf_op jit(solution)/shard_map/ppermute | solution.py:246
  10.7 5.1 %collective-permute-start.3 = (bf16[512,128]{1,0:T(8,128)(2,1)S(1)}, bf16[512,128]{1,0:T(8,128)(2,1)S(1)}, u32[]{:S(2)}, u32[]{:S(2)}) collective-permute-start(bf16[512,128]{1,0:T(8,128)(2,1)S(1)} %fusion.10), channel_id=1, source_target_pairs={{0,4},{1,5},{2,6},{3,7},{4,0},{5,1},{6,2},{7,3},{8,12},{9,13},{10,... | collective-permute-start | bytes 393224 | tf_op jit(solution)/shard_map/ppermute | solution.py:246
  15.8 7.9 %collective-permute-start.4 = (bf16[512,128]{1,0:T(8,128)(2,1)S(1)}, bf16[512,128]{1,0:T(8,128)(2,1)S(1)}, u32[]{:S(2)}, u32[]{:S(2)}) collective-permute-start(bf16[512,128]{1,0:T(8,128)(2,1)S(1)} %fusion.12), channel_id=1, source_target_pairs={{0,8},{1,9},{2,10},{3,11},{4,12},{5,13},{6,14},{7,15},{8,0},{9,1},... | collective-permute-start | bytes 393224 | tf_op jit(solution)/shard_map/ppermute | solution.py:246
  22.0 3.0 %copy-start = (f32[2048]{0:T(1024)S(1)}, f32[2048]{0:T(1024)}, u32[]{:S(2)}) copy-start(f32[2048]{0:T(1024)} %param.9) | copy-start | bytes 24580
  23.9 5.0 %collective-permute-start.5 = (bf16[512,128]{1,0:T(8,128)(2,1)S(1)}, bf16[512,128]{1,0:T(8,128)(2,1)S(1)}, u32[]{:S(2)}, u32[]{:S(2)}) collective-permute-start(bf16[512,128]{1,0:T(8,128)(2,1)S(1)} %get-tuple-element.183), channel_id=1, source_target_pairs={{0,2},{1,3},{2,0},{3,1},{4,6},{5,7},{6,4},{7,5},{8,10},{9,11},{10,... | collective-permute-start | bytes 393224 | tf_op jit(solution)/shard_map/ppermute | solution.py:246
  25.1 1.6 %collective-permute-start.6 = (bf16[512,128]{1,0:T(8,128)(2,1)S(1)}, bf16[512,128]{1,0:T(8,128)(2,1)S(1)}, u32[]{:S(2)}, u32[]{:S(2)}) collective-permute-start(bf16[512,128]{1,0:T(8,128)(2,1)S(1)} %get-tuple-element.184), channel_id=1, source_target_pairs={{0,1},{1,0},{2,3},{3,2},{4,5},{5,4},{6,7},{7,6},{8,9},{9,8},{10,11... | collective-permute-start | bytes 393224 | tf_op jit(solution)/shard_map/ppermute | solution.py:246
  26.0 1.6 %collective-permute-start.7 = (bf16[528,128]{1,0:T(8,128)(2,1)S(1)}, bf16[528,128]{1,0:T(8,128)(2,1)S(1)}, u32[]{:S(2)}, u32[]{:S(2)}) collective-permute-start(bf16[528,128]{1,0:T(8,128)(2,1)S(1)} %get-tuple-element.136), channel_id=1, source_target_pairs={{0,1},{1,0},{2,3},{3,2},{4,5},{5,4},{6,7},{7,6},{8,9},{9,8},{10,11... | collective-permute-start | bytes 405512 | tf_op jit(solution)/shard_map/ppermute | solution.py:246
  27.7 5.9 %collective-permute-start.10 = (bf16[528,128]{1,0:T(8,128)(2,1)S(1)}, bf16[528,128]{1,0:T(8,128)(2,1)S(1)}, u32[]{:S(2)}, u32[]{:S(2)}) collective-permute-start(bf16[528,128]{1,0:T(8,128)(2,1)S(1)} %add_convert_fusion.4), channel_id=1, source_target_pairs={{0,2},{1,3},{2,0},{3,1},{4,6},{5,7},{6,4},{7,5},{8,10},{9,11},{10,... | collective-permute-start | bytes 405512 | tf_op jit(solution)/shard_map/ppermute | solution.py:246
  29.0 1.6 %collective-permute-start.8 = (bf16[512,128]{1,0:T(8,128)(2,1)S(1)}, bf16[512,128]{1,0:T(8,128)(2,1)S(1)}, u32[]{:S(2)}, u32[]{:S(2)}) collective-permute-start(bf16[512,128]{1,0:T(8,128)(2,1)S(1)} %get-tuple-element.188), channel_id=1, source_target_pairs={{0,1},{1,0},{2,3},{3,2},{4,5},{5,4},{6,7},{7,6},{8,9},{9,8},{10,11... | collective-permute-start | bytes 393224 | tf_op jit(solution)/shard_map/ppermute | solution.py:246
  30.1 3.5 %collective-permute-start.9 = (bf16[528,128]{1,0:T(8,128)(2,1)S(1)}, bf16[528,128]{1,0:T(8,128)(2,1)S(1)}, u32[]{:S(2)}, u32[]{:S(2)}) collective-permute-start(bf16[528,128]{1,0:T(8,128)(2,1)S(1)} %get-tuple-element.141), channel_id=1, source_target_pairs={{0,1},{1,0},{2,3},{3,2},{4,5},{5,4},{6,7},{7,6},{8,9},{9,8},{10,11... | collective-permute-start | bytes 405512 | tf_op jit(solution)/shard_map/ppermute | solution.py:246
  33.6 6.5 %collective-permute-start.11 = (bf16[528,128]{1,0:T(8,128)(2,1)S(1)}, bf16[528,128]{1,0:T(8,128)(2,1)S(1)}, u32[]{:S(2)}, u32[]{:S(2)}) collective-permute-start(bf16[528,128]{1,0:T(8,128)(2,1)S(1)} %add_convert_fusion.3), channel_id=1, source_target_pairs={{0,4},{1,5},{2,6},{3,7},{4,0},{5,1},{6,2},{7,3},{8,12},{9,13},{10,... | collective-permute-start | bytes 405512 | tf_op jit(solution)/shard_map/ppermute | solution.py:246
  40.2 8.7 %collective-permute-start.12 = (bf16[528,128]{1,0:T(8,128)(2,1)S(1)}, bf16[528,128]{1,0:T(8,128)(2,1)S(1)}, u32[]{:S(2)}, u32[]{:S(2)}) collective-permute-start(bf16[528,128]{1,0:T(8,128)(2,1)S(1)} %fusion.3), channel_id=1, source_target_pairs={{0,8},{1,9},{2,10},{3,11},{4,12},{5,13},{6,14},{7,15},{8,0},{9,1},... | collective-permute-start | bytes 405512 | tf_op jit(solution)/shard_map/ppermute | solution.py:246
  49.2 2.2 %collective-permute-start.14 = (bf16[528,128]{1,0:T(8,128)(2,1)S(1)}, bf16[528,128]{1,0:T(8,128)(2,1)S(1)}, u32[]{:S(2)}, u32[]{:S(2)}) collective-permute-start(bf16[528,128]{1,0:T(8,128)(2,1)S(1)} %get-tuple-element.180), channel_id=1, source_target_pairs={{0,1},{1,0},{2,3},{3,2},{4,5},{5,4},{6,7},{7,6},{8,9},{9,8},{10,11... | collective-permute-start | bytes 405512 | tf_op jit(solution)/shard_map/ppermute | solution.py:246
  49.2 6.0 %collective-permute-start.13 = (bf16[528,128]{1,0:T(8,128)(2,1)S(1)}, bf16[528,128]{1,0:T(8,128)(2,1)S(1)}, u32[]{:S(2)}, u32[]{:S(2)}) collective-permute-start(bf16[528,128]{1,0:T(8,128)(2,1)S(1)} %get-tuple-element.181), channel_id=1, source_target_pairs={{0,2},{1,3},{2,0},{3,1},{4,6},{5,7},{6,4},{7,5},{8,10},{9,11},{10,... | collective-permute-start | bytes 405512 | tf_op jit(solution)/shard_map/ppermute | solution.py:246
  55.4 1.4 %collective-permute-start.15 = (bf16[528,128]{1,0:T(8,128)(2,1)S(1)}, bf16[528,128]{1,0:T(8,128)(2,1)S(1)}, u32[]{:S(2)}, u32[]{:S(2)}) collective-permute-start(bf16[528,128]{1,0:T(8,128)(2,1)S(1)} %get-tuple-element.187), channel_id=1, source_target_pairs={{0,1},{1,0},{2,3},{3,2},{4,5},{5,4},{6,7},{7,6},{8,9},{9,8},{10,11... | collective-permute-start | bytes 405512 | tf_op jit(solution)/shard_map/ppermute | solution.py:246

commit v7 on v6

--- a/solution.py
+++ b/solution.py
@@ -12,7 +12,7 @@
 TILE = 128
 QUARTER = HEADS // 4
 SPAN = QUARTER * HEAD
-WORK, LIGHT = 2_000_000_000, 300_000_000
+WORK = 2_000_000_000
 PIECES = 2
 EXTRA = 16
 norm_eps = 1e-05
@@ -461,7 +461,6 @@
             held(*tiles("kv", which), back_state, *inner_grads[which]),
             [low, low],
             put=put,
-            flops=LIGHT,
         )
         ready.extend([(which, key_grad, "key"), (which, value_grad, "value")])
         return key_grad

time: 59.3 us -> 58.7 us (0.990)
  no operation moved by 1% of the time
where the time goes in v7:
time: 58.7 us; the launch traced here: 58.5 us
  Pallas kernels  30.5 us (52%)
  starting transfers between devices  16.4 us (28%)
  waiting for transfers between devices  9.45 us (16%)
  between operations  1.07 us (2%)
  other arithmetic  0.99 us (2%)
    pallas_call x20, Pallas kernels, call(): pl.pallas_call(kernel, out_shape=[jax.ShapeDtypeStruct(shape, dtype) for...  30.5 us
    ppermute x16, starting transfers between devices, permute(): return lax.ppermute(value, 'seq', pairs)  16.4 us
    ppermute x16, waiting for transfers between devices, permute(): return lax.ppermute(value, 'seq', pairs)  9.45 us
  transfers between devices with their start and end apart: 16, of which 9 were waited for; matrix products, arithmetic and copies ran while one was open for 0% of the time, Pallas kernels for 46%

profile of v7, /device:TPU:0, one launch (start us, length us, event | category | flops | bytes accessed | tf_op | source)
XLA Modules:
  0.0 58.5 jit_solution(1592828446839279347)
XLA Ops:
  0.6 1.7 %shard_map.84 = (bf16[512,128]{1,0:T(8,128)(2,1)S(1)}, bf16[384,512]{1,0:T(8,128)(2,1)S(1)}, bf16[384,512]{1,0:T(8,128)(2,1)S(1)}, bf16[384,512]{1,0:T(8,128)(2,1)S(1)}, bf16[384,512]{1,0:T(8,128)(2,1)S(1)}) custom-call(s32[1]{0:T(128)} %bitcast.refs_0_.index_ref.refs_1_, bf16[384,2048]{1,0:T(8,128)(2,1)} %refs_3_.3, bf16[384,2048]{1,0:T(8,128)(2,1)} %refs_4_.4, ...), custom_call_target="tpu_custom_call" | custom-call | flops 2000000000 | bytes 4194304 | tf_op jit(solution)/shard_map/pallas_call | solution.py:233
  2.3 0.5 collective-permute-start
  2.9 0.4 shard_map.85
  3.3 0.6 collective-permute-done
  3.9 2.9 %collective-permute-start.2 = (bf16[512,128]{1,0:T(8,128)(2,1)S(1)}, bf16[512,128]{1,0:T(8,128)(2,1)S(1)}, u32[]{:S(2)}, u32[]{:S(2)}) collective-permute-start(bf16[512,128]{1,0:T(8,128)(2,1)S(1)} %fusion.7), channel_id=1, source_target_pairs={{0,2},{1,3},{2,0},{3,1},{4,6},{5,7},{6,4},{7,5},{8,10},{9,11},{10,... | collective-permute-start | bytes 393224 | tf_op jit(solution)/shard_map/ppermute | solution.py:246
  6.8 1.7 %shard_map.86 = (bf16[512,128]{1,0:T(8,128)(2,1)S(1)}, bf16[384,512]{1,0:T(8,128)(2,1)S(1)}, bf16[384,512]{1,0:T(8,128)(2,1)S(1)}, bf16[384,512]{1,0:T(8,128)(2,1)S(1)}, bf16[384,512]{1,0:T(8,128)(2,1)S(1)}) custom-call(s32[1]{0:T(128)} %bitcast.refs_0_.index_ref.refs_1_, bf16[384,2048]{1,0:T(8,128)(2,1)} %refs_3_.3, bf16[384,2048]{1,0:T(8,128)(2,1)} %refs_4_.4, ...), custom_call_target="tpu_custom_call" | custom-call | flops 2000000000 | bytes 4194304 | tf_op jit(solution)/shard_map/pallas_call | solution.py:233
  8.5 0.1 collective-permute-start.1
  8.6 0.4 shard_map.87
  9.0 1.6 %collective-permute-done.2 = bf16[512,128]{1,0:T(8,128)(2,1)S(1)} collective-permute-done((bf16[512,128]{1,0:T(8,128)(2,1)S(1)}, bf16[512,128]{1,0:T(8,128)(2,1)S(1)}, u32[]{:S(2)}, u32[]{:S(2)}) %collective-permute-start.2) | collective-permute-done | bytes 131104 | tf_op jit(solution)/shard_map/ppermute | solution.py:246
  10.7 1.9 %collective-permute-start.3 = (bf16[512,128]{1,0:T(8,128)(2,1)S(1)}, bf16[512,128]{1,0:T(8,128)(2,1)S(1)}, u32[]{:S(2)}, u32[]{:S(2)}) collective-permute-start(bf16[512,128]{1,0:T(8,128)(2,1)S(1)} %fusion.10), channel_id=1, source_target_pairs={{0,4},{1,5},{2,6},{3,7},{4,0},{5,1},{6,2},{7,3},{8,12},{9,13},{10,... | collective-permute-start | bytes 393224 | tf_op jit(solution)/shard_map/ppermute | solution.py:246
  12.5 2.1 %shard_map.88 = (f32[384,512]{1,0:T(8,128)S(1)}, bf16[384,512]{1,0:T(8,128)(2,1)S(1)}, bf16[384,512]{1,0:T(8,128)(2,1)S(1)}, bf16[384,512]{1,0:T(8,128)(2,1)S(1)}, bf16[384,512]{1,0:T(8,128)(2,1)S(1)}) custom-call(s32[1]{0:T(128)} %bitcast.refs_0_.index_ref.refs_1_, bf16[384,512]{1,0:T(8,128)(2,1)S(1)} %get-tuple-element.110.refs_1_.refs_2_, ...), custom_call_target="tpu_custom_call" | custom-call | flops 2000000000 | bytes 4194304 | tf_op jit(solution)/shard_map/pallas_call | solution.py:233
  14.6 1.1 %collective-permute-done.3 = bf16[512,128]{1,0:T(8,128)(2,1)S(1)} collective-permute-done((bf16[512,128]{1,0:T(8,128)(2,1)S(1)}, bf16[512,128]{1,0:T(8,128)(2,1)S(1)}, u32[]{:S(2)}, u32[]{:S(2)}) %collective-permute-start.3) | collective-permute-done | bytes 131104 | tf_op jit(solution)/shard_map/ppermute | solution.py:246
  15.8 2.8 %collective-permute-start.4 = (bf16[512,128]{1,0:T(8,128)(2,1)S(1)}, bf16[512,128]{1,0:T(8,128)(2,1)S(1)}, u32[]{:S(2)}, u32[]{:S(2)}) collective-permute-start(bf16[512,128]{1,0:T(8,128)(2,1)S(1)} %fusion.12), channel_id=1, source_target_pairs={{0,8},{1,9},{2,10},{3,11},{4,12},{5,13},{6,14},{7,15},{8,0},{9,1},... | collective-permute-start | bytes 393224 | tf_op jit(solution)/shard_map/ppermute | solution.py:246
  18.6 2.3 %shard_map.89 = (f32[384,512]{1,0:T(8,128)S(1)}, bf16[384,512]{1,0:T(8,128)(2,1)S(1)}, bf16[384,512]{1,0:T(8,128)(2,1)S(1)}, bf16[384,512]{1,0:T(8,128)(2,1)S(1)}, bf16[384,512]{1,0:T(8,128)(2,1)S(1)}) custom-call(s32[1]{0:T(128)} %bitcast.refs_0_.index_ref.refs_1_, bf16[384,512]{1,0:T(8,128)(2,1)S(1)} %get-tuple-element.116.refs_1_.query_ref, ...), custom_call_target="tpu_custom_call" | custom-call | flops 2000000000 | bytes 4194304 | tf_op jit(solution)/shard_map/pallas_call | solution.py:233
  21.0 1.0 %shard_map.90.mixed_ref = f32[384,512]{1,0:T(8,128)S(1)} custom-call(s32[1]{0:T(128)} %bitcast.refs_0_.index_ref.refs_1_, bf16[384,512]{1,0:T(8,128)(2,1)S(1)} %get-tuple-element.123.refs_1_.query_ref, bf16[384,512]{1,0:T(8,128)(2,1)S(1)} %get-tuple-element.124.refs_1_.refs_2_, bf16[384,512]{1,0:T(8,128)(2,1)S(1)} %get-tuple-element.125.refs_2_.refs_3_), custom_call_target="tpu_custom_call" | custom-call | flops 2000000000 | bytes 4194304 | tf_op jit(solution)/shard_map/pallas_call | solution.py:233
  22.0 1.0 %shard_map.91.mixed_ref = f32[384,512]{1,0:T(8,128)S(1)} custom-call(s32[1]{0:T(128)} %bitcast.refs_0_.index_ref.refs_1_, bf16[384,512]{1,0:T(8,128)(2,1)S(1)} %get-tuple-element.126.refs_1_.query_ref, bf16[384,512]{1,0:T(8,128)(2,1)S(1)} %get-tuple-element.127.refs_2_.refs_1_, bf16[384,512]{1,0:T(8,128)(2,1)S(1)} %get-tuple-element.128.refs_3_.refs_2_), custom_call_target="tpu_custom_call" | custom-call | flops 2000000000 | bytes 4194304 | tf_op jit(solution)/shard_map/pallas_call | solution.py:233
  23.0 0.7 %collective-permute-done.4 = bf16[512,128]{1,0:T(8,128)(2,1)S(1)} collective-permute-done((bf16[512,128]{1,0:T(8,128)(2,1)S(1)}, bf16[512,128]{1,0:T(8,128)(2,1)S(1)}, u32[]{:S(2)}, u32[]{:S(2)}) %collective-permute-start.4) | collective-permute-done | bytes 131104 | tf_op jit(solution)/shard_map/ppermute | solution.py:246
  23.7 0.2 add_convert_fusion.6
  23.9 1.2 %collective-permute-start.5 = (bf16[512,128]{1,0:T(8,128)(2,1)S(1)}, bf16[512,128]{1,0:T(8,128)(2,1)S(1)}, u32[]{:S(2)}, u32[]{:S(2)}) collective-permute-start(bf16[512,128]{1,0:T(8,128)(2,1)S(1)} %get-tuple-element.183), channel_id=1, source_target_pairs={{0,2},{1,3},{2,0},{3,1},{4,6},{5,7},{6,4},{7,5},{8,10},{9,11},{10,... | collective-permute-start | bytes 393224 | tf_op jit(solution)/shard_map/ppermute | solution.py:246
  25.1 0.9 %shard_map.93 = (bf16[384,512]{1,0:T(8,128)(2,1)S(1)}, bf16[528,128]{1,0:T(8,128)(2,1)S(1)}) custom-call(s32[1]{0:T(128)} %bitcast.refs_0_.index_ref.refs_1_, bf16[384,512]{1,0:T(8,128)(2,1)S(1)} %get-tuple-element.116.refs_1_.query_ref, bf16[384,512]{1,0:T(8,128)(2,1)S(1)} %get-tuple-element.135.cotan_ref, f32[1,2048]{1,0:T(1,128)S(1)} %bitcast.3, ...), custom_call_target="tpu_custom_call" | custom-call | flops 2000000000 | bytes 4194304 | tf_op jit(solution)/shard_map/pallas_call | solution.py:233
  26.0 0.6 collective-permute-start.7
  26.6 1.0 %shard_map.92 = (bf16[384,512]{1,0:T(8,128)(2,1)S(1)}, f32[528,128]{1,0:T(8,128)S(1)}) custom-call(s32[1]{0:T(128)} %bitcast.refs_0_.index_ref.refs_1_, bf16[384,512]{1,0:T(8,128)(2,1)S(1)} %get-tuple-element.131.query_ref.refs_1_, bf16[384,512]{1,0:T(8,128)(2,1)S(1)} %get-tuple-element.132.cotan_ref, f32[1,2048]{1,0:T(1,128)S(1)} %bitcast.4, ...), custom_call_target="tpu_custom_call" | custom-call | flops 2000000000 | bytes 4194304 | tf_op jit(solution)/shard_map/pallas_call | solution.py:233
  27.6 1.0 %collective-permute-start.10 = (bf16[528,128]{1,0:T(8,128)(2,1)S(1)}, bf16[528,128]{1,0:T(8,128)(2,1)S(1)}, u32[]{:S(2)}, u32[]{:S(2)}) collective-permute-start(bf16[528,128]{1,0:T(8,128)(2,1)S(1)} %add_convert_fusion.4), channel_id=1, source_target_pairs={{0,2},{1,3},{2,0},{3,1},{4,6},{5,7},{6,4},{7,5},{8,10},{9,11},{10,... | collective-permute-start | bytes 405512 | tf_op jit(solution)/shard_map/ppermute | solution.py:246
  28.6 0.3 collective-permute-done.5
  28.9 0.1 fusion.14
  29.0 0.1 collective-permute-start.8
  29.1 1.0 %shard_map.95 = (bf16[384,512]{1,0:T(8,128)(2,1)S(1)}, bf16[528,128]{1,0:T(8,128)(2,1)S(1)}) custom-call(s32[1]{0:T(128)} %bitcast.refs_0_.index_ref.refs_1_, bf16[384,512]{1,0:T(8,128)(2,1)S(1)} %get-tuple-element.123.refs_1_.query_ref, bf16[384,512]{1,0:T(8,128)(2,1)S(1)} %get-tuple-element.140.cotan_ref, f32[1,2048]{1,0:T(1,128)S(1)} %bitcast.5, ...), custom_call_target="tpu_custom_call" | custom-call | flops 2000000000 | bytes 4194304 | tf_op jit(solution)/shard_map/pallas_call | solution.py:233
  30.0 0.6 collective-permute-start.9
  30.6 1.0 %shard_map.94 = (bf16[384,512]{1,0:T(8,128)(2,1)S(1)}, f32[528,128]{1,0:T(8,128)S(1)}) custom-call(s32[1]{0:T(128)} %bitcast.refs_0_.index_ref.refs_1_, bf16[384,512]{1,0:T(8,128)(2,1)S(1)} %get-tuple-element.126.refs_1_.query_ref, bf16[384,512]{1,0:T(8,128)(2,1)S(1)} %get-tuple-element.119.cotan_ref, f32[1,2048]{1,0:T(1,128)S(1)} %bitcast.6, ...), custom_call_target="tpu_custom_call" | custom-call | flops 2000000000 | bytes 4194304 | tf_op jit(solution)/shard_map/pallas_call | solution.py:233
  31.6 1.9 %collective-permute-done.10 = bf16[528,128]{1,0:T(8,128)(2,1)S(1)} collective-permute-done((bf16[528,128]{1,0:T(8,128)(2,1)S(1)}, bf16[528,128]{1,0:T(8,128)(2,1)S(1)}, u32[]{:S(2)}, u32[]{:S(2)}) %collective-permute-start.10) | collective-permute-done | bytes 135200 | tf_op jit(solution)/shard_map/ppermute | solution.py:246
  33.5 0.1 add_convert_fusion.3
  33.6 1.4 %collective-permute-start.11 = (bf16[528,128]{1,0:T(8,128)(2,1)S(1)}, bf16[528,128]{1,0:T(8,128)(2,1)S(1)}, u32[]{:S(2)}, u32[]{:S(2)}) collective-permute-start(bf16[528,128]{1,0:T(8,128)(2,1)S(1)} %add_convert_fusion.3), channel_id=1, source_target_pairs={{0,4},{1,5},{2,6},{3,7},{4,0},{5,1},{6,2},{7,3},{8,12},{9,13},{10,... | collective-permute-start | bytes 405512 | tf_op jit(solution)/shard_map/ppermute | solution.py:246
  35.0 2.4 %shard_map.96 = (f32[384,512]{1,0:T(8,128)S(1)}, f32[384,512]{1,0:T(8,128)S(1)}, bf16[384,512]{1,0:T(8,128)(2,1)S(1)}) custom-call(s32[1]{0:T(128)} %bitcast.refs_0_.index_ref.refs_1_, bf16[384,512]{1,0:T(8,128)(2,1)S(1)} %get-tuple-element.126.refs_1_.query_ref, bf16[384,512]{1,0:T(8,128)(2,1)S(1)} %get-tuple-element.127.refs_2_.refs_1_, ...), custom_call_target="tpu_custom_call" | custom-call | flops 2000000000 | bytes 4194304 | tf_op jit(solution)/shard_map/pallas_call | solution.py:233
  37.4 2.6 %shard_map.97 = (f32[384,512]{1,0:T(8,128)S(1)}, f32[384,512]{1,0:T(8,128)S(1)}, bf16[384,512]{1,0:T(8,128)(2,1)S(1)}) custom-call(s32[1]{0:T(128)} %bitcast.refs_0_.index_ref.refs_1_, bf16[384,512]{1,0:T(8,128)(2,1)S(1)} %get-tuple-element.123.refs_1_.query_ref, bf16[384,512]{1,0:T(8,128)(2,1)S(1)} %get-tuple-element.124.refs_1_.refs_2_, ...), custom_call_target="tpu_custom_call" | custom-call | flops 2000000000 | bytes 4194304 | tf_op jit(solution)/shard_map/pallas_call | solution.py:233
  40.1 2.8 %collective-permute-start.12 = (bf16[528,128]{1,0:T(8,128)(2,1)S(1)}, bf16[528,128]{1,0:T(8,128)(2,1)S(1)}, u32[]{:S(2)}, u32[]{:S(2)}) collective-permute-start(bf16[528,128]{1,0:T(8,128)(2,1)S(1)} %fusion.3), channel_id=1, source_target_pairs={{0,8},{1,9},{2,10},{3,11},{4,12},{5,13},{6,14},{7,15},{8,0},{9,1},... | collective-permute-start | bytes 405512 | tf_op jit(solution)/shard_map/ppermute | solution.py:246
  42.9 2.5 %shard_map.98 = (f32[384,512]{1,0:T(8,128)S(1)}, f32[384,512]{1,0:T(8,128)S(1)}, bf16[384,512]{1,0:T(8,128)(2,1)S(1)}) custom-call(s32[1]{0:T(128)} %bitcast.refs_0_.index_ref.refs_1_, bf16[384,512]{1,0:T(8,128)(2,1)S(1)} %get-tuple-element.131.query_ref.refs_1_, bf16[384,512]{1,0:T(8,128)(2,1)S(1)} %get-tuple-element.110.refs_1_.refs_2_, ...), custom_call_target="tpu_custom_call" | custom-call | flops 2000000000 | bytes 4194304 | tf_op jit(solution)/shard_map/pallas_call | solution.py:233
  45.4 2.5 %shard_map.99 = (f32[384,512]{1,0:T(8,128)S(1)}, f32[384,512]{1,0:T(8,128)S(1)}, bf16[384,512]{1,0:T(8,128)(2,1)S(1)}) custom-call(s32[1]{0:T(128)} %bitcast.refs_0_.index_ref.refs_1_, bf16[384,512]{1,0:T(8,128)(2,1)S(1)} %get-tuple-element.116.refs_1_.query_ref, bf16[384,512]{1,0:T(8,128)(2,1)S(1)} %get-tuple-element.117.refs_1_.refs_2_, ...), custom_call_target="tpu_custom_call" | custom-call | flops 2000000000 | bytes 4194304 | tf_op jit(solution)/shard_map/pallas_call | solution.py:233
  47.9 1.0 %collective-permute-done.12 = bf16[528,128]{1,0:T(8,128)(2,1)S(1)} collective-permute-done((bf16[528,128]{1,0:T(8,128)(2,1)S(1)}, bf16[528,128]{1,0:T(8,128)(2,1)S(1)}, u32[]{:S(2)}, u32[]{:S(2)}) %collective-permute-start.12) | collective-permute-done | bytes 135200 | tf_op jit(solution)/shard_map/ppermute | solution.py:246
  48.8 0.3 add_convert_fusion
  49.1 0.6 %collective-permute-start.13 = (bf16[528,128]{1,0:T(8,128)(2,1)S(1)}, bf16[528,128]{1,0:T(8,128)(2,1)S(1)}, u32[]{:S(2)}, u32[]{:S(2)}) collective-permute-start(bf16[528,128]{1,0:T(8,128)(2,1)S(1)} %get-tuple-element.181), channel_id=1, source_target_pairs={{0,2},{1,3},{2,0},{3,1},{4,6},{5,7},{6,4},{7,5},{8,10},{9,11},{10,... | collective-permute-start | bytes 405512 | tf_op jit(solution)/shard_map/ppermute | solution.py:246
  49.7 1.5 %shard_map.100 = (bf16[384,512]{1,0:T(8,128)(2,1)S(1)}, bf16[384,512]{1,0:T(8,128)(2,1)S(1)}, bf16[384,2048]{1,0:T(8,128)(2,1)}) custom-call(s32[1]{0:T(128)} %bitcast.refs_0_.index_ref.refs_1_, bf16[384,512]{1,0:T(8,128)(2,1)S(1)} %get-tuple-element.127.refs_2_.refs_1_, bf16[384,512]{1,0:T(8,128)(2,1)S(1)} %get-tuple-element.128.refs_3_.refs_2_, ...), custom_call_target="tpu_custom_call" | custom-call | flops 2000000000 | bytes 4194304 | tf_op jit(solution)/shard_map/pallas_call | solution.py:233
  51.3 1.2 %shard_map.101 = (bf16[384,512]{1,0:T(8,128)(2,1)S(1)}, bf16[384,512]{1,0:T(8,128)(2,1)S(1)}, bf16[384,2048]{1,0:T(8,128)(2,1)}, bf16[384,2048]{1,0:T(8,128)(2,1)}) custom-call(s32[1]{0:T(128)} %bitcast.refs_0_.index_ref.refs_1_, bf16[384,512]{1,0:T(8,128)(2,1)S(1)} %get-tuple-element.124.refs_1_.refs_2_, ...), custom_call_target="tpu_custom_call" | custom-call | flops 2000000000 | bytes 4194304 | tf_op jit(solution)/shard_map/pallas_call | solution.py:233
  52.5 2.2 %collective-permute-done.13 = bf16[528,128]{1,0:T(8,128)(2,1)S(1)} collective-permute-done((bf16[528,128]{1,0:T(8,128)(2,1)S(1)}, bf16[528,128]{1,0:T(8,128)(2,1)S(1)}, u32[]{:S(2)}, u32[]{:S(2)}) %collective-permute-start.13) | collective-permute-done | bytes 135200 | tf_op jit(solution)/shard_map/ppermute | solution.py:246
  54.7 0.2 fusion.6
  54.8 0.1 collective-permute-start.15
  54.9 1.2 %shard_map.102 = (bf16[384,512]{1,0:T(8,128)(2,1)S(1)}, bf16[384,512]{1,0:T(8,128)(2,1)S(1)}, bf16[384,2048]{1,0:T(8,128)(2,1)}, bf16[384,2048]{1,0:T(8,128)(2,1)}) custom-call(s32[1]{0:T(128)} %bitcast.refs_0_.index_ref.refs_1_, bf16[384,512]{1,0:T(8,128)(2,1)S(1)} %get-tuple-element.110.refs_1_.refs_2_, ...), custom_call_target="tpu_custom_call", output_to_operand_aliasing={{2}: (8, {}), {3}: (9, {})} | custom-call | flops 2000000000 | bytes 4194304 | tf_op jit(solution)/shard_map/pallas_call | solution.py:233
  56.2 0.1 collective-permute-done.15.refs_6_
  56.3 2.0 %shard_map.103 = (f32[1,2048]{1,0:T(1,128)}, bf16[384,2048]{1,0:T(8,128)(2,1)}, bf16[384,2048]{1,0:T(8,128)(2,1)}) custom-call(s32[1]{0:T(128)} %bitcast.refs_0_.index_ref.refs_1_, s32[1]{0:T(128)} %bitcast.refs_0_.index_ref.refs_1_, bf16[384,512]{1,0:T(8,128)(2,1)S(1)} %get-tuple-element.117.refs_1_.refs_2_, ...), custom_call_target="tpu_custom_call", output_to_operand_aliasing={{1}: (12, {}), {2}: (13, {})} | custom-call | flops 2000000000 | bytes 4194304 | tf_op jit(solution)/shard_map/pallas_call | solution.py:233
  (17 shorter events, 0.2 us)
Async XLA Ops:
  2.3 1.5 %collective-permute-start = (bf16[512,128]{1,0:T(8,128)(2,1)S(1)}, bf16[512,128]{1,0:T(8,128)(2,1)S(1)}, u32[]{:S(2)}, u32[]{:S(2)}) collective-permute-start(bf16[512,128]{1,0:T(8,128)(2,1)S(1)} %get-tuple-element.98), channel_id=1, source_target_pairs={{0,1},{1,0},{2,3},{3,2},{4,5},{5,4},{6,7},{7,6},{8,9},{9,8},{10,11... | collective-permute-start | bytes 393224 | tf_op jit(solution)/shard_map/ppermute | solution.py:246
  3.9 6.7 %collective-permute-start.2 = (bf16[512,128]{1,0:T(8,128)(2,1)S(1)}, bf16[512,128]{1,0:T(8,128)(2,1)S(1)}, u32[]{:S(2)}, u32[]{:S(2)}) collective-permute-start(bf16[512,128]{1,0:T(8,128)(2,1)S(1)} %fusion.7), channel_id=1, source_target_pairs={{0,2},{1,3},{2,0},{3,1},{4,6},{5,7},{6,4},{7,5},{8,10},{9,11},{10,... | collective-permute-start | bytes 393224 | tf_op jit(solution)/shard_map/ppermute | solution.py:246
  8.5 2.1 %collective-permute-start.1 = (bf16[512,128]{1,0:T(8,128)(2,1)S(1)}, bf16[512,128]{1,0:T(8,128)(2,1)S(1)}, u32[]{:S(2)}, u32[]{:S(2)}) collective-permute-start(bf16[512,128]{1,0:T(8,128)(2,1)S(1)} %get-tuple-element.107), channel_id=1, source_target_pairs={{0,1},{1,0},{2,3},{3,2},{4,5},{5,4},{6,7},{7,6},{8,9},{9,8},{10,11... | collective-permute-start | bytes 393224 | tf_op jit(solution)/shard_map/ppermute | solution.py:246
  10.7 5.1 %collective-permute-start.3 = (bf16[512,128]{1,0:T(8,128)(2,1)S(1)}, bf16[512,128]{1,0:T(8,128)(2,1)S(1)}, u32[]{:S(2)}, u32[]{:S(2)}) collective-permute-start(bf16[512,128]{1,0:T(8,128)(2,1)S(1)} %fusion.10), channel_id=1, source_target_pairs={{0,4},{1,5},{2,6},{3,7},{4,0},{5,1},{6,2},{7,3},{8,12},{9,13},{10,... | collective-permute-start | bytes 393224 | tf_op jit(solution)/shard_map/ppermute | solution.py:246
  15.8 7.9 %collective-permute-start.4 = (bf16[512,128]{1,0:T(8,128)(2,1)S(1)}, bf16[512,128]{1,0:T(8,128)(2,1)S(1)}, u32[]{:S(2)}, u32[]{:S(2)}) collective-permute-start(bf16[512,128]{1,0:T(8,128)(2,1)S(1)} %fusion.12), channel_id=1, source_target_pairs={{0,8},{1,9},{2,10},{3,11},{4,12},{5,13},{6,14},{7,15},{8,0},{9,1},... | collective-permute-start | bytes 393224 | tf_op jit(solution)/shard_map/ppermute | solution.py:246
  22.0 3.0 %copy-start = (f32[2048]{0:T(1024)S(1)}, f32[2048]{0:T(1024)}, u32[]{:S(2)}) copy-start(f32[2048]{0:T(1024)} %param.9) | copy-start | bytes 24580
  23.9 5.0 %collective-permute-start.5 = (bf16[512,128]{1,0:T(8,128)(2,1)S(1)}, bf16[512,128]{1,0:T(8,128)(2,1)S(1)}, u32[]{:S(2)}, u32[]{:S(2)}) collective-permute-start(bf16[512,128]{1,0:T(8,128)(2,1)S(1)} %get-tuple-element.183), channel_id=1, source_target_pairs={{0,2},{1,3},{2,0},{3,1},{4,6},{5,7},{6,4},{7,5},{8,10},{9,11},{10,... | collective-permute-start | bytes 393224 | tf_op jit(solution)/shard_map/ppermute | solution.py:246
  25.1 1.5 %collective-permute-start.6 = (bf16[512,128]{1,0:T(8,128)(2,1)S(1)}, bf16[512,128]{1,0:T(8,128)(2,1)S(1)}, u32[]{:S(2)}, u32[]{:S(2)}) collective-permute-start(bf16[512,128]{1,0:T(8,128)(2,1)S(1)} %get-tuple-element.184), channel_id=1, source_target_pairs={{0,1},{1,0},{2,3},{3,2},{4,5},{5,4},{6,7},{7,6},{8,9},{9,8},{10,11... | collective-permute-start | bytes 393224 | tf_op jit(solution)/shard_map/ppermute | solution.py:246
  26.0 1.6 %collective-permute-start.7 = (bf16[528,128]{1,0:T(8,128)(2,1)S(1)}, bf16[528,128]{1,0:T(8,128)(2,1)S(1)}, u32[]{:S(2)}, u32[]{:S(2)}) collective-permute-start(bf16[528,128]{1,0:T(8,128)(2,1)S(1)} %get-tuple-element.136), channel_id=1, source_target_pairs={{0,1},{1,0},{2,3},{3,2},{4,5},{5,4},{6,7},{7,6},{8,9},{9,8},{10,11... | collective-permute-start | bytes 405512 | tf_op jit(solution)/shard_map/ppermute | solution.py:246
  27.6 5.9 %collective-permute-start.10 = (bf16[528,128]{1,0:T(8,128)(2,1)S(1)}, bf16[528,128]{1,0:T(8,128)(2,1)S(1)}, u32[]{:S(2)}, u32[]{:S(2)}) collective-permute-start(bf16[528,128]{1,0:T(8,128)(2,1)S(1)} %add_convert_fusion.4), channel_id=1, source_target_pairs={{0,2},{1,3},{2,0},{3,1},{4,6},{5,7},{6,4},{7,5},{8,10},{9,11},{10,... | collective-permute-start | bytes 405512 | tf_op jit(solution)/shard_map/ppermute | solution.py:246
  29.0 1.6 %collective-permute-start.8 = (bf16[512,128]{1,0:T(8,128)(2,1)S(1)}, bf16[512,128]{1,0:T(8,128)(2,1)S(1)}, u32[]{:S(2)}, u32[]{:S(2)}) collective-permute-start(bf16[512,128]{1,0:T(8,128)(2,1)S(1)} %get-tuple-element.188), channel_id=1, source_target_pairs={{0,1},{1,0},{2,3},{3,2},{4,5},{5,4},{6,7},{7,6},{8,9},{9,8},{10,11... | collective-permute-start | bytes 393224 | tf_op jit(solution)/shard_map/ppermute | solution.py:246
  30.0 3.5 %collective-permute-start.9 = (bf16[528,128]{1,0:T(8,128)(2,1)S(1)}, bf16[528,128]{1,0:T(8,128)(2,1)S(1)}, u32[]{:S(2)}, u32[]{:S(2)}) collective-permute-start(bf16[528,128]{1,0:T(8,128)(2,1)S(1)} %get-tuple-element.141), channel_id=1, source_target_pairs={{0,1},{1,0},{2,3},{3,2},{4,5},{5,4},{6,7},{7,6},{8,9},{9,8},{10,11... | collective-permute-start | bytes 405512 | tf_op jit(solution)/shard_map/ppermute | solution.py:246
  33.6 6.5 %collective-permute-start.11 = (bf16[528,128]{1,0:T(8,128)(2,1)S(1)}, bf16[528,128]{1,0:T(8,128)(2,1)S(1)}, u32[]{:S(2)}, u32[]{:S(2)}) collective-permute-start(bf16[528,128]{1,0:T(8,128)(2,1)S(1)} %add_convert_fusion.3), channel_id=1, source_target_pairs={{0,4},{1,5},{2,6},{3,7},{4,0},{5,1},{6,2},{7,3},{8,12},{9,13},{10,... | collective-permute-start | bytes 405512 | tf_op jit(solution)/shard_map/ppermute | solution.py:246
  40.1 8.7 %collective-permute-start.12 = (bf16[528,128]{1,0:T(8,128)(2,1)S(1)}, bf16[528,128]{1,0:T(8,128)(2,1)S(1)}, u32[]{:S(2)}, u32[]{:S(2)}) collective-permute-start(bf16[528,128]{1,0:T(8,128)(2,1)S(1)} %fusion.3), channel_id=1, source_target_pairs={{0,8},{1,9},{2,10},{3,11},{4,12},{5,13},{6,14},{7,15},{8,0},{9,1},... | collective-permute-start | bytes 405512 | tf_op jit(solution)/shard_map/ppermute | solution.py:246
  49.1 5.5 %collective-permute-start.13 = (bf16[528,128]{1,0:T(8,128)(2,1)S(1)}, bf16[528,128]{1,0:T(8,128)(2,1)S(1)}, u32[]{:S(2)}, u32[]{:S(2)}) collective-permute-start(bf16[528,128]{1,0:T(8,128)(2,1)S(1)} %get-tuple-element.181), channel_id=1, source_target_pairs={{0,2},{1,3},{2,0},{3,1},{4,6},{5,7},{6,4},{7,5},{8,10},{9,11},{10,... | collective-permute-start | bytes 405512 | tf_op jit(solution)/shard_map/ppermute | solution.py:246
  49.7 1.5 %collective-permute-start.14 = (bf16[528,128]{1,0:T(8,128)(2,1)S(1)}, bf16[528,128]{1,0:T(8,128)(2,1)S(1)}, u32[]{:S(2)}, u32[]{:S(2)}) collective-permute-start(bf16[528,128]{1,0:T(8,128)(2,1)S(1)} %get-tuple-element.180), channel_id=1, source_target_pairs={{0,1},{1,0},{2,3},{3,2},{4,5},{5,4},{6,7},{7,6},{8,9},{9,8},{10,11... | collective-permute-start | bytes 405512 | tf_op jit(solution)/shard_map/ppermute | solution.py:246
  54.8 1.4 %collective-permute-start.15 = (bf16[528,128]{1,0:T(8,128)(2,1)S(1)}, bf16[528,128]{1,0:T(8,128)(2,1)S(1)}, u32[]{:S(2)}, u32[]{:S(2)}) collective-permute-start(bf16[528,128]{1,0:T(8,128)(2,1)S(1)} %get-tuple-element.187), channel_id=1, source_target_pairs={{0,1},{1,0},{2,3},{3,2},{4,5},{5,4},{6,7},{7,6},{8,9},{9,8},{10,11... | collective-permute-start | bytes 405512 | tf_op jit(solution)/shard_map/ppermute | solution.py:246
